TPU v7x, 512 devices: a whole 4x4x16 slice. The times are simulated.
512 devices in a mesh: outer: 32 (over y, x, core), inner: 16 (over z).
Axes of the slice: x: 4, y: 4, z: 16, core: 2. Of those that a mesh axis runs over, the one named last changes fastest.
Arguments:
- right_sides: float32 [65536, 128], P(('outer', 'inner')), may hold values from -6 to 6
- leaf_order: int32 [512, 128], P(('outer', 'inner')), may hold values from 0 to 127, each once within a row
- leaf_inverse: float32 [65536, 128], P(('outer', 'inner')), may hold values from -0.1237436867076458 to 2.5, as said below
- basis_blocks: float32 [9, 65536, 128], P(None, ('outer', 'inner')), may hold values from -0.25013902 to 0.25013902
Outputs:
- solution: float32 [65536, 128], P(('outer', 'inner'))
Inputs may be any that keep to these rules, and one draw needn't show every extreme that they name: `leaf_inverse`: each leaf's block is lower triangular, its diagonal between 1.5 and 2.5.
All inputs are finite; a program needn't handle non-finite values.
Results may differ from a plain program's by a relative error of at most 0.00013.
Values sent between devices are 32-bit elements; how exact they have to be, the bound alone decides.
No kernel may reach another device: no remote copies, remote signals or barrier semaphores. Data moves between devices by JAX's collectives and lax.ppermute only.
A program may use at most 64 MiB of HBM per device.

v0:
```python
import jax
import jax.numpy as jnp
from jax import lax
from jax.sharding import PartitionSpec as P


def swapped(block, axis, bit):
    count = lax.axis_size(axis)
    route = []
    for low in range(count):
        high = low | 1 << bit
        if high != low and high < count:
            route += [(low, high), (high, low)]
    return lax.ppermute(block, axis, route)


def coupling_inverse(size):
    unit = jnp.eye(size, dtype=jnp.float32)
    return jnp.block([[2.0 * unit, -unit], [-unit, 2.0 * unit]]) / 3.0


def subtree_sum(products, height, inner_bits):
    first_bit = 0
    for bit_index in range(first_bit, height):
        if bit_index < inner_bits:
            products = products + swapped(products, "inner", bit_index)
        else:
            products = products + swapped(products, "outer", bit_index - inner_bits)
    return products


def sibling_of(summed, height, inner_bits):
    if height < inner_bits:
        sibling = swapped(summed, "inner", height)
        branch_bit = lax.axis_index("inner") >> height & 1
    else:
        sibling = swapped(summed, "outer", height - inner_bits)
        branch_bit = lax.axis_index("outer") >> height - inner_bits & 1
    return (sibling, branch_bit == 0)


def node_weights(first_block, second_block, coupling, basis_rank):
    zero_block = jnp.zeros((basis_rank, basis_rank), jnp.float32)
    system = coupling + jnp.block(
        [[first_block[:, :basis_rank], zero_block], [zero_block, second_block[:, :basis_rank]]]
    )
    targets = jnp.concatenate([first_block[:, basis_rank:], second_block[:, basis_rank:]], axis=0)
    factor_low = jnp.linalg.cholesky(system)
    middle = jax.scipy.linalg.solve_triangular(factor_low, targets, lower=True)
    return jax.scipy.linalg.solve_triangular(factor_low, middle, lower=True, trans=1)


def body(right_sides, leaf_order, leaf_inverse, basis_blocks):
    levels = basis_blocks.shape[0]
    basis_rank = basis_blocks.shape[2]
    inner_bits = lax.axis_size("inner").bit_length() - 1
    point_order = leaf_order[0]
    tree_sides = jnp.take(right_sides, point_order, axis=0)
    columns = jnp.concatenate(
        [basis_blocks[slot_index] for slot_index in range(levels)] + [tree_sides], axis=1
    )
    inner_product = jnp.dot(
        leaf_inverse, columns, precision=lax.Precision.HIGHEST, preferred_element_type=jnp.float32
    )
    applied = jnp.einsum("qp,qc->pc", leaf_inverse, inner_product, precision=lax.Precision.HIGHEST)
    coupling = coupling_inverse(basis_rank)
    for height in range(levels):
        products = jnp.einsum(
            "pr,pc->rc", basis_blocks[height], applied, precision=lax.Precision.HIGHEST
        )
        summed = subtree_sum(products, height, inner_bits)
        sibling, is_first = sibling_of(summed, height, inner_bits)
        first_block = jnp.where(is_first, summed, sibling)
        second_block = jnp.where(is_first, sibling, summed)
        weights = node_weights(first_block, second_block, coupling, basis_rank)
        own_weights = jnp.where(is_first, weights[:basis_rank], weights[basis_rank:])
        applied = applied[:, basis_rank:] - jnp.dot(
            applied[:, :basis_rank],
            own_weights,
            precision=lax.Precision.HIGHEST,
            preferred_element_type=jnp.float32,
        )
    solution = jnp.zeros_like(right_sides).at[point_order].set(applied)
    return solution


def solution(mesh):
    in_specs = (
        P(("outer", "inner"), None),
        P(("outer", "inner"), None),
        P(("outer", "inner"), None),
        P(None, ("outer", "inner"), None),
    )
    out_specs = P(("outer", "inner"), None)
    return jax.shard_map(body, mesh=mesh, in_specs=in_specs, out_specs=out_specs, check_vma=False)
```

profile of v0, /device:TPU:16, one launch (start us, length us, event | category | flops | bytes accessed | tf_op | source)
XLA Modules:
  0.0 1414.7 jit_solution(6814168345176006871)
XLA Ops:
  13.3 14.6 %collective-permute-done = f32[128,1280]{0,1:T(8,128)} collective-permute-done((f32[128,1280]{0,1:T(8,128)S(1)}, f32[128,1280]{0,1:T(8,128)}, u32[]{:S(2)}, u32[]{:S(2)}) %collective-permute-start) | collective-permute-done | bytes 655392 | tf_op jit(solution)/shard_map/ppermute | solution.py:14
  71.6 19.7 %custom-call.71 = f32[2,128,128]{1,2,0:T(8,128)S(1)} custom-call(f32[2,128,128]{2,1,0:T(8,128)S(1)} %get-tuple-element.13), custom_call_target="InvertDiagBlocksLowerTriangular" | custom-call | tf_op jit(solution)/shard_map/jit(_solve_triangular)/triangular_solve | solution.py:50
  119.6 24.1 %collective-permute-done.2 = f32[128,1152]{0,1:T(8,128)} collective-permute-done((f32[128,1152]{0,1:T(8,128)S(1)}, f32[128,1152]{0,1:T(8,128)}, u32[]{:S(2)}, u32[]{:S(2)}) %collective-permute-start.2) | collective-permute-done | bytes 589856 | tf_op jit(solution)/shard_map/ppermute | solution.py:14
  185.9 19.7 %custom-call.72 = f32[2,128,128]{1,2,0:T(8,128)S(1)} custom-call(f32[2,128,128]{2,1,0:T(8,128)S(1)} %get-tuple-element.21), custom_call_target="InvertDiagBlocksLowerTriangular" | custom-call | tf_op jit(solution)/shard_map/jit(_solve_triangular)/triangular_solve | solution.py:50
  231.1 22.6 %collective-permute-done.4 = f32[128,1024]{0,1:T(8,128)S(1)} collective-permute-done((f32[128,1024]{0,1:T(8,128)S(1)}, f32[128,1024]{0,1:T(8,128)S(1)}, u32[]{:S(2)}, u32[]{:S(2)}) %collective-permute-start.4) | collective-permute-done | bytes 524320 | tf_op jit(solution)/shard_map/ppermute | solution.py:14
  263.1 43.8 %collective-permute-done.5 = f32[128,1024]{0,1:T(8,128)} collective-permute-done((f32[128,1024]{0,1:T(8,128)S(1)}, f32[128,1024]{0,1:T(8,128)}, u32[]{:S(2)}, u32[]{:S(2)}) %collective-permute-start.5) | collective-permute-done | bytes 524320 | tf_op jit(solution)/shard_map/ppermute | solution.py:14
  349.3 19.7 %custom-call.73 = f32[2,128,128]{1,2,0:T(8,128)S(1)} custom-call(f32[2,128,128]{2,1,0:T(8,128)S(1)} %get-tuple-element.29), custom_call_target="InvertDiagBlocksLowerTriangular" | custom-call | tf_op jit(solution)/shard_map/jit(_solve_triangular)/triangular_solve | solution.py:50
  390.5 22.3 %collective-permute-done.7 = f32[128,896]{0,1:T(8,128)S(1)} collective-permute-done((f32[128,896]{0,1:T(8,128)S(1)}, f32[128,896]{0,1:T(8,128)S(1)}, u32[]{:S(2)}, u32[]{:S(2)}) %collective-permute-start.7) | collective-permute-done | bytes 458784 | tf_op jit(solution)/shard_map/ppermute | solution.py:14
  418.4 50.3 %collective-permute-done.8 = f32[128,896]{0,1:T(8,128)S(1)} collective-permute-done((f32[128,896]{0,1:T(8,128)S(1)}, f32[128,896]{0,1:T(8,128)S(1)}, u32[]{:S(2)}, u32[]{:S(2)}) %collective-permute-start.8) | collective-permute-done | bytes 458784 | tf_op jit(solution)/shard_map/ppermute | solution.py:14
  479.8 14.7 %collective-permute-done.9 = f32[128,896]{0,1:T(8,128)} collective-permute-done((f32[128,896]{0,1:T(8,128)S(1)}, f32[128,896]{0,1:T(8,128)}, u32[]{:S(2)}, u32[]{:S(2)}) %collective-permute-start.9) | collective-permute-done | bytes 458784 | tf_op jit(solution)/shard_map/ppermute | solution.py:14
  536.7 19.7 %custom-call.74 = f32[2,128,128]{1,2,0:T(8,128)S(1)} custom-call(f32[2,128,128]{2,1,0:T(8,128)S(1)} %get-tuple-element.37), custom_call_target="InvertDiagBlocksLowerTriangular" | custom-call | tf_op jit(solution)/shard_map/jit(_solve_triangular)/triangular_solve | solution.py:50
  573.9 14.3 %collective-permute-start.11 = (f32[128,768]{0,1:T(8,128)S(1)}, f32[128,768]{0,1:T(8,128)S(1)}, u32[]{:S(2)}, u32[]{:S(2)}) collective-permute-start(f32[128,768]{0,1:T(8,128)S(1)} %add.260), channel_id=1, source_target_pairs={{0,2},{2,0},{1,3},{3,1},{4,6},{6,4},{5,7},{7,5},{8,10},{10,8},{9,1... | collective-permute-start | bytes 1179656 | tf_op jit(solution)/shard_map/ppermute | solution.py:14
  588.2 17.0 %collective-permute-done.11 = f32[128,768]{0,1:T(8,128)S(1)} collective-permute-done((f32[128,768]{0,1:T(8,128)S(1)}, f32[128,768]{0,1:T(8,128)S(1)}, u32[]{:S(2)}, u32[]{:S(2)}) %collective-permute-start.11) | collective-permute-done | bytes 393248 | tf_op jit(solution)/shard_map/ppermute | solution.py:14
  612.2 33.5 %collective-permute-done.12 = f32[128,768]{0,1:T(8,128)S(1)} collective-permute-done((f32[128,768]{0,1:T(8,128)S(1)}, f32[128,768]{0,1:T(8,128)S(1)}, u32[]{:S(2)}, u32[]{:S(2)}) %collective-permute-start.12) | collective-permute-done | bytes 393248 | tf_op jit(solution)/shard_map/ppermute | solution.py:14
  645.7 19.6 %collective-permute-start.13 = (f32[128,768]{0,1:T(8,128)S(1)}, f32[128,768]{0,1:T(8,128)S(1)}, u32[]{:S(2)}, u32[]{:S(2)}) collective-permute-start(f32[128,768]{0,1:T(8,128)S(1)} %add.262), channel_id=1, source_target_pairs={{0,8},{8,0},{1,9},{9,1},{2,10},{10,2},{3,11},{11,3},{4,12},{12,4},... | collective-permute-start | bytes 1179656 | tf_op jit(solution)/shard_map/ppermute | solution.py:14
  665.4 19.7 %collective-permute-done.13 = f32[128,768]{0,1:T(8,128)S(1)} collective-permute-done((f32[128,768]{0,1:T(8,128)S(1)}, f32[128,768]{0,1:T(8,128)S(1)}, u32[]{:S(2)}, u32[]{:S(2)}) %collective-permute-start.13) | collective-permute-done | bytes 393248 | tf_op jit(solution)/shard_map/ppermute | solution.py:14
  729.7 19.7 %custom-call.75 = f32[2,128,128]{1,2,0:T(8,128)S(1)} custom-call(f32[2,128,128]{2,1,0:T(8,128)S(1)} %get-tuple-element.45), custom_call_target="InvertDiagBlocksLowerTriangular" | custom-call | tf_op jit(solution)/shard_map/jit(_solve_triangular)/triangular_solve | solution.py:50
  770.9 14.5 %collective-permute-done.16 = f32[128,640]{0,1:T(8,128)S(1)} collective-permute-done((f32[128,640]{0,1:T(8,128)S(1)}, f32[128,640]{0,1:T(8,128)S(1)}, u32[]{:S(2)}, u32[]{:S(2)}) %collective-permute-start.16) | collective-permute-done | bytes 327712 | tf_op jit(solution)/shard_map/ppermute | solution.py:14
  791.9 28.1 %collective-permute-done.17 = f32[128,640]{0,1:T(8,128)S(1)} collective-permute-done((f32[128,640]{0,1:T(8,128)S(1)}, f32[128,640]{0,1:T(8,128)S(1)}, u32[]{:S(2)}, u32[]{:S(2)}) %collective-permute-start.17) | collective-permute-done | bytes 327712 | tf_op jit(solution)/shard_map/ppermute | solution.py:14
  820.0 18.1 %collective-permute-start.18 = (f32[128,640]{0,1:T(8,128)S(1)}, f32[128,640]{0,1:T(8,128)S(1)}, u32[]{:S(2)}, u32[]{:S(2)}) collective-permute-start(f32[128,640]{0,1:T(8,128)S(1)} %add.267), channel_id=1, source_target_pairs={{0,8},{8,0},{1,9},{9,1},{2,10},{10,2},{3,11},{11,3},{4,12},{12,4},... | collective-permute-start | bytes 983048 | tf_op jit(solution)/shard_map/ppermute | solution.py:14
  838.1 19.9 %collective-permute-done.18 = f32[128,640]{0,1:T(8,128)S(1)} collective-permute-done((f32[128,640]{0,1:T(8,128)S(1)}, f32[128,640]{0,1:T(8,128)S(1)}, u32[]{:S(2)}, u32[]{:S(2)}) %collective-permute-start.18) | collective-permute-done | bytes 327712 | tf_op jit(solution)/shard_map/ppermute | solution.py:14
  914.0 19.7 %custom-call.76 = f32[2,128,128]{1,2,0:T(8,128)S(1)} custom-call(f32[2,128,128]{2,1,0:T(8,128)S(1)} %get-tuple-element.53), custom_call_target="InvertDiagBlocksLowerTriangular" | custom-call | tf_op jit(solution)/shard_map/jit(_solve_triangular)/triangular_solve | solution.py:50
  948.7 13.1 collective-permute-done.22
  965.2 23.6 %collective-permute-done.23 = f32[128,512]{0,1:T(8,128)S(1)} collective-permute-done((f32[128,512]{0,1:T(8,128)S(1)}, f32[128,512]{0,1:T(8,128)S(1)}, u32[]{:S(2)}, u32[]{:S(2)}) %collective-permute-start.23) | collective-permute-done | bytes 262176 | tf_op jit(solution)/shard_map/ppermute | solution.py:14
  988.8 15.7 %collective-permute-start.24 = (f32[128,512]{0,1:T(8,128)S(1)}, f32[128,512]{0,1:T(8,128)S(1)}, u32[]{:S(2)}, u32[]{:S(2)}) collective-permute-start(f32[128,512]{0,1:T(8,128)S(1)} %add.273), channel_id=1, source_target_pairs={{0,8},{8,0},{1,9},{9,1},{2,10},{10,2},{3,11},{11,3},{4,12},{12,4},... | collective-permute-start | bytes 786440 | tf_op jit(solution)/shard_map/ppermute | solution.py:14
  1004.4 17.1 %collective-permute-done.24 = f32[128,512]{0,1:T(8,128)S(1)} collective-permute-done((f32[128,512]{0,1:T(8,128)S(1)}, f32[128,512]{0,1:T(8,128)S(1)}, u32[]{:S(2)}, u32[]{:S(2)}) %collective-permute-start.24) | collective-permute-done | bytes 262176 | tf_op jit(solution)/shard_map/ppermute | solution.py:14
  1087.0 19.7 %custom-call.77 = f32[2,128,128]{1,2,0:T(8,128)S(1)} custom-call(f32[2,128,128]{2,1,0:T(8,128)S(1)} %get-tuple-element.61), custom_call_target="InvertDiagBlocksLowerTriangular" | custom-call | tf_op jit(solution)/shard_map/jit(_solve_triangular)/triangular_solve | solution.py:50
  1131.4 17.7 %collective-permute-done.30 = f32[128,384]{0,1:T(8,128)S(1)} collective-permute-done((f32[128,384]{0,1:T(8,128)S(1)}, f32[128,384]{0,1:T(8,128)S(1)}, u32[]{:S(2)}, u32[]{:S(2)}) %collective-permute-start.30) | collective-permute-done | bytes 196640 | tf_op jit(solution)/shard_map/ppermute | solution.py:14
  1157.7 15.3 %collective-permute-done.31 = f32[128,384]{0,1:T(8,128)S(1)} collective-permute-done((f32[128,384]{0,1:T(8,128)S(1)}, f32[128,384]{0,1:T(8,128)S(1)}, u32[]{:S(2)}, u32[]{:S(2)}) %collective-permute-start.31) | collective-permute-done | bytes 196640 | tf_op jit(solution)/shard_map/ppermute | solution.py:14
  1246.9 19.7 %custom-call.78 = f32[2,128,128]{1,2,0:T(8,128)S(1)} custom-call(f32[2,128,128]{2,1,0:T(8,128)S(1)} %get-tuple-element.69), custom_call_target="InvertDiagBlocksLowerTriangular" | custom-call | tf_op jit(solution)/shard_map/jit(_solve_triangular)/triangular_solve | solution.py:50
  1286.6 13.4 collective-permute-done.38
  1391.1 19.7 %custom-call.79 = f32[2,128,128]{1,2,0:T(8,128)S(1)} custom-call(f32[2,128,128]{2,1,0:T(8,128)S(1)} %get-tuple-element.77), custom_call_target="InvertDiagBlocksLowerTriangular" | custom-call | tf_op jit(solution)/shard_map/jit(_solve_triangular)/triangular_solve | solution.py:50
  (445 shorter events, 766.0 us)
Async XLA Ops:
  9.2 18.7 %collective-permute-start = (f32[128,1280]{0,1:T(8,128)S(1)}, f32[128,1280]{0,1:T(8,128)}, u32[]{:S(2)}, u32[]{:S(2)}) collective-permute-start(f32[128,1280]{0,1:T(8,128)S(1)} %convolution_bitcast_fusion.1), channel_id=1, source_target_pairs={{0,1},{1,0},{2,3},{3,2},{4,5},{5,4},{6,7},{7,6},{8,9},{9,8},{10,11... | collective-permute-start | bytes 1966088 | tf_op jit(solution)/shard_map/ppermute | solution.py:14
  97.5 16.3 %collective-permute-start.1 = (f32[128,1152]{0,1:T(8,128)S(1)}, f32[128,1152]{0,1:T(8,128)S(1)}, u32[]{:S(2)}, u32[]{:S(2)}) collective-permute-start(f32[128,1152]{0,1:T(8,128)S(1)} %convolution_bitcast_fusion), channel_id=1, source_target_pairs={{0,1},{1,0},{2,3},{3,2},{4,5},{5,4},{6,7},{7,6},{8,9},{9,8},{10,11... | collective-permute-start | bytes 1769480 | tf_op jit(solution)/shard_map/ppermute | solution.py:14
  113.9 29.7 %collective-permute-start.2 = (f32[128,1152]{0,1:T(8,128)S(1)}, f32[128,1152]{0,1:T(8,128)}, u32[]{:S(2)}, u32[]{:S(2)}) collective-permute-start(f32[128,1152]{0,1:T(8,128)S(1)} %add.251), channel_id=1, source_target_pairs={{0,2},{2,0},{1,3},{3,1},{4,6},{6,4},{5,7},{7,5},{8,10},{10,8},{9,1... | collective-permute-start | bytes 1769480 | tf_op jit(solution)/shard_map/ppermute | solution.py:14
  211.2 15.0 %collective-permute-start.3 = (f32[128,1024]{0,1:T(8,128)S(1)}, f32[128,1024]{0,1:T(8,128)S(1)}, u32[]{:S(2)}, u32[]{:S(2)}) collective-permute-start(f32[128,1024]{0,1:T(8,128)S(1)} %convolution_bitcast_fusion.2), channel_id=1, source_target_pairs={{0,1},{1,0},{2,3},{3,2},{4,5},{5,4},{6,7},{7,6},{8,9},{9,8},{10,11... | collective-permute-start | bytes 1572872 | tf_op jit(solution)/shard_map/ppermute | solution.py:14
  226.2 27.5 %collective-permute-start.4 = (f32[128,1024]{0,1:T(8,128)S(1)}, f32[128,1024]{0,1:T(8,128)S(1)}, u32[]{:S(2)}, u32[]{:S(2)}) collective-permute-start(f32[128,1024]{0,1:T(8,128)S(1)} %add.253), channel_id=1, source_target_pairs={{0,2},{2,0},{1,3},{3,1},{4,6},{6,4},{5,7},{7,5},{8,10},{10,8},{9,1... | collective-permute-start | bytes 1572872 | tf_op jit(solution)/shard_map/ppermute | solution.py:14
  253.8 53.1 %collective-permute-start.5 = (f32[128,1024]{0,1:T(8,128)S(1)}, f32[128,1024]{0,1:T(8,128)}, u32[]{:S(2)}, u32[]{:S(2)}) collective-permute-start(f32[128,1024]{0,1:T(8,128)S(1)} %add.254), channel_id=1, source_target_pairs={{0,4},{4,0},{1,5},{5,1},{2,6},{6,2},{3,7},{7,3},{8,12},{12,8},{9,1... | collective-permute-start | bytes 1572872 | tf_op jit(solution)/shard_map/ppermute | solution.py:14
  374.2 14.3 %collective-permute-start.6 = (f32[128,896]{0,1:T(8,128)S(1)}, f32[128,896]{0,1:T(8,128)S(1)}, u32[]{:S(2)}, u32[]{:S(2)}) collective-permute-start(f32[128,896]{0,1:T(8,128)S(1)} %convolution_bitcast_fusion.3), channel_id=1, source_target_pairs={{0,1},{1,0},{2,3},{3,2},{4,5},{5,4},{6,7},{7,6},{8,9},{9,8},{10,11... | collective-permute-start | bytes 1376264 | tf_op jit(solution)/shard_map/ppermute | solution.py:14
  388.6 24.2 %collective-permute-start.7 = (f32[128,896]{0,1:T(8,128)S(1)}, f32[128,896]{0,1:T(8,128)S(1)}, u32[]{:S(2)}, u32[]{:S(2)}) collective-permute-start(f32[128,896]{0,1:T(8,128)S(1)} %add.256), channel_id=1, source_target_pairs={{0,2},{2,0},{1,3},{3,1},{4,6},{6,4},{5,7},{7,5},{8,10},{10,8},{9,1... | collective-permute-start | bytes 1376264 | tf_op jit(solution)/shard_map/ppermute | solution.py:14
  412.9 55.8 %collective-permute-start.8 = (f32[128,896]{0,1:T(8,128)S(1)}, f32[128,896]{0,1:T(8,128)S(1)}, u32[]{:S(2)}, u32[]{:S(2)}) collective-permute-start(f32[128,896]{0,1:T(8,128)S(1)} %add.257), channel_id=1, source_target_pairs={{0,4},{4,0},{1,5},{5,1},{2,6},{6,2},{3,7},{7,3},{8,12},{12,8},{9,1... | collective-permute-start | bytes 1376264 | tf_op jit(solution)/shard_map/ppermute | solution.py:14
  468.7 25.8 %collective-permute-start.9 = (f32[128,896]{0,1:T(8,128)S(1)}, f32[128,896]{0,1:T(8,128)}, u32[]{:S(2)}, u32[]{:S(2)}) collective-permute-start(f32[128,896]{0,1:T(8,128)S(1)} %add.258), channel_id=1, source_target_pairs={{0,8},{8,0},{1,9},{9,1},{2,10},{10,2},{3,11},{11,3},{4,12},{12,4},... | collective-permute-start | bytes 1376264 | tf_op jit(solution)/shard_map/ppermute | solution.py:14
  561.0 12.9 collective-permute-start.10
  573.9 31.3 %collective-permute-start.11 = (f32[128,768]{0,1:T(8,128)S(1)}, f32[128,768]{0,1:T(8,128)S(1)}, u32[]{:S(2)}, u32[]{:S(2)}) collective-permute-start(f32[128,768]{0,1:T(8,128)S(1)} %add.260), channel_id=1, source_target_pairs={{0,2},{2,0},{1,3},{3,1},{4,6},{6,4},{5,7},{7,5},{8,10},{10,8},{9,1... | collective-permute-start | bytes 1179656 | tf_op jit(solution)/shard_map/ppermute | solution.py:14
  605.3 40.4 %collective-permute-start.12 = (f32[128,768]{0,1:T(8,128)S(1)}, f32[128,768]{0,1:T(8,128)S(1)}, u32[]{:S(2)}, u32[]{:S(2)}) collective-permute-start(f32[128,768]{0,1:T(8,128)S(1)} %add.261), channel_id=1, source_target_pairs={{0,4},{4,0},{1,5},{5,1},{2,6},{6,2},{3,7},{7,3},{8,12},{12,8},{9,1... | collective-permute-start | bytes 1179656 | tf_op jit(solution)/shard_map/ppermute | solution.py:14
  645.7 39.3 %collective-permute-start.13 = (f32[128,768]{0,1:T(8,128)S(1)}, f32[128,768]{0,1:T(8,128)S(1)}, u32[]{:S(2)}, u32[]{:S(2)}) collective-permute-start(f32[128,768]{0,1:T(8,128)S(1)} %add.262), channel_id=1, source_target_pairs={{0,8},{8,0},{1,9},{9,1},{2,10},{10,2},{3,11},{11,3},{4,12},{12,4},... | collective-permute-start | bytes 1179656 | tf_op jit(solution)/shard_map/ppermute | solution.py:14
  753.6 11.7 collective-permute-start.15
  765.3 20.0 %collective-permute-start.16 = (f32[128,640]{0,1:T(8,128)S(1)}, f32[128,640]{0,1:T(8,128)S(1)}, u32[]{:S(2)}, u32[]{:S(2)}) collective-permute-start(f32[128,640]{0,1:T(8,128)S(1)} %add.265), channel_id=1, source_target_pairs={{0,2},{2,0},{1,3},{3,1},{4,6},{6,4},{5,7},{7,5},{8,10},{10,8},{9,1... | collective-permute-start | bytes 983048 | tf_op jit(solution)/shard_map/ppermute | solution.py:14
  785.4 34.6 %collective-permute-start.17 = (f32[128,640]{0,1:T(8,128)S(1)}, f32[128,640]{0,1:T(8,128)S(1)}, u32[]{:S(2)}, u32[]{:S(2)}) collective-permute-start(f32[128,640]{0,1:T(8,128)S(1)} %add.266), channel_id=1, source_target_pairs={{0,4},{4,0},{1,5},{5,1},{2,6},{6,2},{3,7},{7,3},{8,12},{12,8},{9,1... | collective-permute-start | bytes 983048 | tf_op jit(solution)/shard_map/ppermute | solution.py:14
  820.0 38.0 %collective-permute-start.18 = (f32[128,640]{0,1:T(8,128)S(1)}, f32[128,640]{0,1:T(8,128)S(1)}, u32[]{:S(2)}, u32[]{:S(2)}) collective-permute-start(f32[128,640]{0,1:T(8,128)S(1)} %add.267), channel_id=1, source_target_pairs={{0,8},{8,0},{1,9},{9,1},{2,10},{10,2},{3,11},{11,3},{4,12},{12,4},... | collective-permute-start | bytes 983048 | tf_op jit(solution)/shard_map/ppermute | solution.py:14
  861.6 11.6 collective-permute-start.20
  937.3 9.4 collective-permute-start.21
  946.7 15.0 %collective-permute-start.22 = (f32[128,512]{0,1:T(8,128)S(1)}, f32[128,512]{0,1:T(8,128)S(1)}, u32[]{:S(2)}, u32[]{:S(2)}) collective-permute-start(f32[128,512]{0,1:T(8,128)S(1)} %add.271), channel_id=1, source_target_pairs={{0,2},{2,0},{1,3},{3,1},{4,6},{6,4},{5,7},{7,5},{8,10},{10,8},{9,1... | collective-permute-start | bytes 786440 | tf_op jit(solution)/shard_map/ppermute | solution.py:14
  961.8 26.9 %collective-permute-start.23 = (f32[128,512]{0,1:T(8,128)S(1)}, f32[128,512]{0,1:T(8,128)S(1)}, u32[]{:S(2)}, u32[]{:S(2)}) collective-permute-start(f32[128,512]{0,1:T(8,128)S(1)} %add.272), channel_id=1, source_target_pairs={{0,4},{4,0},{1,5},{5,1},{2,6},{6,2},{3,7},{7,3},{8,12},{12,8},{9,1... | collective-permute-start | bytes 786440 | tf_op jit(solution)/shard_map/ppermute | solution.py:14
  988.8 32.8 %collective-permute-start.24 = (f32[128,512]{0,1:T(8,128)S(1)}, f32[128,512]{0,1:T(8,128)S(1)}, u32[]{:S(2)}, u32[]{:S(2)}) collective-permute-start(f32[128,512]{0,1:T(8,128)S(1)} %add.273), channel_id=1, source_target_pairs={{0,8},{8,0},{1,9},{9,1},{2,10},{10,2},{3,11},{11,3},{4,12},{12,4},... | collective-permute-start | bytes 786440 | tf_op jit(solution)/shard_map/ppermute | solution.py:14
  1025.1 10.2 collective-permute-start.26
  1035.3 10.9 collective-permute-start.27
  1117.4 10.8 collective-permute-start.29
  1128.2 20.9 %collective-permute-start.30 = (f32[128,384]{0,1:T(8,128)S(1)}, f32[128,384]{0,1:T(8,128)S(1)}, u32[]{:S(2)}, u32[]{:S(2)}) collective-permute-start(f32[128,384]{0,1:T(8,128)S(1)} %add.279), channel_id=1, source_target_pairs={{0,4},{4,0},{1,5},{5,1},{2,6},{6,2},{3,7},{7,3},{8,12},{12,8},{9,1... | collective-permute-start | bytes 589832 | tf_op jit(solution)/shard_map/ppermute | solution.py:14
  1149.1 23.9 %collective-permute-start.31 = (f32[128,384]{0,1:T(8,128)S(1)}, f32[128,384]{0,1:T(8,128)S(1)}, u32[]{:S(2)}, u32[]{:S(2)}) collective-permute-start(f32[128,384]{0,1:T(8,128)S(1)} %add.280), channel_id=1, source_target_pairs={{0,8},{8,0},{1,9},{9,1},{2,10},{10,2},{3,11},{11,3},{4,12},{12,4},... | collective-permute-start | bytes 589832 | tf_op jit(solution)/shard_map/ppermute | solution.py:14
  1185.3 9.5 collective-permute-start.34
  1194.8 11.3 collective-permute-start.35
  1284.6 15.4 %collective-permute-start.38 = (f32[128,256]{0,1:T(8,128)S(1)}, f32[128,256]{0,1:T(8,128)S(1)}, u32[]{:S(2)}, u32[]{:S(2)}) collective-permute-start(f32[128,256]{0,1:T(8,128)S(1)} %add.287), channel_id=1, source_target_pairs={{0,4},{4,0},{1,5},{5,1},{2,6},{6,2},{3,7},{7,3},{8,12},{12,8},{9,1... | collective-permute-start | bytes 393224 | tf_op jit(solution)/shard_map/ppermute | solution.py:14
  1300.0 15.6 %collective-permute-start.39 = (f32[128,256]{0,1:T(8,128)S(1)}, f32[128,256]{0,1:T(8,128)S(1)}, u32[]{:S(2)}, u32[]{:S(2)}) collective-permute-start(f32[128,256]{0,1:T(8,128)S(1)} %add.288), channel_id=1, source_target_pairs={{0,8},{8,0},{1,9},{9,1},{2,10},{10,2},{3,11},{11,3},{4,12},{12,4},... | collective-permute-start | bytes 393224 | tf_op jit(solution)/shard_map/ppermute | solution.py:14
  (21 other events, 117.8 us)
where the time goes:
time: 1420 us; the launch traced here: 1410 us
  waiting for transfers between devices  589 us (41%)
  other arithmetic  497 us (35%)
  starting transfers between devices  223 us (16%)
  local copies, waits for them, and re-layouts  45.3 us (3%)
  matrix products  43.4 us (3%)
    ppermute x45, waiting for transfers between devices, swapped(): return lax.ppermute(block, axis, route)  589 us
    another operation x63, other arithmetic, node_weights(): factor_low = jnp.linalg.cholesky(system)  312 us
    ppermute x45, starting transfers between devices, swapped(): return lax.ppermute(block, axis, route)  223 us
    another operation x19, other arithmetic, node_weights(): jax.scipy.linalg.solve_triangular(factor_low, middle, lower=True, trans=1)  177 us
    another operation x54, local copies, waits for them, and re-layouts  35.1 us
  transfers between devices with their start and end apart: 45, of which 45 were waited for; matrix products, arithmetic and copies ran while one was open for 0% of the time, Pallas kernels for 0%

commit v1 on v0

v1 whole, which is shorter than its diff:
```python
import functools

import jax
import jax.numpy as jnp
from jax import lax
from jax.experimental import pallas as pl
from jax.experimental.pallas import tpu as pltpu
from jax.sharding import PartitionSpec as P

B = 128
F32 = jnp.float32


def mm(a, b):
    return jnp.dot(a, b, precision=lax.Precision.HIGHEST, preferred_element_type=F32)


def tn(a, b):
    return lax.dot_general(
        a, b, (((0,), (0,)), ((), ())), precision=lax.Precision.HIGHEST, preferred_element_type=F32
    )


def eye():
    return (
        lax.broadcasted_iota(jnp.int32, (B, B), 0) == lax.broadcasted_iota(jnp.int32, (B, B), 1)
    ).astype(F32)


def sl(i, j):
    return slice(i * B, j * B)


def unit_inverse(grams, x_ref, r_ref):
    unit = eye()
    count = len(grams)
    h = jnp.ones((1, 1), F32)
    for g in grams:
        h = jnp.maximum(
            h, jnp.max(jnp.sum(jnp.abs(g), axis=0, keepdims=True), axis=1, keepdims=True)
        )
    s = 2.0 / h
    s = 2.0 * s * (s + 2.0)
    left = jnp.zeros((1, 1), jnp.int32)
    ahead = s
    for _ in range(14):
        left = left + (ahead < 4000.0).astype(jnp.int32)
        ahead = 2.0 * ahead * (ahead + 2.0)
    steps = jnp.max(left)
    inv_t = 1.0 / (1.0 + s)
    c = 1.0 + inv_t
    scale = 2.0 / (h + 2.0)
    for k, g in enumerate(grams):
        r = (h * unit - 2.0 * g) / (h + 2.0)
        x_ref[k] = (c * scale) * (unit + r)
        r_ref[k] = c * mm(r, r) - inv_t * unit

    def double(_, s):
        s = 2.0 * s * (s + 2.0)
        inv_t = 1.0 / (1.0 + s)
        c = 1.0 + inv_t
        for k in range(count):
            r = r_ref[k]
            x = x_ref[k]
            x_ref[k] = c * (x + mm(x, r))
            r_ref[k] = c * mm(r, r) - inv_t * unit
        return s

    lax.fori_loop(0, steps, double, s)
    found = []
    for k, g in enumerate(grams):
        x = x_ref[k]
        found.append(x + mm(x, unit - x - mm(g, x)))
    return found


def pair_inverse(s_first, s_second):
    unit = eye()
    r = 0.5 * (s_first + s_second - unit)
    t = 7.0
    x = (0.5 * (1.0 + 1.0 / t)) * (unit + r)
    r = (1.0 + 1.0 / t) * mm(r, r) - (1.0 / t) * unit
    for last in (False, False, True):
        t = 2.0 * t * t - 1.0
        c = 1.0 + 1.0 / t
        x = c * (x + mm(x, r))
        if not last:
            r = c * mm(r, r) - (1.0 / t) * unit
    return x


def leaf_kernel(nb, order_ref, r_ref, u_ref, rhs_ref, z_ref, x_scr, r_scr):
    pick = (lax.broadcasted_iota(jnp.int32, (B, B), 0) == order_ref[...]).astype(F32)
    r = r_ref[...]
    for b in range(nb - 1):
        z_ref[:, sl(b, b + 1)] = mm(r, u_ref[b])
    z_ref[:, sl(nb - 1, nb)] = mm(r, tn(pick, rhs_ref[...]))
    z0 = z_ref[:, sl(0, 1)]
    (s,) = unit_inverse([tn(z0, z0)], x_scr, r_scr)
    z_ref[:, sl(nb, nb + 1)] = s


def quad_kernel(nb, slots, table_ref, zs0, zs1, zs2, zs3, act_ref, pas_ref, own_ref, z, y, w, x1, m2_scr, n2_scr, x_scr, r_scr, sem):
    last = nb - 1
    copies = [
        pltpu.make_async_copy(src, z.at[pl.ds(i * B, B)], sem.at[i])
        for i, src in enumerate((zs0, zs1, zs2, zs3))
    ]
    for copy in copies:
        copy.start()
    for copy in copies:
        copy.wait()
    w0 = (nb - 1) * B

    def first(i, carry):
        rows = pl.ds(pl.multiple_of(i * B, B), B)
        p = tn(z[rows, sl(0, 1)], z[rows, sl(1, nb)])
        w[rows, :] = mm(z[rows, sl(nb, nb + 1)], p)
        return carry

    lax.fori_loop(0, 4, first, 0)
    for n in range(2):
        a, b = slice(2 * n * B, (2 * n + 1) * B), slice((2 * n + 1) * B, (2 * n + 2) * B)
        t = pair_inverse(z[a, sl(nb, nb + 1)], z[b, sl(nb, nb + 1)])
        x1[n] = mm(t, w[a, :] + w[b, :])

    def second(i, carry):
        rows = pl.ds(pl.multiple_of(i * B, B), B)
        x = x1[i // 2]
        weights = w[rows, :] + mm(z[rows, sl(nb, nb + 1)], x)
        y[rows, sl(1, nb)] = z[rows, sl(1, nb)] - mm(z[rows, sl(0, 1)], weights)
        return carry

    lax.fori_loop(0, 4, second, 0)
    rows = [slice(0, 2 * B), slice(2 * B, 4 * B)]
    m = [tn(z[rows[n], sl(1, 2)], y[rows[n], sl(1, nb)]) for n in range(2)]
    s = unit_inverse([m[n][:, :B] for n in range(2)], x_scr, r_scr)
    nn = [mm(s[n], m[n][:, B:]) for n in range(2)]
    x = mm(pair_inverse(s[0], s[1]), nn[0] + nn[1])
    for n in range(2):
        weights = nn[n] + mm(s[n], x)
        y[rows[n], sl(2, nb)] = y[rows[n], sl(2, nb)] - mm(y[rows[n], sl(1, 2)], weights)
    m2 = tn(z[:, sl(2, 3)], y[:, sl(2, nb)])
    (s2,) = unit_inverse([m2[:, :B]], x_scr, r_scr)
    n2 = mm(s2, m2[:, B:])
    m2_scr[...] = m2
    n2_scr[...] = n2
    m3 = tn(z[:, sl(3, 4)], y[:, sl(3, nb)]) - tn(m2[:, sl(1, 2)], n2)
    wide = nb - 3
    act_ref[:, sl(0, 1)] = s2
    act_ref[:, sl(1, 1 + wide)] = n2
    act_ref[:, sl(1 + wide, 1 + 2 * wide)] = m3
    total = act_ref.shape[1] // B
    if total > 1 + 2 * wide:
        act_ref[:, sl(1 + 2 * wide, total)] = jnp.zeros((B, (total - 1 - 2 * wide) * B), F32)
    y2 = y[0:B, sl(2, 3)]
    own_ref[:, sl(1, nb - 2)] = y[0:B, sl(3, nb)] - mm(y2, n2)
    own_ref[:, sl(0, 1)] = mm(y2, s2)

    def passive(k, carry):
        a = table_ref[0, k]
        b = table_ref[1, k]

        def at(block):
            return pl.ds(pl.multiple_of(block * B, B), B)

        pas_ref[:, at(k)] = tn(z[:, at(a)], y[:, at(b)]) - tn(m2_scr[:, at(a - 2)], n2_scr[:, at(b - 3)])
        return carry

    lax.fori_loop(0, slots, passive, 0)


def ring_kernel(nb, share, slots, side_ref, act_ref, own_ref, pay_ref, out_ref, la, lb, q, m, nn, tot, x_scr, r_scr, s_scr):
    wide = nb - 3
    deep = nb - 4

    def piece(group, k):
        return act_ref[4 * group + k // share, :, sl(k % share, k % share + 1)]

    for node in range(2):
        g, h = 2 * node, 2 * node + 1
        for k in range(wide):
            q[node, :, sl(k, k + 1)] = piece(g, 1 + k) + piece(h, 1 + k)
        t = pair_inverse(piece(g, 0), piece(h, 0))
        x = mm(t, q[node])
        m[node] = x
        lb[sl(node, node + 1), :] = x[:, B:]
        la[sl(node, node + 1), :] = q[node, :, B:]
        m3 = tn(q[node, :, :B], x)
        for k in range(wide):
            nn[node, :, sl(k, k + 1)] = (
                piece(g, 1 + wide + k) + piece(h, 1 + wide + k) - m3[:, sl(k, k + 1)]
            )
    s = unit_inverse([nn[0, :, :B], nn[1, :, :B]], x_scr, r_scr)
    for node in range(2):
        s_scr[node] = s[node]
        la[sl(2 + node, 3 + node), :] = nn[node, :, B:]
        lb[sl(2 + node, 3 + node), :] = mm(s[node], nn[node, :, B:])
    q3 = lb[sl(2, 3), :] + lb[sl(3, 4), :]
    x3 = mm(pair_inverse(s[0], s[1]), q3)
    la[sl(4, 5), :] = q3
    lb[sl(4, 5), :] = x3
    at = 0
    for k in range(deep - 1):
        for b in range(k, deep):
            who, slot = (at + b - k) // slots, share + (at + b - k) % slots
            tot[:, sl(at + b - k, at + b - k + 1)] = (
                act_ref[who, :, sl(slot, slot + 1)]
                + act_ref[4 + who, :, sl(slot, slot + 1)]
                + act_ref[8 + who, :, sl(slot, slot + 1)]
                + act_ref[12 + who, :, sl(slot, slot + 1)]
            )
        part = sl(at, at + deep - k)
        tot[:, part] = tot[:, part] - tn(la[:, sl(k, k + 1)], lb[:, sl(k, deep)])
        at += deep - k

    def panel(a):
        at = sum(nb - k for k in range(4, a))
        return tot[:, sl(at, at + nb - a)]

    own_side(nb, 4, panel, pay_ref, x_scr, r_scr)
    side = side_ref[0]
    y = own_ref[:, sl(1, nb - 2)] - mm(own_ref[:, :B], m[side])
    n3 = lb[pl.ds(pl.multiple_of((2 + side) * B, B), B), :]
    weights = n3 + mm(s_scr[side], x3)
    out_ref[...] = y[:, B:] - mm(y[:, :B], weights)


def own_side(nb, level, m, pay_ref, x_scr, r_scr):
    row = m(level)
    wide = nb - 1 - level
    (s,) = unit_inverse([row[:, :B]], x_scr, r_scr)
    n = mm(s, row[:, B:])
    pay_ref[:, sl(0, 1)] = s
    pay_ref[:, sl(1, 1 + wide)] = n
    at = 1 + wide
    for a in range(level + 1, nb - 1):
        k = a - level
        pay_ref[:, sl(at, at + nb - a)] = m(a) - tn(
            row[:, sl(k, k + 1)], n[:, sl(k - 1, wide)]
        )
        at += nb - a


def merge_kernel(nb, level, own_ref, other_ref, pay_ref, x_ref, x_scr, r_scr):
    wide = nb - 1 - level
    q = own_ref[:, sl(1, 1 + wide)] + other_ref[:, sl(1, 1 + wide)]
    x = mm(pair_inverse(own_ref[:, :B], other_ref[:, :B]), q)
    x_ref[...] = x

    def panel(a):
        k = a - level - 1
        at = 1 + wide + sum(nb - j for j in range(level + 1, a))
        part = sl(at, at + nb - a)
        return own_ref[:, part] + other_ref[:, part] - tn(q[:, sl(k, k + 1)], x[:, sl(k, wide)])

    own_side(nb, level + 1, panel, pay_ref, x_scr, r_scr)


def update_kernel(pay_ref, x_ref, y_ref, out_ref):
    wide = x_ref.shape[1]
    weights = pay_ref[:, B : B + wide] + mm(pay_ref[:, :B], x_ref[...])
    out_ref[...] = y_ref[:, B:] - mm(y_ref[:, :B], weights)


def finish_kernel(order_ref, r_ref, own_ref, other_ref, y_ref, out_ref):
    s = own_ref[:, :B]
    n = own_ref[:, B:]
    x = mm(pair_inverse(s, other_ref[:, :B]), n + other_ref[:, B:])
    y = y_ref[:, B:] - mm(y_ref[:, :B], n + mm(s, x))
    pick = (lax.broadcasted_iota(jnp.int32, (B, B), 0) == order_ref[...]).astype(F32)
    out_ref[...] = mm(pick, tn(r_ref[...], y))


def call(kernel, out_widths, args, scratch=(), in_specs=None, interpret=False):
    shapes = [jax.ShapeDtypeStruct((B, w * B), F32) for w in out_widths]
    vmem = pl.BlockSpec(memory_space=pltpu.VMEM)
    one = len(shapes) == 1
    return pl.pallas_call(
        kernel,
        out_shape=shapes[0] if one else shapes,
        in_specs=[vmem] * len(args) if in_specs is None else in_specs,
        out_specs=vmem if one else [vmem] * len(shapes),
        scratch_shapes=list(scratch),
        interpret=interpret,
    )(*args)


def swapped(block, axis, bit):
    count = lax.axis_size(axis)
    return lax.ppermute(block, axis, [(k, k ^ (1 << bit)) for k in range(count)])


def pay_width(levels, level):
    return 1 + (levels - level) + sum(levels + 1 - a for a in range(level + 1, levels))


def body(right_sides, leaf_order, leaf_inverse, basis_blocks, interpret=False):
    run = functools.partial(call, interpret=interpret)
    part = functools.partial
    levels = basis_blocks.shape[0]
    nb = levels + 1
    two = [pltpu.VMEM((2, B, B), F32)] * 2
    vmem = pl.BlockSpec(memory_space=pltpu.VMEM)
    anywhere = pl.BlockSpec(memory_space=pl.ANY)

    z0 = run(part(leaf_kernel, nb), [nb + 1], [leaf_order, leaf_inverse, basis_blocks, right_sides], two)
    z1 = swapped(z0, "inner", 0)
    z2 = swapped(z0, "inner", 1)
    z3 = swapped(z2, "inner", 0)

    active = 1 + 2 * (nb - 3)
    share = -(-active // 4)
    pairs = [(a, b) for a in range(4, levels) for b in range(a, nb)]
    slots = -(-len(pairs) // 4)
    pairs = pairs + [pairs[-1]] * (4 * slots - len(pairs))
    table = jnp.array(pairs, jnp.int32).reshape(4, slots, 2)
    place = lax.axis_index("inner")
    mine = lax.dynamic_index_in_dim(table, place & 3, 0, keepdims=False).T
    smem = pl.BlockSpec(memory_space=pltpu.SMEM)
    act, pas, own = run(
        part(quad_kernel, nb, slots),
        [4 * share, slots, nb - 2],
        [mine, z0, z1, z2, z3],
        [
            pltpu.VMEM((4 * B, (nb + 1) * B), F32),
            pltpu.VMEM((4 * B, nb * B), F32),
            pltpu.VMEM((4 * B, (nb - 1) * B), F32),
            pltpu.VMEM((2, B, (nb - 1) * B), F32),
            pltpu.VMEM((B, (nb - 2) * B), F32),
            pltpu.VMEM((B, (nb - 3) * B), F32),
            *two,
            pltpu.SemaphoreType.DMA((4,)),
        ],
        [smem] + [anywhere] * 4,
    )
    act = lax.dynamic_slice(act, (0, (place & 3) * (share * B)), (B, share * B))
    gathered = lax.all_gather(jnp.concatenate([act, pas], axis=1), "inner")
    side = (place >> 3).astype(jnp.int32).reshape(1)
    pay, y = run(
        part(ring_kernel, nb, share, slots),
        [pay_width(levels, 4), nb - 4],
        [side, gathered, own],
        [
            pltpu.VMEM((5 * B, (nb - 4) * B), F32),
            pltpu.VMEM((5 * B, (nb - 4) * B), F32),
            pltpu.VMEM((2, B, (nb - 3) * B), F32),
            pltpu.VMEM((2, B, (nb - 3) * B), F32),
            pltpu.VMEM((2, B, (nb - 3) * B), F32),
            pltpu.VMEM((B, len(pairs) * B), F32),
            *two,
            pltpu.VMEM((2, B, B), F32),
        ],
        [smem, vmem, vmem],
    )

    for level in range(4, levels - 1):
        other = swapped(pay, "outer", level - 4)
        after, x = run(
            part(merge_kernel, nb, level), [pay_width(levels, level + 1), levels - level], [pay, other], two
        )
        y = run(update_kernel, [levels - level], [pay[:, : (1 + levels - level) * B], x, y])
        pay = after
    other = swapped(pay, "outer", levels - 5)
    return run(finish_kernel, [1], [leaf_order, leaf_inverse, pay, other, y])


def solution(mesh):
    in_specs = (
        P(("outer", "inner"), None),
        P(("outer", "inner"), None),
        P(("outer", "inner"), None),
        P(None, ("outer", "inner"), None),
    )
    out_specs = P(("outer", "inner"), None)
    return jax.shard_map(body, mesh=mesh, in_specs=in_specs, out_specs=out_specs, check_vma=False)
```

time: 1420 us -> 365 us (0.26)
  the two profiles are of different devices: /device:TPU:16 before, /device:TPU:2 now
where the time goes in v1:
time: 365 us; the launch traced here: 358 us
  waiting for transfers between devices  210 us (58%)
  Pallas kernels  91 us (25%)
  starting transfers between devices  28.5 us (8%)
  between operations  13.9 us (4%)
  local copies, waits for them, and re-layouts  13.2 us (4%)
    all_gather x1, waiting for transfers between devices, body(): gathered = lax.all_gather(jnp.concatenate([act, pas], axis=1), 'inner')  121 us
    pallas_call x12, Pallas kernels, call(): pl.pallas_call(kernel, out_shape=shapes[0] if one else shapes, in_specs=[...  91 us
    ppermute x8, waiting for transfers between devices, swapped(): return lax.ppermute(block, axis, [(k, k ^ 1 << bit) for k in range(count)])  89.1 us
    ppermute x8, starting transfers between devices, swapped(): return lax.ppermute(block, axis, [(k, k ^ 1 << bit) for k in range(count)])  28.5 us
  transfers between devices with their start and end apart: 9, of which 7 were waited for; matrix products, arithmetic and copies ran while one was open for 2% of the time, Pallas kernels for 3%

profile of v1, /device:TPU:2, one launch (start us, length us, event | category | flops | bytes accessed | tf_op | source)
XLA Modules:
  0.0 358.2 jit_solution(2816401353096805317)
XLA Ops:
  6.5 4.7 %shard_map.55.zs0 = f32[128,1408]{1,0:T(8,128)} custom-call(s32[1,128]{1,0:T(1,128)} %order_ref.3, f32[128,128]{1,0:T(8,128)} %r_ref.3, f32[9,128,128]{2,1,0:T(8,128)} %u_ref.1, f32[128,128]{1,0:T(8,128)} %rhs_ref.1), custom_call_target="tpu_custom_call" | custom-call | tf_op jit(solution)/shard_map/pallas_call | solution.py:279
  11.2 5.2 %collective-permute-start.1 = (f32[128,1408]{1,0:T(8,128)}, f32[128,1408]{1,0:T(8,128)S(1)}, u32[]{:S(2)}, u32[]{:S(2)}) collective-permute-start(f32[128,1408]{1,0:T(8,128)} %shard_map.55.zs0), channel_id=1, source_target_pairs={{0,2},{1,3},{2,0},{3,1},{4,6},{5,7},{6,4},{7,5},{8,10},{9,11},{10,... | collective-permute-start | bytes 2162696 | tf_op jit(solution)/shard_map/ppermute | solution.py:291
  16.4 3.8 %collective-permute-start = (f32[128,1408]{1,0:T(8,128)}, f32[128,1408]{1,0:T(8,128)S(1)}, u32[]{:S(2)}, u32[]{:S(2)}) collective-permute-start(f32[128,1408]{1,0:T(8,128)} %shard_map.55.zs0), channel_id=1, source_target_pairs={{0,1},{1,0},{2,3},{3,2},{4,5},{5,4},{6,7},{7,6},{8,9},{9,8},{10,11... | collective-permute-start | bytes 2162696 | tf_op jit(solution)/shard_map/ppermute | solution.py:291
  20.2 28.0 %collective-permute-done.1.zs2 = f32[128,1408]{1,0:T(8,128)S(1)} collective-permute-done((f32[128,1408]{1,0:T(8,128)}, f32[128,1408]{1,0:T(8,128)S(1)}, u32[]{:S(2)}, u32[]{:S(2)}) %collective-permute-start.1) | collective-permute-done | bytes 720928 | tf_op jit(solution)/shard_map/ppermute | solution.py:291
  48.3 2.7 collective-permute-start.2
  50.9 1.2 dynamic-slice_bitcast_fusion.table_ref
  52.2 15.2 %collective-permute-done.2.zs3 = f32[128,1408]{1,0:T(8,128)S(1)} collective-permute-done((f32[128,1408]{1,0:T(8,128)S(1)}, f32[128,1408]{1,0:T(8,128)S(1)}, u32[]{:S(2)}, u32[]{:S(2)}) %collective-permute-start.2) | collective-permute-done | bytes 720928 | tf_op jit(solution)/shard_map/ppermute | solution.py:291
  68.3 30.2 %shard_map.56 = (f32[128,2048]{1,0:T(8,128)}, f32[128,640]{1,0:T(8,128)}, f32[128,1024]{1,0:T(8,128)}) custom-call(s32[2,5]{1,0:T(2,128)} %dynamic-slice_bitcast_fusion.table_ref, f32[128,1408]{1,0:T(8,128)} %shard_map.55.zs0, f32[128,1408]{1,0:T(8,128)} %copy-done.4, f32[128,1408]{1,0:T(8,128)} %copy-done.3, f32[128,1408]{1,0:T(8,128)} %copy-done.5), custom_call_target="tpu_custom_call" | custom-call | tf_op jit(solution)/shard_map/pallas_call | solution.py:279
  99.5 1.8 pad_maximum_fusion
  101.3 120.7 %all-gather.3.cloned.1.call-done = f32[2048,1152]{1,0:T(8,128)} async-done(((f32[128,1152]{1,0:T(8,128)}), f32[2048,1152]{1,0:T(8,128)}) %all-gather.3.cloned.1.call-update) | async-done | bytes 9437200 | tf_op jit(solution)/shard_map/all_gather | solution.py:338
  222.0 19.1 %shard_map.57 = (f32[128,2560]{1,0:T(8,128)}, f32[128,768]{1,0:T(8,128)}) custom-call(s32[1]{0:T(128)} %bitcast.side_ref, f32[16,128,1152]{2,1,0:T(8,128)} %bitcast.6, f32[128,1024]{1,0:T(8,128)} %get-tuple-element.20.own_ref), custom_call_target="tpu_custom_call" | custom-call | tf_op jit(solution)/shard_map/pallas_call | solution.py:279
  241.0 1.9 collective-permute-start.3
  243.0 3.2 collective-permute-done.3.other_ref
  247.2 6.8 %shard_map.58 = (f32[128,1792]{1,0:T(8,128)}, f32[128,640]{1,0:T(8,128)}) custom-call(f32[128,2560]{1,0:T(8,128)} %get-tuple-element.21.own_ref, f32[128,2560]{1,0:T(8,128)} %copy-done), custom_call_target="tpu_custom_call" | custom-call | tf_op jit(solution)/shard_map/pallas_call | solution.py:279
  254.1 2.7 collective-permute-start.4
  256.8 21.8 %collective-permute-done.4.other_ref = f32[128,1792]{1,0:T(8,128)S(1)} collective-permute-done((f32[128,1792]{1,0:T(8,128)}, f32[128,1792]{1,0:T(8,128)S(1)}, u32[]{:S(2)}, u32[]{:S(2)}) %collective-permute-start.4) | collective-permute-done | bytes 917536 | tf_op jit(solution)/shard_map/ppermute | solution.py:291
  279.5 6.0 %shard_map.59 = (f32[128,1152]{1,0:T(8,128)}, f32[128,512]{1,0:T(8,128)}) custom-call(f32[128,1792]{1,0:T(8,128)} %get-tuple-element.22.own_ref, f32[128,1792]{1,0:T(8,128)} %copy-done.1), custom_call_target="tpu_custom_call" | custom-call | tf_op jit(solution)/shard_map/pallas_call | solution.py:279
  285.5 4.0 %collective-permute-start.5 = (f32[128,1152]{1,0:T(8,128)}, f32[128,1152]{1,0:T(8,128)S(1)}, u32[]{:S(2)}, u32[]{:S(2)}) collective-permute-start(f32[128,1152]{1,0:T(8,128)} %get-tuple-element.23.own_ref), channel_id=1, source_target_pairs={{0,64},{16,80},{32,96},{48,112},{64,0},{80,16},{96,32},{112,48},{1... | collective-permute-start | bytes 1769480 | tf_op jit(solution)/shard_map/ppermute | solution.py:291
  289.5 14.1 %collective-permute-done.5.other_ref = f32[128,1152]{1,0:T(8,128)S(1)} collective-permute-done((f32[128,1152]{1,0:T(8,128)}, f32[128,1152]{1,0:T(8,128)S(1)}, u32[]{:S(2)}, u32[]{:S(2)}) %collective-permute-start.5) | collective-permute-done | bytes 589856 | tf_op jit(solution)/shard_map/ppermute | solution.py:291
  304.5 5.5 %shard_map.60 = (f32[128,640]{1,0:T(8,128)}, f32[128,384]{1,0:T(8,128)}) custom-call(f32[128,1152]{1,0:T(8,128)} %get-tuple-element.23.own_ref, f32[128,1152]{1,0:T(8,128)} %copy-done.6), custom_call_target="tpu_custom_call" | custom-call | tf_op jit(solution)/shard_map/pallas_call | solution.py:279
  309.9 3.4 collective-permute-start.6
  313.3 6.7 %collective-permute-done.6.other_ref = f32[128,640]{1,0:T(8,128)S(1)} collective-permute-done((f32[128,640]{1,0:T(8,128)}, f32[128,640]{1,0:T(8,128)S(1)}, u32[]{:S(2)}, u32[]{:S(2)}) %collective-permute-start.6) | collective-permute-done | bytes 327712 | tf_op jit(solution)/shard_map/ppermute | solution.py:291
  320.8 4.8 %shard_map.61 = (f32[128,256]{1,0:T(8,128)}, f32[128,256]{1,0:T(8,128)}) custom-call(f32[128,640]{1,0:T(8,128)} %get-tuple-element.24.own_ref, f32[128,640]{1,0:T(8,128)} %copy-done.7), custom_call_target="tpu_custom_call" | custom-call | tf_op jit(solution)/shard_map/pallas_call | solution.py:279
  325.6 4.9 %collective-permute-start.7 = (f32[128,256]{1,0:T(8,128)}, f32[128,256]{1,0:T(8,128)S(1)}, u32[]{:S(2)}, u32[]{:S(2)}) collective-permute-start(f32[128,256]{1,0:T(8,128)} %get-tuple-element.25.own_ref), channel_id=1, source_target_pairs={{0,256},{16,272},{32,288},{48,304},{64,320},{80,336},{96,352},{112... | collective-permute-start | bytes 393224 | tf_op jit(solution)/shard_map/ppermute | solution.py:291
  330.5 1.8 slice.15.pay_ref
  332.3 1.7 slice.14.pay_ref
  334.0 2.8 shard_map.62.y_ref
  336.8 1.7 slice.13.pay_ref
  338.5 2.6 shard_map.63.y_ref
  341.7 2.5 shard_map.64.y_ref
  344.2 2.4 shard_map.65.y_ref
  347.2 3.7 %shard_map.66 = f32[128,128]{1,0:T(8,128)} custom-call(s32[1,128]{1,0:T(1,128)} %order_ref.3, f32[128,128]{1,0:T(8,128)} %r_ref.3, f32[128,256]{1,0:T(8,128)} %get-tuple-element.25.own_ref, f32[128,256]{1,0:T(8,128)} %copy-done.8, f32[128,256]{1,0:T(8,128)} %shard_map.65.y_ref), custom_call_target="tpu_custom_call" | custom-call | tf_op jit(solution)/shard_map/pallas_call | solution.py:279
  (24 shorter events, 6.8 us)
Async XLA Ops:
  6.5 215.5 %all-gather.3.cloned.1.call-start = ((), (), s32[]{:S(2)}) async-start(), calls=%async_computation | async-start | bytes 10027008 | tf_op jit(solution)/shard_map/all_gather | solution.py:338
  11.2 37.1 %collective-permute-start.1 = (f32[128,1408]{1,0:T(8,128)}, f32[128,1408]{1,0:T(8,128)S(1)}, u32[]{:S(2)}, u32[]{:S(2)}) collective-permute-start(f32[128,1408]{1,0:T(8,128)} %shard_map.55.zs0), channel_id=1, source_target_pairs={{0,2},{1,3},{2,0},{3,1},{4,6},{5,7},{6,4},{7,5},{8,10},{9,11},{10,... | collective-permute-start | bytes 2162696 | tf_op jit(solution)/shard_map/ppermute | solution.py:291
  16.4 35.8 %collective-permute-start = (f32[128,1408]{1,0:T(8,128)}, f32[128,1408]{1,0:T(8,128)S(1)}, u32[]{:S(2)}, u32[]{:S(2)}) collective-permute-start(f32[128,1408]{1,0:T(8,128)} %shard_map.55.zs0), channel_id=1, source_target_pairs={{0,1},{1,0},{2,3},{3,2},{4,5},{5,4},{6,7},{7,6},{8,9},{9,8},{10,11... | collective-permute-start | bytes 2162696 | tf_op jit(solution)/shard_map/ppermute | solution.py:291
  48.3 19.1 %copy-start.3 = (f32[128,1408]{1,0:T(8,128)}, f32[128,1408]{1,0:T(8,128)S(1)}, u32[]{:S(2)}) copy-start(f32[128,1408]{1,0:T(8,128)S(1)} %collective-permute-done.1.zs2) | copy-start | bytes 2162692
  48.3 19.1 %collective-permute-start.2 = (f32[128,1408]{1,0:T(8,128)S(1)}, f32[128,1408]{1,0:T(8,128)S(1)}, u32[]{:S(2)}, u32[]{:S(2)}) collective-permute-start(f32[128,1408]{1,0:T(8,128)S(1)} %collective-permute-done.1.zs2), channel_id=1, source_target_pairs={{0,1},{1,0},{2,3},{3,2},{4,5},{5,4},{6,7},{7,6},{8,9},{9,8},{10,11... | collective-permute-start | bytes 2162696 | tf_op jit(solution)/shard_map/ppermute | solution.py:291
  52.2 15.2 %copy-start.4 = (f32[128,1408]{1,0:T(8,128)}, f32[128,1408]{1,0:T(8,128)S(1)}, u32[]{:S(2)}) copy-start(f32[128,1408]{1,0:T(8,128)S(1)} %collective-permute-done.zs1) | copy-start | bytes 2162692
  67.4 0.9 copy-start.5
  241.0 5.1 %collective-permute-start.3 = (f32[128,2560]{1,0:T(8,128)}, f32[128,2560]{1,0:T(8,128)S(1)}, u32[]{:S(2)}, u32[]{:S(2)}) collective-permute-start(f32[128,2560]{1,0:T(8,128)} %get-tuple-element.21.own_ref), channel_id=1, source_target_pairs={{0,16},{16,0},{32,48},{48,32},{64,80},{80,64},{96,112},{112,96},{1... | collective-permute-start | bytes 3932168 | tf_op jit(solution)/shard_map/ppermute | solution.py:291
  246.2 1.1 copy-start
  254.1 24.5 %collective-permute-start.4 = (f32[128,1792]{1,0:T(8,128)}, f32[128,1792]{1,0:T(8,128)S(1)}, u32[]{:S(2)}, u32[]{:S(2)}) collective-permute-start(f32[128,1792]{1,0:T(8,128)} %get-tuple-element.22.own_ref), channel_id=1, source_target_pairs={{0,32},{16,48},{32,0},{48,16},{64,96},{80,112},{96,64},{112,80},{1... | collective-permute-start | bytes 2752520 | tf_op jit(solution)/shard_map/ppermute | solution.py:291
  278.5 0.9 copy-start.1
  285.5 18.1 %collective-permute-start.5 = (f32[128,1152]{1,0:T(8,128)}, f32[128,1152]{1,0:T(8,128)S(1)}, u32[]{:S(2)}, u32[]{:S(2)}) collective-permute-start(f32[128,1152]{1,0:T(8,128)} %get-tuple-element.23.own_ref), channel_id=1, source_target_pairs={{0,64},{16,80},{32,96},{48,112},{64,0},{80,16},{96,32},{112,48},{1... | collective-permute-start | bytes 1769480 | tf_op jit(solution)/shard_map/ppermute | solution.py:291
  303.6 0.8 copy-start.6
  309.9 10.1 %collective-permute-start.6 = (f32[128,640]{1,0:T(8,128)}, f32[128,640]{1,0:T(8,128)S(1)}, u32[]{:S(2)}, u32[]{:S(2)}) collective-permute-start(f32[128,640]{1,0:T(8,128)} %get-tuple-element.24.own_ref), channel_id=1, source_target_pairs={{0,128},{16,144},{32,160},{48,176},{64,192},{80,208},{96,224},{112... | collective-permute-start | bytes 983048 | tf_op jit(solution)/shard_map/ppermute | solution.py:291
  320.1 0.7 copy-start.7
  325.6 21.0 %collective-permute-start.7 = (f32[128,256]{1,0:T(8,128)}, f32[128,256]{1,0:T(8,128)S(1)}, u32[]{:S(2)}, u32[]{:S(2)}) collective-permute-start(f32[128,256]{1,0:T(8,128)} %get-tuple-element.25.own_ref), channel_id=1, source_target_pairs={{0,256},{16,272},{32,288},{48,304},{64,320},{80,336},{96,352},{112... | collective-permute-start | bytes 393224 | tf_op jit(solution)/shard_map/ppermute | solution.py:291
  334.0 7.0 %copy-start.2 = (f32[128,640]{1,0:T(8,128)S(1)}, f32[128,640]{1,0:T(8,128)}, u32[]{:S(2)}) copy-start(f32[128,640]{1,0:T(8,128)} %get-tuple-element.24.own_ref) | copy-start | bytes 983044
  346.6 0.6 copy-start.8
Sparse Core Ops, SparseCore 0:
  101.4 120.5 all-gather.2

commit v2 on v1

v2 whole, which is shorter than its diff:
```python
import functools

import jax
import jax.numpy as jnp
from jax import lax
from jax.experimental import pallas as pl
from jax.experimental.pallas import tpu as pltpu
from jax.sharding import PartitionSpec as P

B = 128
F32 = jnp.float32


HIGH = lax.Precision.HIGHEST
HALF = jnp.bfloat16


def halves(a):
    top = a.astype(HALF)
    return top, (a - top.astype(F32)).astype(HALF)


def product(a, b, dims):
    def dot(x, y):
        return lax.dot_general(x, y, (dims, ((), ())), preferred_element_type=F32)

    a_top, a_low = halves(a)
    b_top, b_low = halves(b)
    return dot(a_top, b_top) + (dot(a_top, b_low) + dot(a_low, b_top))


def mm(a, b):
    return product(a, b, ((1,), (0,)))


def tn(a, b):
    return product(a, b, ((0,), (0,)))


def exact(a, b):
    return jnp.dot(a, b, precision=HIGH, preferred_element_type=F32)


def exact_tn(a, b):
    return lax.dot_general(
        a, b, (((0,), (0,)), ((), ())), precision=HIGH, preferred_element_type=F32
    )


def eye():
    return (
        lax.broadcasted_iota(jnp.int32, (B, B), 0) == lax.broadcasted_iota(jnp.int32, (B, B), 1)
    ).astype(F32)


def sl(i, j):
    return slice(i * B, j * B)


def unit_inverse(grams, x_ref, r_ref):
    unit = eye()
    count = len(grams)
    h = jnp.ones((1, 1), F32)
    for g in grams:
        h = jnp.maximum(
            h, jnp.max(jnp.sum(jnp.abs(g), axis=0, keepdims=True), axis=1, keepdims=True)
        )
    s = 2.0 / h
    s = 2.0 * s * (s + 2.0)
    left = jnp.zeros((1, 1), jnp.int32)
    ahead = s
    for _ in range(14):
        left = left + (ahead < 4000.0).astype(jnp.int32)
        ahead = 2.0 * ahead * (ahead + 2.0)
    steps = jnp.max(left)
    inv_t = 1.0 / (1.0 + s)
    c = 1.0 + inv_t
    scale = 2.0 / (h + 2.0)
    for k, g in enumerate(grams):
        r = (h * unit - 2.0 * g) / (h + 2.0)
        x_ref[k] = (c * scale) * (unit + r)
        r_ref[k] = c * mm(r, r) - inv_t * unit

    def double(_, s):
        s = 2.0 * s * (s + 2.0)
        inv_t = 1.0 / (1.0 + s)
        c = 1.0 + inv_t
        for k in range(count):
            r = r_ref[k]
            x = x_ref[k]
            x_ref[k] = c * (x + mm(x, r))
            r_ref[k] = c * mm(r, r) - inv_t * unit
        return s

    lax.fori_loop(0, steps, double, s)
    found = []
    for k, g in enumerate(grams):
        x = x_ref[k]
        found.append(x + mm(x, unit - x - exact(g, x)))
    return found


def pair_inverse(s_first, s_second):
    unit = eye()
    r = 0.5 * (s_first + s_second - unit)
    t = 7.0
    x = (0.5 * (1.0 + 1.0 / t)) * (unit + r)
    r = (1.0 + 1.0 / t) * mm(r, r) - (1.0 / t) * unit
    for last in (False, False, True):
        t = 2.0 * t * t - 1.0
        c = 1.0 + 1.0 / t
        x = c * (x + mm(x, r))
        if not last:
            r = c * mm(r, r) - (1.0 / t) * unit
    return x


def leaf_kernel(nb, order_ref, r_ref, u_ref, rhs_ref, z_ref, x_scr, r_scr):
    pick = (lax.broadcasted_iota(jnp.int32, (B, B), 0) == order_ref[...]).astype(F32)
    r = r_ref[...]
    for b in range(nb - 1):
        z_ref[:, sl(b, b + 1)] = mm(r, u_ref[b])
    z_ref[:, sl(nb - 1, nb)] = mm(r, exact_tn(pick, rhs_ref[...]))
    z0 = z_ref[:, sl(0, 1)]
    (s,) = unit_inverse([tn(z0, z0)], x_scr, r_scr)
    z_ref[:, sl(nb, nb + 1)] = s


def pair_kernel(nb, first_ref, second_ref, y_ref):
    refs = (first_ref, second_ref)
    n = [
        exact(z[:, sl(nb, nb + 1)], tn(z[:, sl(0, 1)], z[:, sl(1, nb)]))
        for z in refs
    ]
    t = pair_inverse(first_ref[:, sl(nb, nb + 1)], second_ref[:, sl(nb, nb + 1)])
    x = mm(t, n[0] + n[1])
    for i, z in enumerate(refs):
        weights = n[i] + mm(z[:, sl(nb, nb + 1)], x)
        y_ref[sl(i, i + 1), :] = z[:, sl(1, nb)] - mm(z[:, sl(0, 1)], weights)


def quad_kernel(
    nb, place_ref, zs0, zs1, zs2, zs3, y01, y23,
    out_ref, send_ref, own_ref, z, y, act_ref, x_scr, r_scr, sem,
):
    copies = [
        pltpu.make_async_copy(y01, y.at[pl.ds(0, 2 * B), pl.ds(B, (nb - 1) * B)], sem.at[4]),
        pltpu.make_async_copy(y23, y.at[pl.ds(2 * B, 2 * B), pl.ds(B, (nb - 1) * B)], sem.at[5]),
    ] + [
        pltpu.make_async_copy(
            src.at[:, pl.ds(B, (nb - 1) * B)],
            z.at[pl.ds(i * B, B), pl.ds(B, (nb - 1) * B)],
            sem.at[i],
        )
        for i, src in enumerate((zs0, zs1, zs2, zs3))
    ]
    for copy in copies:
        copy.start()
    for copy in copies:
        copy.wait()
    rows = [slice(0, 2 * B), slice(2 * B, 4 * B)]
    m = [tn(z[rows[n], sl(1, 2)], y[rows[n], sl(1, nb)]) for n in range(2)]
    s = unit_inverse([m[n][:, :B] for n in range(2)], x_scr, r_scr)
    nn = [mm(s[n], m[n][:, B:]) for n in range(2)]
    x = mm(pair_inverse(s[0], s[1]), nn[0] + nn[1])
    last = nb - 1
    for n in range(2):
        weights = nn[n] + mm(s[n], x)
        y[rows[n], sl(2, nb)] = y[rows[n], sl(2, nb)] - mm(y[rows[n], sl(1, 2)], weights)
    m2 = tn(z[:, sl(2, 3)], y[:, sl(2, nb)])
    (s2,) = unit_inverse([m2[:, :B]], x_scr, r_scr)
    n2 = mm(s2, m2[:, B:])
    m3 = tn(z[:, sl(3, 4)], y[:, sl(3, nb)]) - tn(m2[:, sl(1, 2)], n2)
    wide = nb - 3
    act_ref[:, sl(0, 1)] = s2
    act_ref[:, sl(1, 1 + wide)] = n2
    act_ref[:, sl(1 + wide, 1 + 2 * wide)] = m3
    y2 = y[0:B, sl(2, 3)]
    own_ref[:, sl(1, nb - 2)] = y[0:B, sl(3, nb)] - mm(y2, n2)
    own_ref[:, sl(0, 1)] = mm(y2, s2)

    at = 1 + 2 * wide
    for a in range(4, last):
        act_ref[:, sl(at, at + nb - a)] = tn(z[:, sl(a, a + 1)], y[:, sl(a, nb)]) - tn(
            m2[:, sl(a - 2, a - 1)], n2[:, sl(a - 3, wide)]
        )
        at += nb - a
    rows = pl.ds(pl.multiple_of(place_ref[0] * (B // 4), B // 4), B // 4)
    head, half = cuts(nb)
    out_ref[:, sl(0, head)] = act_ref[rows, sl(0, head)]
    first = sl(head, head + half)
    second = sl(head + half, head + 2 * half)

    @pl.when(place_ref[1] == 0)
    def _():
        out_ref[:, first] = act_ref[rows, first]
        send_ref[...] = act_ref[rows, second]

    @pl.when(place_ref[1] == 1)
    def _():
        out_ref[:, first] = act_ref[rows, second]
        send_ref[...] = act_ref[rows, first]


def cuts(nb):
    rest = sum(nb - a for a in range(5, nb - 1))
    return 1 + 2 * (nb - 3) + nb - 4, rest // 2


def ring_kernel(
    nb, side_ref, all_ref, own_ref, pay_ref, out_ref,
    act_ref, pas_ref, la, lb, q, m, nn, tot, x_scr, r_scr, s_scr, sem,
):
    wide = nb - 3
    deep = nb - 4
    active = 1 + 2 * wide
    copies = [
        pltpu.make_async_copy(all_ref.at[:, pl.ds(0, active * B)], act_ref, sem.at[0]),
        pltpu.make_async_copy(
            all_ref.at[:, pl.ds(active * B, pas_ref.shape[1])], pas_ref, sem.at[1]
        ),
    ]
    for copy in copies:
        copy.start()
    copies[0].wait()

    def piece(group, k):
        return act_ref[sl(group, group + 1), sl(k, k + 1)]

    for node in range(2):
        g, h = 2 * node, 2 * node + 1
        for k in range(wide):
            q[node, :, sl(k, k + 1)] = piece(g, 1 + k) + piece(h, 1 + k)
        t = pair_inverse(piece(g, 0), piece(h, 0))
        x = mm(t, q[node])
        m[node] = x
        lb[sl(node, node + 1), :] = x[:, B:]
        la[sl(node, node + 1), :] = q[node, :, B:]
        m3 = tn(q[node, :, :B], x)
        for k in range(wide):
            nn[node, :, sl(k, k + 1)] = (
                piece(g, 1 + wide + k) + piece(h, 1 + wide + k) - m3[:, sl(k, k + 1)]
            )
    s = unit_inverse([nn[0, :, :B], nn[1, :, :B]], x_scr, r_scr)
    for node in range(2):
        s_scr[node] = s[node]
        la[sl(2 + node, 3 + node), :] = nn[node, :, B:]
        lb[sl(2 + node, 3 + node), :] = mm(s[node], nn[node, :, B:])
    q3 = lb[sl(2, 3), :] + lb[sl(3, 4), :]
    x3 = mm(pair_inverse(s[0], s[1]), q3)
    la[sl(4, 5), :] = q3
    lb[sl(4, 5), :] = x3
    copies[1].wait()
    half = cuts(nb)[1]
    tot[...] = jnp.zeros_like(tot)

    def over(part):
        return (
            pas_ref[sl(0, 1), part]
            + pas_ref[sl(1, 2), part]
            + pas_ref[sl(2, 3), part]
            + pas_ref[sl(3, 4), part]
        )

    tot[:, sl(0, deep)] = over(sl(0, deep))
    lanes = pl.ds(pl.multiple_of((deep + half * side_ref[1]) * B, B), half * B)
    tot[:, lanes] = over(sl(deep, deep + half))
    at = 0
    for k in range(deep - 1):
        part = sl(at, at + deep - k)
        tot[:, part] = tot[:, part] - tn(la[:, sl(k, k + 1)], lb[:, sl(k, deep)])
        at += deep - k

    def panel(a):
        at = sum(nb - k for k in range(4, a))
        return tot[:, sl(at, at + nb - a)]

    own_side(nb, 4, panel, pay_ref, x_scr, r_scr)
    side = side_ref[0]
    y = own_ref[:, sl(1, nb - 2)] - mm(own_ref[:, :B], m[side])
    n3 = lb[pl.ds(pl.multiple_of((2 + side) * B, B), B), :]
    weights = n3 + mm(s_scr[side], x3)
    out_ref[...] = y[:, B:] - mm(y[:, :B], weights)


def own_side(nb, level, m, pay_ref, x_scr, r_scr):
    row = m(level)
    wide = nb - 1 - level
    (s,) = unit_inverse([row[:, :B]], x_scr, r_scr)
    n = mm(s, row[:, B:])
    pay_ref[:, sl(0, 1)] = s
    pay_ref[:, sl(1, 1 + wide)] = n
    at = 1 + wide
    for a in range(level + 1, nb - 1):
        k = a - level
        pay_ref[:, sl(at, at + nb - a)] = m(a) - tn(
            row[:, sl(k, k + 1)], n[:, sl(k - 1, wide)]
        )
        at += nb - a


def merge_kernel(nb, level, split, core_ref, own_ref, *refs):
    refs = list(refs)
    if split:
        kept, fetched = refs[:2]
        full, core = refs[-1], core_ref[0]
        full[core] = kept[...]
        full[1 - core] = fetched[...]
        other = functools.partial(two_part, full, full.shape[2] // B)
        refs = refs[3:-1]
    else:
        whole = refs[0]
        other = lambda i, j: whole[:, sl(i, j)]
        refs = refs[2:]
    after = refs[2:-2]
    pay_ref, x_ref = refs[:2]
    x_scr, r_scr = refs[-2:]
    wide = nb - 1 - level
    q = own_ref[:, sl(1, 1 + wide)] + other(1, 1 + wide)
    x = mm(pair_inverse(own_ref[:, :B], other(0, 1)), q)
    x_ref[...] = x

    def panel(a):
        k = a - level - 1
        at = 1 + wide + sum(nb - j for j in range(level + 1, a))
        return (
            own_ref[:, sl(at, at + nb - a)]
            + other(at, at + nb - a)
            - tn(q[:, sl(k, k + 1)], x[:, sl(k, wide)])
        )

    own_side(nb, level + 1, panel, pay_ref, x_scr, r_scr)
    if after:
        put_half(core_ref, pay_ref, after[0])


def two_part(full, half, i, j):
    if j <= half:
        return full[0, :, sl(i, j)]
    if i >= half:
        return full[1, :, sl(i - half, j - half)]
    return jnp.concatenate([full[0, :, sl(i, half)], full[1, :, sl(0, j - half)]], axis=1)


def put_half(core_ref, pay_ref, half_ref):
    count, half = pay_ref.shape[1] // B, half_ref.shape[1] // B

    @pl.when(core_ref[0] == 0)
    def _():
        half_ref[...] = pay_ref[:, sl(0, half)]

    @pl.when(core_ref[0] == 1)
    def _():
        half_ref[:, sl(0, count - half)] = pay_ref[:, sl(half, count)]
        if 2 * half > count:
            half_ref[:, sl(count - half, half)] = pay_ref[:, sl(count - 1, count)]


def update_kernel(pay_ref, x_ref, y_ref, out_ref):
    wide = x_ref.shape[1]
    weights = pay_ref[:, B : B + wide] + mm(pay_ref[:, :B], x_ref[...])
    out_ref[...] = y_ref[:, B:] - mm(y_ref[:, :B], weights)


def finish_kernel(order_ref, r_ref, own_ref, other_ref, y_ref, out_ref):
    s = own_ref[:, :B]
    n = own_ref[:, B:]
    x = mm(pair_inverse(s, other_ref[:, :B]), n + other_ref[:, B:])
    y = y_ref[:, B:] - mm(y_ref[:, :B], n + mm(s, x))
    pick = (lax.broadcasted_iota(jnp.int32, (B, B), 0) == order_ref[...]).astype(F32)
    out_ref[...] = exact(pick, tn(r_ref[...], y))


def call(kernel, shapes, args, scratch=(), in_specs=None, grid=(), interpret=False):
    shapes = [
        jax.ShapeDtypeStruct((B, w * B) if isinstance(w, int) else w, F32) for w in shapes
    ]
    vmem = pl.BlockSpec(memory_space=pltpu.VMEM)
    one = len(shapes) == 1
    return pl.pallas_call(
        kernel,
        out_shape=shapes[0] if one else shapes,
        grid=grid,
        in_specs=[vmem] * len(args) if in_specs is None else in_specs,
        out_specs=vmem if one else [vmem] * len(shapes),
        scratch_shapes=list(scratch),
        interpret=interpret,
    )(*args)


def swapped(block, axis, bit):
    count = lax.axis_size(axis)
    return lax.ppermute(block, axis, [(k, k ^ (1 << bit)) for k in range(count)])


def pay_width(levels, level):
    return 1 + (levels - level) + sum(levels + 1 - a for a in range(level + 1, levels))


def ring_call(run, levels, side, gathered, own):
    nb = levels + 1
    head, half = cuts(nb)
    active = 2 * levels - 3
    two = [pltpu.VMEM((2, B, B), F32)] * 2
    smem = pl.BlockSpec(memory_space=pltpu.SMEM)
    vmem = pl.BlockSpec(memory_space=pltpu.VMEM)
    anywhere = pl.BlockSpec(memory_space=pl.ANY)
    return run(
        functools.partial(ring_kernel, nb),
        [pay_width(levels, 4), nb - 4],
        [side, gathered, own],
        [
            pltpu.VMEM((4 * B, active * B), F32),
            pltpu.VMEM((4 * B, (head + half - active) * B), F32),
            pltpu.VMEM((5 * B, (nb - 4) * B), F32),
            pltpu.VMEM((5 * B, (nb - 4) * B), F32),
            pltpu.VMEM((2, B, (nb - 3) * B), F32),
            pltpu.VMEM((2, B, (nb - 3) * B), F32),
            pltpu.VMEM((2, B, (nb - 3) * B), F32),
            pltpu.VMEM((B, (nb - 4 + 2 * half) * B), F32),
            *two,
            pltpu.VMEM((2, B, B), F32),
            pltpu.SemaphoreType.DMA((2,)),
        ],
        [smem, anywhere, vmem],
    )


def quad_call(run, levels, place, zs, ys):
    nb = levels + 1
    head, half = cuts(nb)
    two = [pltpu.VMEM((2, B, B), F32)] * 2
    smem = pl.BlockSpec(memory_space=pltpu.SMEM)
    anywhere = pl.BlockSpec(memory_space=pl.ANY)
    return run(
        functools.partial(quad_kernel, nb),
        [(B // 4, (head + half) * B), (B // 4, half * B), nb - 2],
        [place, *zs, *ys],
        [
            pltpu.VMEM((4 * B, nb * B), F32),
            pltpu.VMEM((4 * B, nb * B), F32),
            pltpu.VMEM((B, (head + 2 * half) * B), F32),
            *two,
            pltpu.SemaphoreType.DMA((6,)),
        ],
        [smem] + [anywhere] * 6,
    )


def merge_call(run, levels, level, core, pay, others, behind, half):
    nb = levels + 1
    split = len(others) == 2
    two = [pltpu.VMEM((2, B, B), F32)] * 2
    smem = pl.BlockSpec(memory_space=pltpu.SMEM)
    vmem = pl.BlockSpec(memory_space=pltpu.VMEM)
    anywhere = pl.BlockSpec(memory_space=pl.ANY)
    return run(
        functools.partial(merge_kernel, nb, level, split),
        [pay_width(levels, level + 1), levels - level] + ([half] if half else []),
        [core, pay, *others, behind],
        two + ([pltpu.VMEM((2, *others[0].shape), F32)] if split else []),
        [smem] + [vmem] * (1 + len(others)) + [anywhere],
    )


def body(right_sides, leaf_order, leaf_inverse, basis_blocks, interpret=False):
    run = functools.partial(call, interpret=interpret)
    part = functools.partial
    levels = basis_blocks.shape[0]
    nb = levels + 1
    two = [pltpu.VMEM((2, B, B), F32)] * 2
    vmem = pl.BlockSpec(memory_space=pltpu.VMEM)

    z0 = run(part(leaf_kernel, nb), [nb + 1], [leaf_order, leaf_inverse, basis_blocks, right_sides], two)
    z1 = swapped(z0, "inner", 0)
    z2 = swapped(z0, "inner", 1)
    z3 = swapped(z2, "inner", 0)
    ys = [
        run(part(pair_kernel, nb), [(2 * B, (nb - 1) * B)], pair) for pair in ((z0, z1), (z2, z3))
    ]
    place = lax.axis_index("inner").astype(jnp.int32)
    core = lax.axis_index("outer").astype(jnp.int32) & 1
    mine, send, own = quad_call(run, levels, jnp.stack([place & 3, core]), [z0, z1, z2, z3], ys)
    cut = cuts(nb)[0] * B
    mine = jnp.concatenate([mine[:, :cut], mine[:, cut:] + swapped(send, "outer", 0)], axis=1)
    gathered = lax.all_gather(mine, "inner", tiled=True)
    pay, y = ring_call(run, levels, jnp.stack([place >> 3, core]), gathered, own)
    core = core.reshape(1)
    half = None
    for level in range(4, levels):
        if half is None:
            others = [swapped(pay, "outer", level - 4)]
        else:
            kept = swapped(half, "outer", level - 4)
            others = [kept, swapped(kept, "outer", 0)]
        if level == levels - 1:
            break
        width = pay_width(levels, level + 1)
        cut = -(-width // 2) if width > 6 else 0
        found = merge_call(run, levels, level, core, pay, others, y, cut)
        wide = levels - level
        head = pl.BlockSpec((B, (1 + wide) * B), lambda i: (0, 0))
        y = run(update_kernel, [wide], [pay, found[1], y], (), [head, vmem, vmem], (1,))
        pay = found[0]
        half = found[2] if cut else None
    return run(finish_kernel, [1], [leaf_order, leaf_inverse, pay, others[0], y])


def solution(mesh):
    in_specs = (
        P(("outer", "inner"), None),
        P(("outer", "inner"), None),
        P(("outer", "inner"), None),
        P(None, ("outer", "inner"), None),
    )
    out_specs = P(("outer", "inner"), None)
    return jax.shard_map(body, mesh=mesh, in_specs=in_specs, out_specs=out_specs, check_vma=False)
```

time: 365 us -> 306 us (0.84); the launches traced: 358 us -> 305 us
  waiting for transfers between devices: 210 us -> 169 us
  Pallas kernels: 91 us -> 78.5 us
  local copies, waits for them, and re-layouts: 13.2 us -> 6.69 us
  starting transfers between devices: 28.5 us -> 34.2 us
    all_gather x1, waiting for transfers between devices: 121 us -> 99 us  [body(): gathered = lax.all_gather(mine, 'inner', tiled=True)]
    ppermute x8 -> x11, waiting for transfers between devices: 89.1 us -> 70.3 us  [swapped(): return lax.ppermute(block, axis, [(k, k ^ 1 << bit) for k in range(count)])]
    pallas_call x12 -> x14, Pallas kernels: 91 us -> 78.5 us  [call(): pl.pallas_call(kernel, out_shape=shapes[0] if one else shapes, grid=grid,...]
    ppermute x8 -> x11, starting transfers between devices: 28.5 us -> 34.2 us  [swapped(): return lax.ppermute(block, axis, [(k, k ^ 1 << bit) for k in range(count)])]
    slice x4 -> x1, local copies, waits for them, and re-layouts: 5.85 us -> 1 us  [body(): mine[:, :cut]]
  transfers between devices with their start and end apart: 9 -> 12, of which waited for: 7 -> 9; matrix products, arithmetic and copies ran while one was open for 2% -> 1% of each run, Pallas kernels for 3% -> 5%
where the time goes in v2:
time: 306 us; the launch traced here: 305 us
  waiting for transfers between devices  169 us (55%)
  Pallas kernels  78.5 us (26%)
  starting transfers between devices  34.2 us (11%)
  between operations  13.5 us (4%)
  local copies, waits for them, and re-layouts  6.69 us (2%)
    all_gather x1, waiting for transfers between devices, body(): gathered = lax.all_gather(mine, 'inner', tiled=True)  99 us
    pallas_call x14, Pallas kernels, call(): pl.pallas_call(kernel, out_shape=shapes[0] if one else shapes, grid=grid,...  78.5 us
    ppermute x11, waiting for transfers between devices, swapped(): return lax.ppermute(block, axis, [(k, k ^ 1 << bit) for k in range(count)])  70.3 us
    ppermute x11, starting transfers between devices, swapped(): return lax.ppermute(block, axis, [(k, k ^ 1 << bit) for k in range(count)])  34.2 us
  transfers between devices with their start and end apart: 12, of which 9 were waited for; matrix products, arithmetic and copies ran while one was open for 1% of the time, Pallas kernels for 5%

profile of v2, /device:TPU:2, one launch (start us, length us, event | category | flops | bytes accessed | tf_op | source)
XLA Modules:
  0.0 305.1 jit_solution(3869396520993541421)
XLA Ops:
  6.5 4.2 %shard_map.46.first_ref.zs0 = f32[128,1408]{1,0:T(8,128)} custom-call(s32[1,128]{1,0:T(1,128)} %order_ref.3, f32[128,128]{1,0:T(8,128)} %r_ref.3, f32[9,128,128]{2,1,0:T(8,128)} %u_ref.1, f32[128,128]{1,0:T(8,128)} %rhs_ref.1), custom_call_target="tpu_custom_call" | custom-call | tf_op jit(solution)/shard_map/pallas_call | solution.py:380
  10.7 5.2 %collective-permute-start.1 = (f32[128,1408]{1,0:T(8,128)}, f32[128,1408]{1,0:T(8,128)S(1)}, u32[]{:S(2)}, u32[]{:S(2)}) collective-permute-start(f32[128,1408]{1,0:T(8,128)} %shard_map.46.first_ref.zs0), channel_id=1, source_target_pairs={{0,2},{1,3},{2,0},{3,1},{4,6},{5,7},{6,4},{7,5},{8,10},{9,11},{10,... | collective-permute-start | bytes 2162696 | tf_op jit(solution)/shard_map/ppermute | solution.py:393
  15.9 3.8 %collective-permute-start = (f32[128,1408]{1,0:T(8,128)}, f32[128,1408]{1,0:T(8,128)S(1)}, u32[]{:S(2)}, u32[]{:S(2)}) collective-permute-start(f32[128,1408]{1,0:T(8,128)} %shard_map.46.first_ref.zs0), channel_id=1, source_target_pairs={{0,1},{1,0},{2,3},{3,2},{4,5},{5,4},{6,7},{7,6},{8,9},{9,8},{10,11... | collective-permute-start | bytes 2162696 | tf_op jit(solution)/shard_map/ppermute | solution.py:393
  19.7 28.1 %collective-permute-done.1.first_ref.zs2 = f32[128,1408]{1,0:T(8,128)S(1)} collective-permute-done((f32[128,1408]{1,0:T(8,128)}, f32[128,1408]{1,0:T(8,128)S(1)}, u32[]{:S(2)}, u32[]{:S(2)}) %collective-permute-start.1) | collective-permute-done | bytes 720928 | tf_op jit(solution)/shard_map/ppermute | solution.py:393
  47.8 2.7 collective-permute-start.2
  51.9 6.5 %shard_map.47.y01 = f32[256,1152]{1,0:T(8,128)} custom-call(f32[128,1408]{1,0:T(8,128)} %shard_map.46.first_ref.zs0, f32[128,1408]{1,0:T(8,128)} %copy-done.1), custom_call_target="tpu_custom_call" | custom-call | tf_op jit(solution)/shard_map/pallas_call | solution.py:380
  58.4 8.5 %collective-permute-done.2.second_ref.zs3 = f32[128,1408]{1,0:T(8,128)S(1)} collective-permute-done((f32[128,1408]{1,0:T(8,128)S(1)}, f32[128,1408]{1,0:T(8,128)S(1)}, u32[]{:S(2)}, u32[]{:S(2)}) %collective-permute-start.2) | collective-permute-done | bytes 720928 | tf_op jit(solution)/shard_map/ppermute | solution.py:393
  67.8 6.5 %shard_map.48.y23 = f32[256,1152]{1,0:T(8,128)} custom-call(f32[128,1408]{1,0:T(8,128)} %copy-done, f32[128,1408]{1,0:T(8,128)} %copy-done.2), custom_call_target="tpu_custom_call" | custom-call | tf_op jit(solution)/shard_map/pallas_call | solution.py:380
  74.3 14.2 %shard_map.49 = (f32[32,3584]{1,0:T(8,128)}, f32[32,896]{1,0:T(8,128)}, f32[128,1024]{1,0:T(8,128)}) custom-call(s32[2]{0:T(128)} %pad_add_fusion.1.place_ref, f32[128,1408]{1,0:T(8,128)} %shard_map.46.first_ref.zs0, f32[128,1408]{1,0:T(8,128)} %copy-done.1, f32[128,1408]{1,0:T(8,128)} %copy-done, f32[128,1408]{1,0:T(8,128)} %copy-done.2, ...), custom_call_target="tpu_custom_call" | custom-call | tf_op jit(solution)/shard_map/pallas_call | solution.py:380
  88.5 1.9 collective-permute-start.3
  94.2 99.0 %all-gather.2.cloned.1.call-done.all_ref = f32[512,3584]{1,0:T(8,128)} async-done(((f32[32,3584]{1,0:T(8,128)}), f32[512,3584]{1,0:T(8,128)}) %all-gather.2.cloned.1.call-update) | async-done | bytes 7340048 | tf_op jit(solution)/shard_map/all_gather | solution.py:486
  193.2 14.0 %shard_map.50 = (f32[128,2560]{1,0:T(8,128)}, f32[128,768]{1,0:T(8,128)}) custom-call(s32[2]{0:T(128)} %pad_add_fusion.side_ref, f32[512,3584]{1,0:T(8,128)} %all-gather.2.cloned.1.call-done.all_ref, f32[128,1024]{1,0:T(8,128)} %get-tuple-element.22.own_ref), custom_call_target="tpu_custom_call" | custom-call | tf_op jit(solution)/shard_map/pallas_call | solution.py:380
  207.2 1.9 collective-permute-start.4
  209.2 3.2 %collective-permute-done.4.refs_0_ = f32[128,2560]{1,0:T(8,128)S(1)} collective-permute-done((f32[128,2560]{1,0:T(8,128)}, f32[128,2560]{1,0:T(8,128)S(1)}, u32[]{:S(2)}, u32[]{:S(2)}) %collective-permute-start.4) | collective-permute-done | bytes 1310752 | tf_op jit(solution)/shard_map/ppermute | solution.py:393
  213.4 6.1 %shard_map.51 = (f32[128,1792]{1,0:T(8,128)}, f32[128,640]{1,0:T(8,128)}, f32[128,896]{1,0:T(8,128)}) custom-call(s32[1]{0:T(128)} %bitcast.core_ref, f32[128,2560]{1,0:T(8,128)} %get-tuple-element.23.own_ref.pay_ref, f32[128,2560]{1,0:T(8,128)} %copy-done.3, f32[128,768]{1,0:T(8,128)} %get-tuple-element.24.refs_1_.y_ref), custom_call_target="tpu_custom_call" | custom-call | tf_op jit(solution)/shard_map/pallas_call | solution.py:380
  219.6 2.4 collective-permute-start.5
  222.0 12.2 %collective-permute-done.5.refs_0_ = f32[128,896]{1,0:T(8,128)S(1)} collective-permute-done((f32[128,896]{1,0:T(8,128)}, f32[128,896]{1,0:T(8,128)S(1)}, u32[]{:S(2)}, u32[]{:S(2)}) %collective-permute-start.5) | collective-permute-done | bytes 458784 | tf_op jit(solution)/shard_map/ppermute | solution.py:393
  234.2 2.1 collective-permute-start.6
  236.4 2.6 shard_map.52.refs_2_.y_ref
  239.8 5.3 %shard_map.53 = (f32[128,1152]{1,0:T(8,128)}, f32[128,512]{1,0:T(8,128)}, f32[128,640]{1,0:T(8,128)}) custom-call(s32[1]{0:T(128)} %bitcast.core_ref, f32[128,1792]{1,0:T(8,128)} %get-tuple-element.25.own_ref.pay_ref, f32[128,896]{1,0:T(8,128)} %copy-done.4, f32[128,896]{1,0:T(8,128)} %copy-done.5, f32[128,640]{1,0:T(8,128)} %shard_map.52.refs_2_.y_ref), custom_call_target="tpu_custom_call" | custom-call | tf_op jit(solution)/shard_map/pallas_call | solution.py:380
  245.1 4.0 %collective-permute-start.7 = (f32[128,640]{1,0:T(8,128)}, f32[128,640]{1,0:T(8,128)S(1)}, u32[]{:S(2)}, u32[]{:S(2)}) collective-permute-start(f32[128,640]{1,0:T(8,128)} %get-tuple-element.29), channel_id=1, source_target_pairs={{0,64},{16,80},{32,96},{48,112},{64,0},{80,16},{96,32},{112,48},{1... | collective-permute-start | bytes 983048 | tf_op jit(solution)/shard_map/ppermute | solution.py:393
  249.0 9.8 %collective-permute-done.7.refs_0_ = f32[128,640]{1,0:T(8,128)S(1)} collective-permute-done((f32[128,640]{1,0:T(8,128)}, f32[128,640]{1,0:T(8,128)S(1)}, u32[]{:S(2)}, u32[]{:S(2)}) %collective-permute-start.7) | collective-permute-done | bytes 327712 | tf_op jit(solution)/shard_map/ppermute | solution.py:393
  258.8 1.9 collective-permute-start.8
  260.7 2.3 shard_map.54.refs_2_.y_ref
  263.8 4.8 %shard_map.55 = (f32[128,640]{1,0:T(8,128)}, f32[128,384]{1,0:T(8,128)}) custom-call(s32[1]{0:T(128)} %bitcast.core_ref, f32[128,1152]{1,0:T(8,128)} %get-tuple-element.28.own_ref.pay_ref, f32[128,640]{1,0:T(8,128)} %copy-done.7, f32[128,640]{1,0:T(8,128)} %copy-done.8, f32[128,512]{1,0:T(8,128)} %shard_map.54.refs_2_.y_ref), custom_call_target="tpu_custom_call" | custom-call | tf_op jit(solution)/shard_map/pallas_call | solution.py:380
  268.6 3.4 %collective-permute-start.9 = (f32[128,640]{1,0:T(8,128)}, f32[128,640]{1,0:T(8,128)S(1)}, u32[]{:S(2)}, u32[]{:S(2)}) collective-permute-start(f32[128,640]{1,0:T(8,128)} %get-tuple-element.31.own_ref.pay_ref), channel_id=1, source_target_pairs={{0,128},{16,144},{32,160},{48,176},{64,192},{80,208},{96,224},{112... | collective-permute-start | bytes 983048 | tf_op jit(solution)/shard_map/ppermute | solution.py:393
  271.9 2.3 shard_map.56.refs_1_.y_ref
  274.3 6.5 %collective-permute-done.9.refs_0_ = f32[128,640]{1,0:T(8,128)S(1)} collective-permute-done((f32[128,640]{1,0:T(8,128)}, f32[128,640]{1,0:T(8,128)S(1)}, u32[]{:S(2)}, u32[]{:S(2)}) %collective-permute-start.9) | collective-permute-done | bytes 327712 | tf_op jit(solution)/shard_map/ppermute | solution.py:393
  281.5 4.1 %shard_map.57 = (f32[128,256]{1,0:T(8,128)}, f32[128,256]{1,0:T(8,128)}) custom-call(s32[1]{0:T(128)} %bitcast.core_ref, f32[128,640]{1,0:T(8,128)} %get-tuple-element.31.own_ref.pay_ref, f32[128,640]{1,0:T(8,128)} %copy-done.6, f32[128,384]{1,0:T(8,128)} %shard_map.56.refs_1_.y_ref), custom_call_target="tpu_custom_call" | custom-call | tf_op jit(solution)/shard_map/pallas_call | solution.py:380
  285.6 4.9 %collective-permute-start.10 = (f32[128,256]{1,0:T(8,128)}, f32[128,256]{1,0:T(8,128)S(1)}, u32[]{:S(2)}, u32[]{:S(2)}) collective-permute-start(f32[128,256]{1,0:T(8,128)} %get-tuple-element.33.own_ref), channel_id=1, source_target_pairs={{0,256},{16,272},{32,288},{48,304},{64,320},{80,336},{96,352},{112... | collective-permute-start | bytes 393224 | tf_op jit(solution)/shard_map/ppermute | solution.py:393
  290.5 2.2 shard_map.58.y_ref
  294.9 3.3 %shard_map.59 = f32[128,128]{1,0:T(8,128)} custom-call(s32[1,128]{1,0:T(1,128)} %order_ref.3, f32[128,128]{1,0:T(8,128)} %r_ref.3, f32[128,256]{1,0:T(8,128)} %get-tuple-element.33.own_ref, f32[128,256]{1,0:T(8,128)} %copy-done.9, f32[128,256]{1,0:T(8,128)} %shard_map.58.y_ref), custom_call_target="tpu_custom_call" | custom-call | tf_op jit(solution)/shard_map/pallas_call | solution.py:380
  (32 shorter events, 11.7 us)
Async XLA Ops:
  6.5 186.7 %all-gather.2.cloned.1.call-start = ((), (), s32[]{:S(2)}) async-start(), calls=%async_computation | async-start | bytes 7798784 | tf_op jit(solution)/shard_map/all_gather | solution.py:486
  10.7 37.1 %collective-permute-start.1 = (f32[128,1408]{1,0:T(8,128)}, f32[128,1408]{1,0:T(8,128)S(1)}, u32[]{:S(2)}, u32[]{:S(2)}) collective-permute-start(f32[128,1408]{1,0:T(8,128)} %shard_map.46.first_ref.zs0), channel_id=1, source_target_pairs={{0,2},{1,3},{2,0},{3,1},{4,6},{5,7},{6,4},{7,5},{8,10},{9,11},{10,... | collective-permute-start | bytes 2162696 | tf_op jit(solution)/shard_map/ppermute | solution.py:393
  15.9 35.2 %collective-permute-start = (f32[128,1408]{1,0:T(8,128)}, f32[128,1408]{1,0:T(8,128)S(1)}, u32[]{:S(2)}, u32[]{:S(2)}) collective-permute-start(f32[128,1408]{1,0:T(8,128)} %shard_map.46.first_ref.zs0), channel_id=1, source_target_pairs={{0,1},{1,0},{2,3},{3,2},{4,5},{5,4},{6,7},{7,6},{8,9},{9,8},{10,11... | collective-permute-start | bytes 2162696 | tf_op jit(solution)/shard_map/ppermute | solution.py:393
  47.8 10.6 %copy-start = (f32[128,1408]{1,0:T(8,128)}, f32[128,1408]{1,0:T(8,128)S(1)}, u32[]{:S(2)}) copy-start(f32[128,1408]{1,0:T(8,128)S(1)} %collective-permute-done.1.first_ref.zs2) | copy-start | bytes 2162692
  47.8 19.1 %collective-permute-start.2 = (f32[128,1408]{1,0:T(8,128)S(1)}, f32[128,1408]{1,0:T(8,128)S(1)}, u32[]{:S(2)}, u32[]{:S(2)}) collective-permute-start(f32[128,1408]{1,0:T(8,128)S(1)} %collective-permute-done.1.first_ref.zs2), channel_id=1, source_target_pairs={{0,1},{1,0},{2,3},{3,2},{4,5},{5,4},{6,7},{7,6},{8,9},{9,8},{10,11... | collective-permute-start | bytes 2162696 | tf_op jit(solution)/shard_map/ppermute | solution.py:393
  51.0 0.9 copy-start.1
  66.9 0.9 copy-start.2
  88.5 3.4 %collective-permute-start.3 = (f32[32,896]{1,0:T(8,128)}, f32[32,896]{1,0:T(8,128)S(1)}, u32[]{:S(2)}, u32[]{:S(2)}) collective-permute-start(f32[32,896]{1,0:T(8,128)} %get-tuple-element.21), channel_id=1, source_target_pairs={{0,16},{16,0},{32,48},{48,32},{64,80},{80,64},{96,112},{112,96},{1... | collective-permute-start | bytes 344072 | tf_op jit(solution)/shard_map/ppermute | solution.py:393
  207.2 5.1 %collective-permute-start.4 = (f32[128,2560]{1,0:T(8,128)}, f32[128,2560]{1,0:T(8,128)S(1)}, u32[]{:S(2)}, u32[]{:S(2)}) collective-permute-start(f32[128,2560]{1,0:T(8,128)} %get-tuple-element.23.own_ref.pay_ref), channel_id=1, source_target_pairs={{0,16},{16,0},{32,48},{48,32},{64,80},{80,64},{96,112},{112,96},{1... | collective-permute-start | bytes 3932168 | tf_op jit(solution)/shard_map/ppermute | solution.py:393
  212.4 1.1 copy-start.3
  219.6 14.7 %collective-permute-start.5 = (f32[128,896]{1,0:T(8,128)}, f32[128,896]{1,0:T(8,128)S(1)}, u32[]{:S(2)}, u32[]{:S(2)}) collective-permute-start(f32[128,896]{1,0:T(8,128)} %get-tuple-element.26), channel_id=1, source_target_pairs={{0,32},{16,48},{32,0},{48,16},{64,96},{80,112},{96,64},{112,80},{1... | collective-permute-start | bytes 1376264 | tf_op jit(solution)/shard_map/ppermute | solution.py:393
  234.2 4.8 %copy-start.4 = (f32[128,896]{1,0:T(8,128)}, f32[128,896]{1,0:T(8,128)S(1)}, u32[]{:S(2)}) copy-start(f32[128,896]{1,0:T(8,128)S(1)} %collective-permute-done.5.refs_0_) | copy-start | bytes 1376260
  234.2 4.8 %collective-permute-start.6 = (f32[128,896]{1,0:T(8,128)S(1)}, f32[128,896]{1,0:T(8,128)S(1)}, u32[]{:S(2)}, u32[]{:S(2)}) collective-permute-start(f32[128,896]{1,0:T(8,128)S(1)} %collective-permute-done.5.refs_0_), channel_id=1, source_target_pairs={{0,16},{16,0},{32,48},{48,32},{64,80},{80,64},{96,112},{112,96},{1... | collective-permute-start | bytes 1376264 | tf_op jit(solution)/shard_map/ppermute | solution.py:393
  239.0 0.8 copy-start.5
  245.1 13.7 %collective-permute-start.7 = (f32[128,640]{1,0:T(8,128)}, f32[128,640]{1,0:T(8,128)S(1)}, u32[]{:S(2)}, u32[]{:S(2)}) collective-permute-start(f32[128,640]{1,0:T(8,128)} %get-tuple-element.29), channel_id=1, source_target_pairs={{0,64},{16,80},{32,96},{48,112},{64,0},{80,16},{96,32},{112,48},{1... | collective-permute-start | bytes 983048 | tf_op jit(solution)/shard_map/ppermute | solution.py:393
  258.8 4.3 %copy-start.7 = (f32[128,640]{1,0:T(8,128)}, f32[128,640]{1,0:T(8,128)S(1)}, u32[]{:S(2)}) copy-start(f32[128,640]{1,0:T(8,128)S(1)} %collective-permute-done.7.refs_0_) | copy-start | bytes 983044
  258.8 4.3 %collective-permute-start.8 = (f32[128,640]{1,0:T(8,128)S(1)}, f32[128,640]{1,0:T(8,128)S(1)}, u32[]{:S(2)}, u32[]{:S(2)}) collective-permute-start(f32[128,640]{1,0:T(8,128)S(1)} %collective-permute-done.7.refs_0_), channel_id=1, source_target_pairs={{0,16},{16,0},{32,48},{48,32},{64,80},{80,64},{96,112},{112,96},{1... | collective-permute-start | bytes 983048 | tf_op jit(solution)/shard_map/ppermute | solution.py:393
  263.1 0.7 copy-start.8
  268.6 12.2 %collective-permute-start.9 = (f32[128,640]{1,0:T(8,128)}, f32[128,640]{1,0:T(8,128)S(1)}, u32[]{:S(2)}, u32[]{:S(2)}) collective-permute-start(f32[128,640]{1,0:T(8,128)} %get-tuple-element.31.own_ref.pay_ref), channel_id=1, source_target_pairs={{0,128},{16,144},{32,160},{48,176},{64,192},{80,208},{96,224},{112... | collective-permute-start | bytes 983048 | tf_op jit(solution)/shard_map/ppermute | solution.py:393
  280.8 0.7 copy-start.6
  285.6 8.6 %collective-permute-start.10 = (f32[128,256]{1,0:T(8,128)}, f32[128,256]{1,0:T(8,128)S(1)}, u32[]{:S(2)}, u32[]{:S(2)}) collective-permute-start(f32[128,256]{1,0:T(8,128)} %get-tuple-element.33.own_ref), channel_id=1, source_target_pairs={{0,256},{16,272},{32,288},{48,304},{64,320},{80,336},{96,352},{112... | collective-permute-start | bytes 393224 | tf_op jit(solution)/shard_map/ppermute | solution.py:393
  294.3 0.6 copy-start.9
Sparse Core Ops, SparseCore 0:
  93.7 99.4 all-gather.1

commit v3 on v2

--- a/solution.py
+++ b/solution.py
@@ -15,26 +15,21 @@
 HALF = jnp.bfloat16
 
 
-def halves(a):
-    top = a.astype(HALF)
-    return top, (a - top.astype(F32)).astype(HALF)
-
-
-def product(a, b, dims):
-    def dot(x, y):
-        return lax.dot_general(x, y, (dims, ((), ())), preferred_element_type=F32)
-
-    a_top, a_low = halves(a)
-    b_top, b_low = halves(b)
-    return dot(a_top, b_top) + (dot(a_top, b_low) + dot(a_low, b_top))
+def product(a, b, axis):
+    a_top, b_top = a.astype(HALF), b.astype(HALF)
+    a_low = (a - a_top.astype(F32)).astype(HALF)
+    b_low = (b - b_top.astype(F32)).astype(HALF)
+    left = jnp.concatenate([a_top, a_low, a_top], axis=axis)
+    right = jnp.concatenate([b_top, b_top, b_low], axis=0)
+    return lax.dot_general(left, right, (((axis,), (0,)), ((), ())), preferred_element_type=F32)
 
 
 def mm(a, b):
-    return product(a, b, ((1,), (0,)))
+    return product(a, b, 1)
 
 
 def tn(a, b):
-    return product(a, b, ((0,), (0,)))
+    return product(a, b, 0)
 
 
 def exact(a, b):
@@ -100,9 +95,9 @@
     return found
 
 
-def pair_inverse(s_first, s_second):
+def pair_inverse(s_sum):
     unit = eye()
-    r = 0.5 * (s_first + s_second - unit)
+    r = 0.5 * (s_sum - unit)
     t = 7.0
     x = (0.5 * (1.0 + 1.0 / t)) * (unit + r)
     r = (1.0 + 1.0 / t) * mm(r, r) - (1.0 / t) * unit
@@ -132,7 +127,7 @@
         exact(z[:, sl(nb, nb + 1)], tn(z[:, sl(0, 1)], z[:, sl(1, nb)]))
         for z in refs
     ]
-    t = pair_inverse(first_ref[:, sl(nb, nb + 1)], second_ref[:, sl(nb, nb + 1)])
+    t = pair_inverse(first_ref[:, sl(nb, nb + 1)] + second_ref[:, sl(nb, nb + 1)])
     x = mm(t, n[0] + n[1])
     for i, z in enumerate(refs):
         weights = n[i] + mm(z[:, sl(nb, nb + 1)], x)
@@ -162,7 +157,7 @@
     m = [tn(z[rows[n], sl(1, 2)], y[rows[n], sl(1, nb)]) for n in range(2)]
     s = unit_inverse([m[n][:, :B] for n in range(2)], x_scr, r_scr)
     nn = [mm(s[n], m[n][:, B:]) for n in range(2)]
-    x = mm(pair_inverse(s[0], s[1]), nn[0] + nn[1])
+    x = mm(pair_inverse(s[0] + s[1]), nn[0] + nn[1])
     last = nb - 1
     for n in range(2):
         weights = nn[n] + mm(s[n], x)
@@ -185,21 +180,34 @@
             m2[:, sl(a - 2, a - 1)], n2[:, sl(a - 3, wide)]
         )
         at += nb - a
-    rows = pl.ds(pl.multiple_of(place_ref[0] * (B // 4), B // 4), B // 4)
     head, half = cuts(nb)
-    out_ref[:, sl(0, head)] = act_ref[rows, sl(0, head)]
     first = sl(head, head + half)
     second = sl(head + half, head + 2 * half)
-
-    @pl.when(place_ref[1] == 0)
-    def _():
-        out_ref[:, first] = act_ref[rows, first]
-        send_ref[...] = act_ref[rows, second]
-
-    @pl.when(place_ref[1] == 1)
-    def _():
-        out_ref[:, first] = act_ref[rows, second]
-        send_ref[...] = act_ref[rows, first]
+    for part in range(2):
+        rows = pl.ds(pl.multiple_of(part * (B // 2) + place_ref[0] * SHARE, SHARE), SHARE)
+        put = slice(part * SHARE, (part + 1) * SHARE)
+        out_ref[put, sl(0, head)] = act_ref[rows, sl(0, head)]
+
+        @pl.when(place_ref[1] == 0)
+        def _():
+            out_ref[put, first] = act_ref[rows, first]
+            send_ref[put, :] = act_ref[rows, second]
+
+        @pl.when(place_ref[1] == 1)
+        def _():
+            out_ref[put, first] = act_ref[rows, second]
+            send_ref[put, :] = act_ref[rows, first]
+
+
+SHARE = B // 8
+
+
+def halve_kernel(cut, bit_ref, out_ref, got_ref, keep_ref, give_ref):
+    bit = bit_ref[0]
+    for to, at in ((keep_ref, bit), (give_ref, 1 - bit)):
+        rows = pl.ds(pl.multiple_of(at * SHARE, SHARE), SHARE)
+        to[:, :cut] = out_ref[rows, :cut]
+        to[:, cut:] = out_ref[rows, cut:] + got_ref[rows, :]
 
 
 def cuts(nb):
@@ -209,7 +217,7 @@
 
 def ring_kernel(
     nb, side_ref, all_ref, own_ref, pay_ref, out_ref,
-    act_ref, pas_ref, la, lb, q, m, nn, tot, x_scr, r_scr, s_scr, sem,
+    act_ref, pas_ref, la, lb, m, nn, tot, x_scr, r_scr, s_scr, sem,
 ):
     wide = nb - 3
     deep = nb - 4
@@ -224,30 +232,21 @@
         copy.start()
     copies[0].wait()
 
-    def piece(group, k):
-        return act_ref[sl(group, group + 1), sl(k, k + 1)]
-
     for node in range(2):
-        g, h = 2 * node, 2 * node + 1
-        for k in range(wide):
-            q[node, :, sl(k, k + 1)] = piece(g, 1 + k) + piece(h, 1 + k)
-        t = pair_inverse(piece(g, 0), piece(h, 0))
-        x = mm(t, q[node])
+        rows = sl(node, node + 1)
+        q = act_ref[rows, sl(1, 1 + wide)]
+        x = mm(pair_inverse(act_ref[rows, :B]), q)
         m[node] = x
-        lb[sl(node, node + 1), :] = x[:, B:]
-        la[sl(node, node + 1), :] = q[node, :, B:]
-        m3 = tn(q[node, :, :B], x)
-        for k in range(wide):
-            nn[node, :, sl(k, k + 1)] = (
-                piece(g, 1 + wide + k) + piece(h, 1 + wide + k) - m3[:, sl(k, k + 1)]
-            )
+        lb[rows, :] = x[:, B:]
+        la[rows, :] = q[:, B:]
+        nn[node] = act_ref[rows, sl(1 + wide, active)] - tn(q[:, :B], x)
     s = unit_inverse([nn[0, :, :B], nn[1, :, :B]], x_scr, r_scr)
     for node in range(2):
         s_scr[node] = s[node]
         la[sl(2 + node, 3 + node), :] = nn[node, :, B:]
         lb[sl(2 + node, 3 + node), :] = mm(s[node], nn[node, :, B:])
     q3 = lb[sl(2, 3), :] + lb[sl(3, 4), :]
-    x3 = mm(pair_inverse(s[0], s[1]), q3)
+    x3 = mm(pair_inverse(s[0] + s[1]), q3)
     la[sl(4, 5), :] = q3
     lb[sl(4, 5), :] = x3
     copies[1].wait()
@@ -255,12 +254,7 @@
     tot[...] = jnp.zeros_like(tot)
 
     def over(part):
-        return (
-            pas_ref[sl(0, 1), part]
-            + pas_ref[sl(1, 2), part]
-            + pas_ref[sl(2, 3), part]
-            + pas_ref[sl(3, 4), part]
-        )
+        return pas_ref[sl(0, 1), part] + pas_ref[sl(1, 2), part]
 
     tot[:, sl(0, deep)] = over(sl(0, deep))
     lanes = pl.ds(pl.multiple_of((deep + half * side_ref[1]) * B, B), half * B)
@@ -317,7 +311,7 @@
     x_scr, r_scr = refs[-2:]
     wide = nb - 1 - level
     q = own_ref[:, sl(1, 1 + wide)] + other(1, 1 + wide)
-    x = mm(pair_inverse(own_ref[:, :B], other(0, 1)), q)
+    x = mm(pair_inverse(own_ref[:, :B] + other(0, 1)), q)
     x_ref[...] = x
 
     def panel(a):
@@ -365,7 +359,7 @@
 def finish_kernel(order_ref, r_ref, own_ref, other_ref, y_ref, out_ref):
     s = own_ref[:, :B]
     n = own_ref[:, B:]
-    x = mm(pair_inverse(s, other_ref[:, :B]), n + other_ref[:, B:])
+    x = mm(pair_inverse(s + other_ref[:, :B]), n + other_ref[:, B:])
     y = y_ref[:, B:] - mm(y_ref[:, :B], n + mm(s, x))
     pick = (lax.broadcasted_iota(jnp.int32, (B, B), 0) == order_ref[...]).astype(F32)
     out_ref[...] = exact(pick, tn(r_ref[...], y))
@@ -410,11 +404,10 @@
         [pay_width(levels, 4), nb - 4],
         [side, gathered, own],
         [
-            pltpu.VMEM((4 * B, active * B), F32),
-            pltpu.VMEM((4 * B, (head + half - active) * B), F32),
+            pltpu.VMEM((2 * B, active * B), F32),
+            pltpu.VMEM((2 * B, (head + half - active) * B), F32),
             pltpu.VMEM((5 * B, (nb - 4) * B), F32),
             pltpu.VMEM((5 * B, (nb - 4) * B), F32),
-            pltpu.VMEM((2, B, (nb - 3) * B), F32),
             pltpu.VMEM((2, B, (nb - 3) * B), F32),
             pltpu.VMEM((2, B, (nb - 3) * B), F32),
             pltpu.VMEM((B, (nb - 4 + 2 * half) * B), F32),
@@ -434,7 +427,7 @@
     anywhere = pl.BlockSpec(memory_space=pl.ANY)
     return run(
         functools.partial(quad_kernel, nb),
-        [(B // 4, (head + half) * B), (B // 4, half * B), nb - 2],
+        [(2 * SHARE, (head + half) * B), (2 * SHARE, half * B), nb - 2],
         [place, *zs, *ys],
         [
             pltpu.VMEM((4 * B, nb * B), F32),
@@ -447,6 +440,10 @@
     )
 
 
+def near(x):
+    return pltpu.with_memory_space_constraint(x, pltpu.VMEM)
+
+
 def merge_call(run, levels, level, core, pay, others, behind, half):
     nb = levels + 1
     split = len(others) == 2
@@ -457,7 +454,7 @@
     return run(
         functools.partial(merge_kernel, nb, level, split),
         [pay_width(levels, level + 1), levels - level] + ([half] if half else []),
-        [core, pay, *others, behind],
+        [core, pay, *[near(o) for o in others], behind],
         two + ([pltpu.VMEM((2, *others[0].shape), F32)] if split else []),
         [smem] + [vmem] * (1 + len(others)) + [anywhere],
     )
@@ -482,7 +479,15 @@
     core = lax.axis_index("outer").astype(jnp.int32) & 1
     mine, send, own = quad_call(run, levels, jnp.stack([place & 3, core]), [z0, z1, z2, z3], ys)
     cut = cuts(nb)[0] * B
-    mine = jnp.concatenate([mine[:, :cut], mine[:, cut:] + swapped(send, "outer", 0)], axis=1)
+    half = (SHARE, mine.shape[1])
+    keep, give = run(
+        part(halve_kernel, cut),
+        [half, half],
+        [(place >> 2 & 1).reshape(1), mine, near(swapped(send, "outer", 0))],
+        (),
+        [pl.BlockSpec(memory_space=pltpu.SMEM)] + [pl.BlockSpec(memory_space=pltpu.VMEM)] * 2,
+    )
+    mine = keep + swapped(give, "inner", 2)
     gathered = lax.all_gather(mine, "inner", tiled=True)
     pay, y = ring_call(run, levels, jnp.stack([place >> 3, core]), gathered, own)
     core = core.reshape(1)
@@ -503,7 +508,7 @@
         y = run(update_kernel, [wide], [pay, found[1], y], (), [head, vmem, vmem], (1,))
         pay = found[0]
         half = found[2] if cut else None
-    return run(finish_kernel, [1], [leaf_order, leaf_inverse, pay, others[0], y])
+    return run(finish_kernel, [1], [leaf_order, leaf_inverse, pay, near(others[0]), y])
 
 
 def solution(mesh):

time: 306 us -> 308 us (level)
  the two profiles are of different devices: /device:TPU:2 before, /device:TPU:8 now
where the time goes in v3:
time: 308 us; the launch traced here: 307 us
  waiting for transfers between devices  173 us (56%)
  Pallas kernels  74.1 us (24%)
  starting transfers between devices  42 us (14%)
  between operations  13.5 us (4%)
    ppermute x12, waiting for transfers between devices, swapped(): return lax.ppermute(block, axis, [(k, k ^ 1 << bit) for k in range(count)])  94.3 us
    all_gather x1, waiting for transfers between devices, body(): gathered = lax.all_gather(mine, 'inner', tiled=True)  78.6 us
    pallas_call x15, Pallas kernels, call(): pl.pallas_call(kernel, out_shape=shapes[0] if one else shapes, grid=grid,...  74.1 us
    ppermute x12, starting transfers between devices, swapped(): return lax.ppermute(block, axis, [(k, k ^ 1 << bit) for k in range(count)])  42 us
  transfers between devices with their start and end apart: 13, of which 10 were waited for; matrix products, arithmetic and copies ran while one was open for 0% of the time, Pallas kernels for 5%

profile of v3, /device:TPU:8, one launch (start us, length us, event | category | flops | bytes accessed | tf_op | source)
XLA Modules:
  0.0 307.2 jit_solution(6871303554413463285)
XLA Ops:
  6.5 4.2 %shard_map.46.first_ref.zs0 = f32[128,1408]{1,0:T(8,128)} custom-call(s32[1,128]{1,0:T(1,128)} %order_ref.3, f32[128,128]{1,0:T(8,128)} %r_ref.3, f32[9,128,128]{2,1,0:T(8,128)} %u_ref.1, f32[128,128]{1,0:T(8,128)} %rhs_ref.1), custom_call_target="tpu_custom_call" | custom-call | tf_op jit(solution)/shard_map/pallas_call | solution.py:374
  10.7 5.2 %collective-permute-start.1 = (f32[128,1408]{1,0:T(8,128)}, f32[128,1408]{1,0:T(8,128)S(1)}, u32[]{:S(2)}, u32[]{:S(2)}) collective-permute-start(f32[128,1408]{1,0:T(8,128)} %shard_map.46.first_ref.zs0), channel_id=1, source_target_pairs={{0,2},{1,3},{2,0},{3,1},{4,6},{5,7},{6,4},{7,5},{8,10},{9,11},{10,... | collective-permute-start | bytes 2162696 | tf_op jit(solution)/shard_map/ppermute | solution.py:387
  15.9 3.8 %collective-permute-start = (f32[128,1408]{1,0:T(8,128)}, f32[128,1408]{1,0:T(8,128)S(1)}, u32[]{:S(2)}, u32[]{:S(2)}) collective-permute-start(f32[128,1408]{1,0:T(8,128)} %shard_map.46.first_ref.zs0), channel_id=1, source_target_pairs={{0,1},{1,0},{2,3},{3,2},{4,5},{5,4},{6,7},{7,6},{8,9},{9,8},{10,11... | collective-permute-start | bytes 2162696 | tf_op jit(solution)/shard_map/ppermute | solution.py:387
  19.7 28.1 %collective-permute-done.1.first_ref.zs2 = f32[128,1408]{1,0:T(8,128)S(1)} collective-permute-done((f32[128,1408]{1,0:T(8,128)}, f32[128,1408]{1,0:T(8,128)S(1)}, u32[]{:S(2)}, u32[]{:S(2)}) %collective-permute-start.1) | collective-permute-done | bytes 720928 | tf_op jit(solution)/shard_map/ppermute | solution.py:387
  47.8 2.7 collective-permute-start.2
  51.9 5.6 %shard_map.47.y01 = f32[256,1152]{1,0:T(8,128)} custom-call(f32[128,1408]{1,0:T(8,128)} %shard_map.46.first_ref.zs0, f32[128,1408]{1,0:T(8,128)} %copy-done.1), custom_call_target="tpu_custom_call" | custom-call | tf_op jit(solution)/shard_map/pallas_call | solution.py:374
  57.5 9.4 %collective-permute-done.2.second_ref.zs3 = f32[128,1408]{1,0:T(8,128)S(1)} collective-permute-done((f32[128,1408]{1,0:T(8,128)S(1)}, f32[128,1408]{1,0:T(8,128)S(1)}, u32[]{:S(2)}, u32[]{:S(2)}) %collective-permute-start.2) | collective-permute-done | bytes 720928 | tf_op jit(solution)/shard_map/ppermute | solution.py:387
  67.8 5.6 %shard_map.48.y23 = f32[256,1152]{1,0:T(8,128)} custom-call(f32[128,1408]{1,0:T(8,128)} %copy-done, f32[128,1408]{1,0:T(8,128)} %copy-done.2), custom_call_target="tpu_custom_call" | custom-call | tf_op jit(solution)/shard_map/pallas_call | solution.py:374
  73.4 13.1 %shard_map.49 = (f32[32,3584]{1,0:T(8,128)}, f32[32,896]{1,0:T(8,128)}, f32[128,1024]{1,0:T(8,128)}) custom-call(s32[2]{0:T(128)} %pad_add_fusion.1.place_ref, f32[128,1408]{1,0:T(8,128)} %shard_map.46.first_ref.zs0, f32[128,1408]{1,0:T(8,128)} %copy-done.1, f32[128,1408]{1,0:T(8,128)} %copy-done, f32[128,1408]{1,0:T(8,128)} %copy-done.2, ...), custom_call_target="tpu_custom_call" | custom-call | tf_op jit(solution)/shard_map/pallas_call | solution.py:374
  86.5 1.9 collective-permute-start.3
  91.7 9.1 %collective-permute-start.4 = (f32[16,3584]{1,0:T(8,128)}, f32[16,3584]{1,0:T(8,128)S(1)}, u32[]{:S(2)}, u32[]{:S(2)}) collective-permute-start(f32[16,3584]{1,0:T(8,128)} %get-tuple-element.25), channel_id=1, source_target_pairs={{0,4},{1,5},{2,6},{3,7},{4,0},{5,1},{6,2},{7,3},{8,12},{9,13},{10,... | collective-permute-start | bytes 688136 | tf_op jit(solution)/shard_map/ppermute | solution.py:387
  100.8 20.9 %collective-permute-done.4 = f32[16,3584]{1,0:T(8,128)S(1)} collective-permute-done((f32[16,3584]{1,0:T(8,128)}, f32[16,3584]{1,0:T(8,128)S(1)}, u32[]{:S(2)}, u32[]{:S(2)}) %collective-permute-start.4) | collective-permute-done | bytes 229408 | tf_op jit(solution)/shard_map/ppermute | solution.py:387
  124.0 78.6 %all-gather.2.cloned.1.call-done.all_ref = f32[256,3584]{1,0:T(8,128)} async-done(((f32[16,3584]{1,0:T(8,128)}), f32[256,3584]{1,0:T(8,128)}) %all-gather.2.cloned.1.call-update) | async-done | bytes 3670032 | tf_op jit(solution)/shard_map/all_gather | solution.py:491
  202.6 12.5 %shard_map.51 = (f32[128,2560]{1,0:T(8,128)}, f32[128,768]{1,0:T(8,128)}) custom-call(s32[2]{0:T(128)} %pad_add_fusion.side_ref, f32[256,3584]{1,0:T(8,128)} %all-gather.2.cloned.1.call-done.all_ref, f32[128,1024]{1,0:T(8,128)} %get-tuple-element.26.own_ref), custom_call_target="tpu_custom_call" | custom-call | tf_op jit(solution)/shard_map/pallas_call | solution.py:374
  217.1 3.2 %collective-permute-done.5.refs_0_ = f32[128,2560]{1,0:T(8,128)S(1)} collective-permute-done((f32[128,2560]{1,0:T(8,128)}, f32[128,2560]{1,0:T(8,128)S(1)}, u32[]{:S(2)}, u32[]{:S(2)}) %collective-permute-start.5) | collective-permute-done | bytes 1310752 | tf_op jit(solution)/shard_map/ppermute | solution.py:387
  220.3 5.4 %shard_map.52 = (f32[128,1792]{1,0:T(8,128)}, f32[128,640]{1,0:T(8,128)}, f32[128,896]{1,0:T(8,128)}) custom-call(s32[1]{0:T(128)} %bitcast.core_ref, f32[128,2560]{1,0:T(8,128)} %get-tuple-element.27.own_ref.pay_ref, f32[128,2560]{1,0:T(8,128)S(1)} %collective-permute-done.5.refs_0_, f32[128,768]{1,0:T(8,128)} %get-tuple-element.28.refs_1_.y_ref), custom_call_target="tpu_custom_call" | custom-call | tf_op jit(solution)/shard_map/pallas_call | solution.py:374
  225.7 3.1 %collective-permute-start.6 = (f32[128,896]{1,0:T(8,128)}, f32[128,896]{1,0:T(8,128)S(1)}, u32[]{:S(2)}, u32[]{:S(2)}) collective-permute-start(f32[128,896]{1,0:T(8,128)} %get-tuple-element.30), channel_id=1, source_target_pairs={{0,32},{16,48},{32,0},{48,16},{64,96},{80,112},{96,64},{112,80},{1... | collective-permute-start | bytes 1376264 | tf_op jit(solution)/shard_map/ppermute | solution.py:387
  228.7 11.6 %collective-permute-done.6.refs_0_ = f32[128,896]{1,0:T(8,128)S(1)} collective-permute-done((f32[128,896]{1,0:T(8,128)}, f32[128,896]{1,0:T(8,128)S(1)}, u32[]{:S(2)}, u32[]{:S(2)}) %collective-permute-start.6) | collective-permute-done | bytes 458784 | tf_op jit(solution)/shard_map/ppermute | solution.py:387
  242.2 2.4 shard_map.53.refs_2_.y_ref
  244.7 5.2 %shard_map.54 = (f32[128,1152]{1,0:T(8,128)}, f32[128,512]{1,0:T(8,128)}, f32[128,640]{1,0:T(8,128)}) custom-call(s32[1]{0:T(128)} %bitcast.core_ref, f32[128,1792]{1,0:T(8,128)} %get-tuple-element.29.own_ref.pay_ref, f32[128,896]{1,0:T(8,128)S(1)} %collective-permute-done.6.refs_0_, f32[128,896]{1,0:T(8,128)S(1)} %collective-permute-done.7.refs_1_, ...), custom_call_target="tpu_custom_call" | custom-call | tf_op jit(solution)/shard_map/pallas_call | solution.py:374
  249.9 4.6 %collective-permute-start.8 = (f32[128,640]{1,0:T(8,128)}, f32[128,640]{1,0:T(8,128)S(1)}, u32[]{:S(2)}, u32[]{:S(2)}) collective-permute-start(f32[128,640]{1,0:T(8,128)} %get-tuple-element.33), channel_id=1, source_target_pairs={{0,64},{16,80},{32,96},{48,112},{64,0},{80,16},{96,32},{112,48},{1... | collective-permute-start | bytes 983048 | tf_op jit(solution)/shard_map/ppermute | solution.py:387
  254.5 9.1 %collective-permute-done.8.refs_0_ = f32[128,640]{1,0:T(8,128)S(1)} collective-permute-done((f32[128,640]{1,0:T(8,128)}, f32[128,640]{1,0:T(8,128)S(1)}, u32[]{:S(2)}, u32[]{:S(2)}) %collective-permute-start.8) | collective-permute-done | bytes 327712 | tf_op jit(solution)/shard_map/ppermute | solution.py:387
  265.6 2.3 shard_map.55.refs_2_.y_ref
  267.9 4.4 %shard_map.56 = (f32[128,640]{1,0:T(8,128)}, f32[128,384]{1,0:T(8,128)}) custom-call(s32[1]{0:T(128)} %bitcast.core_ref, f32[128,1152]{1,0:T(8,128)} %get-tuple-element.32.own_ref.pay_ref, f32[128,640]{1,0:T(8,128)S(1)} %collective-permute-done.8.refs_0_, f32[128,640]{1,0:T(8,128)S(1)} %collective-permute-done.9.refs_1_, f32[128,512]{1,0:T(8,128)} %shard_map.55.refs_2_.y_ref), custom_call_target="tpu_custom_call" | custom-call | tf_op jit(solution)/shard_map/pallas_call | solution.py:374
  272.3 2.2 collective-permute-start.10
  274.5 2.2 shard_map.57.refs_1_.y_ref
  276.7 7.8 %collective-permute-done.10.refs_0_ = f32[128,640]{1,0:T(8,128)S(1)} collective-permute-done((f32[128,640]{1,0:T(8,128)}, f32[128,640]{1,0:T(8,128)S(1)}, u32[]{:S(2)}, u32[]{:S(2)}) %collective-permute-start.10) | collective-permute-done | bytes 327712 | tf_op jit(solution)/shard_map/ppermute | solution.py:387
  284.5 4.0 %shard_map.58 = (f32[128,256]{1,0:T(8,128)}, f32[128,256]{1,0:T(8,128)}) custom-call(s32[1]{0:T(128)} %bitcast.core_ref, f32[128,640]{1,0:T(8,128)} %get-tuple-element.35.own_ref.pay_ref, f32[128,640]{1,0:T(8,128)S(1)} %collective-permute-done.10.refs_0_, f32[128,384]{1,0:T(8,128)} %shard_map.57.refs_1_.y_ref), custom_call_target="tpu_custom_call" | custom-call | tf_op jit(solution)/shard_map/pallas_call | solution.py:374
  288.5 3.7 %collective-permute-start.11 = (f32[128,256]{1,0:T(8,128)}, f32[128,256]{1,0:T(8,128)S(1)}, u32[]{:S(2)}, u32[]{:S(2)}) collective-permute-start(f32[128,256]{1,0:T(8,128)} %get-tuple-element.37.own_ref), channel_id=1, source_target_pairs={{0,256},{16,272},{32,288},{48,304},{64,320},{80,336},{96,352},{112... | collective-permute-start | bytes 393224 | tf_op jit(solution)/shard_map/ppermute | solution.py:387
  292.2 2.2 shard_map.59.y_ref
  294.4 2.7 collective-permute-done.11.other_ref
  297.1 3.2 %shard_map.60 = f32[128,128]{1,0:T(8,128)} custom-call(s32[1,128]{1,0:T(1,128)} %order_ref.3, f32[128,128]{1,0:T(8,128)} %r_ref.3, f32[128,256]{1,0:T(8,128)} %get-tuple-element.37.own_ref, f32[128,256]{1,0:T(8,128)S(1)} %collective-permute-done.11.other_ref, f32[128,256]{1,0:T(8,128)} %shard_map.59.y_ref), custom_call_target="tpu_custom_call" | custom-call | tf_op jit(solution)/shard_map/pallas_call | solution.py:374
  (19 shorter events, 13.8 us)
Async XLA Ops:
  6.5 196.1 %all-gather.2.cloned.1.call-start = ((), (), s32[]{:S(2)}) async-start(), calls=%async_computation | async-start | bytes 3899392 | tf_op jit(solution)/shard_map/all_gather | solution.py:491
  10.7 37.1 %collective-permute-start.1 = (f32[128,1408]{1,0:T(8,128)}, f32[128,1408]{1,0:T(8,128)S(1)}, u32[]{:S(2)}, u32[]{:S(2)}) collective-permute-start(f32[128,1408]{1,0:T(8,128)} %shard_map.46.first_ref.zs0), channel_id=1, source_target_pairs={{0,2},{1,3},{2,0},{3,1},{4,6},{5,7},{6,4},{7,5},{8,10},{9,11},{10,... | collective-permute-start | bytes 2162696 | tf_op jit(solution)/shard_map/ppermute | solution.py:387
  15.9 35.2 %collective-permute-start = (f32[128,1408]{1,0:T(8,128)}, f32[128,1408]{1,0:T(8,128)S(1)}, u32[]{:S(2)}, u32[]{:S(2)}) collective-permute-start(f32[128,1408]{1,0:T(8,128)} %shard_map.46.first_ref.zs0), channel_id=1, source_target_pairs={{0,1},{1,0},{2,3},{3,2},{4,5},{5,4},{6,7},{7,6},{8,9},{9,8},{10,11... | collective-permute-start | bytes 2162696 | tf_op jit(solution)/shard_map/ppermute | solution.py:387
  47.8 9.7 %copy-start = (f32[128,1408]{1,0:T(8,128)}, f32[128,1408]{1,0:T(8,128)S(1)}, u32[]{:S(2)}) copy-start(f32[128,1408]{1,0:T(8,128)S(1)} %collective-permute-done.1.first_ref.zs2) | copy-start | bytes 2162692
  47.8 19.1 %collective-permute-start.2 = (f32[128,1408]{1,0:T(8,128)S(1)}, f32[128,1408]{1,0:T(8,128)S(1)}, u32[]{:S(2)}, u32[]{:S(2)}) collective-permute-start(f32[128,1408]{1,0:T(8,128)S(1)} %collective-permute-done.1.first_ref.zs2), channel_id=1, source_target_pairs={{0,1},{1,0},{2,3},{3,2},{4,5},{5,4},{6,7},{7,6},{8,9},{9,8},{10,11... | collective-permute-start | bytes 2162696 | tf_op jit(solution)/shard_map/ppermute | solution.py:387
  51.1 0.9 copy-start.1
  66.9 0.9 copy-start.2
  86.5 3.4 %collective-permute-start.3 = (f32[32,896]{1,0:T(8,128)}, f32[32,896]{1,0:T(8,128)S(1)}, u32[]{:S(2)}, u32[]{:S(2)}) collective-permute-start(f32[32,896]{1,0:T(8,128)} %get-tuple-element.23), channel_id=1, source_target_pairs={{0,16},{16,0},{32,48},{48,32},{64,80},{80,64},{96,112},{112,96},{1... | collective-permute-start | bytes 344072 | tf_op jit(solution)/shard_map/ppermute | solution.py:387
  91.7 30.0 %collective-permute-start.4 = (f32[16,3584]{1,0:T(8,128)}, f32[16,3584]{1,0:T(8,128)S(1)}, u32[]{:S(2)}, u32[]{:S(2)}) collective-permute-start(f32[16,3584]{1,0:T(8,128)} %get-tuple-element.25), channel_id=1, source_target_pairs={{0,4},{1,5},{2,6},{3,7},{4,0},{5,1},{6,2},{7,3},{8,12},{9,13},{10,... | collective-permute-start | bytes 688136 | tf_op jit(solution)/shard_map/ppermute | solution.py:387
  215.1 5.1 %collective-permute-start.5 = (f32[128,2560]{1,0:T(8,128)}, f32[128,2560]{1,0:T(8,128)S(1)}, u32[]{:S(2)}, u32[]{:S(2)}) collective-permute-start(f32[128,2560]{1,0:T(8,128)} %get-tuple-element.27.own_ref.pay_ref), channel_id=1, source_target_pairs={{0,16},{16,0},{32,48},{48,32},{64,80},{80,64},{96,112},{112,96},{1... | collective-permute-start | bytes 3932168 | tf_op jit(solution)/shard_map/ppermute | solution.py:387
  225.7 14.7 %collective-permute-start.6 = (f32[128,896]{1,0:T(8,128)}, f32[128,896]{1,0:T(8,128)S(1)}, u32[]{:S(2)}, u32[]{:S(2)}) collective-permute-start(f32[128,896]{1,0:T(8,128)} %get-tuple-element.30), channel_id=1, source_target_pairs={{0,32},{16,48},{32,0},{48,16},{64,96},{80,112},{96,64},{112,80},{1... | collective-permute-start | bytes 1376264 | tf_op jit(solution)/shard_map/ppermute | solution.py:387
  240.3 4.4 %collective-permute-start.7 = (f32[128,896]{1,0:T(8,128)S(1)}, f32[128,896]{1,0:T(8,128)S(1)}, u32[]{:S(2)}, u32[]{:S(2)}) collective-permute-start(f32[128,896]{1,0:T(8,128)S(1)} %collective-permute-done.6.refs_0_), channel_id=1, source_target_pairs={{0,16},{16,0},{32,48},{48,32},{64,80},{80,64},{96,112},{112,96},{1... | collective-permute-start | bytes 1376264 | tf_op jit(solution)/shard_map/ppermute | solution.py:387
  249.9 13.7 %collective-permute-start.8 = (f32[128,640]{1,0:T(8,128)}, f32[128,640]{1,0:T(8,128)S(1)}, u32[]{:S(2)}, u32[]{:S(2)}) collective-permute-start(f32[128,640]{1,0:T(8,128)} %get-tuple-element.33), channel_id=1, source_target_pairs={{0,64},{16,80},{32,96},{48,112},{64,0},{80,16},{96,32},{112,48},{1... | collective-permute-start | bytes 983048 | tf_op jit(solution)/shard_map/ppermute | solution.py:387
  263.7 4.2 %collective-permute-start.9 = (f32[128,640]{1,0:T(8,128)S(1)}, f32[128,640]{1,0:T(8,128)S(1)}, u32[]{:S(2)}, u32[]{:S(2)}) collective-permute-start(f32[128,640]{1,0:T(8,128)S(1)} %collective-permute-done.8.refs_0_), channel_id=1, source_target_pairs={{0,16},{16,0},{32,48},{48,32},{64,80},{80,64},{96,112},{112,96},{1... | collective-permute-start | bytes 983048 | tf_op jit(solution)/shard_map/ppermute | solution.py:387
  272.3 12.2 %collective-permute-start.10 = (f32[128,640]{1,0:T(8,128)}, f32[128,640]{1,0:T(8,128)S(1)}, u32[]{:S(2)}, u32[]{:S(2)}) collective-permute-start(f32[128,640]{1,0:T(8,128)} %get-tuple-element.35.own_ref.pay_ref), channel_id=1, source_target_pairs={{0,128},{16,144},{32,160},{48,176},{64,192},{80,208},{96,224},{112... | collective-permute-start | bytes 983048 | tf_op jit(solution)/shard_map/ppermute | solution.py:387
  288.5 8.6 %collective-permute-start.11 = (f32[128,256]{1,0:T(8,128)}, f32[128,256]{1,0:T(8,128)S(1)}, u32[]{:S(2)}, u32[]{:S(2)}) collective-permute-start(f32[128,256]{1,0:T(8,128)} %get-tuple-element.37.own_ref), channel_id=1, source_target_pairs={{0,256},{16,272},{32,288},{48,304},{64,320},{80,336},{96,352},{112... | collective-permute-start | bytes 393224 | tf_op jit(solution)/shard_map/ppermute | solution.py:387
Sparse Core Ops, SparseCore 0:
  123.5 79.0 all-gather.1

commit v4 on v2

--- a/solution.py
+++ b/solution.py
@@ -15,26 +15,21 @@
 HALF = jnp.bfloat16
 
 
-def halves(a):
-    top = a.astype(HALF)
-    return top, (a - top.astype(F32)).astype(HALF)
-
-
-def product(a, b, dims):
-    def dot(x, y):
-        return lax.dot_general(x, y, (dims, ((), ())), preferred_element_type=F32)
-
-    a_top, a_low = halves(a)
-    b_top, b_low = halves(b)
-    return dot(a_top, b_top) + (dot(a_top, b_low) + dot(a_low, b_top))
+def product(a, b, axis):
+    a_top, b_top = a.astype(HALF), b.astype(HALF)
+    a_low = (a - a_top.astype(F32)).astype(HALF)
+    b_low = (b - b_top.astype(F32)).astype(HALF)
+    left = jnp.concatenate([a_top, a_low, a_top], axis=axis)
+    right = jnp.concatenate([b_top, b_top, b_low], axis=0)
+    return lax.dot_general(left, right, (((axis,), (0,)), ((), ())), preferred_element_type=F32)
 
 
 def mm(a, b):
-    return product(a, b, ((1,), (0,)))
+    return product(a, b, 1)
 
 
 def tn(a, b):
-    return product(a, b, ((0,), (0,)))
+    return product(a, b, 0)
 
 
 def exact(a, b):
@@ -115,33 +110,41 @@
     return x
 
 
-def leaf_kernel(nb, order_ref, r_ref, u_ref, rhs_ref, z_ref, x_scr, r_scr):
+def leaf_kernel(nb, order_ref, r_ref, u_ref, rhs_ref, z_ref):
     pick = (lax.broadcasted_iota(jnp.int32, (B, B), 0) == order_ref[...]).astype(F32)
     r = r_ref[...]
     for b in range(nb - 1):
         z_ref[:, sl(b, b + 1)] = mm(r, u_ref[b])
     z_ref[:, sl(nb - 1, nb)] = mm(r, exact_tn(pick, rhs_ref[...]))
-    z0 = z_ref[:, sl(0, 1)]
-    (s,) = unit_inverse([tn(z0, z0)], x_scr, r_scr)
-    z_ref[:, sl(nb, nb + 1)] = s
-
-
-def pair_kernel(nb, first_ref, second_ref, y_ref):
-    refs = (first_ref, second_ref)
-    n = [
-        exact(z[:, sl(nb, nb + 1)], tn(z[:, sl(0, 1)], z[:, sl(1, nb)]))
-        for z in refs
-    ]
-    t = pair_inverse(first_ref[:, sl(nb, nb + 1)], second_ref[:, sl(nb, nb + 1)])
-    x = mm(t, n[0] + n[1])
+
+
+def pair_level(nb, refs, s, n, y_ref):
+    x = mm(pair_inverse(s[0], s[1]), n[0] + n[1])
     for i, z in enumerate(refs):
-        weights = n[i] + mm(z[:, sl(nb, nb + 1)], x)
+        weights = n[i] + mm(s[i], x)
         y_ref[sl(i, i + 1), :] = z[:, sl(1, nb)] - mm(z[:, sl(0, 1)], weights)
+
+
+def near_kernel(nb, z0, z1, z2, y_ref, side_ref, x_scr, r_scr):
+    refs = (z0, z1, z2)
+    p = [tn(z[:, :B], z[...]) for z in refs]
+    s = unit_inverse([a[:, :B] for a in p], x_scr, r_scr)
+    n = [exact(s[i], p[i][:, B:]) for i in range(3)]
+    side_ref[:, :B] = s[2]
+    side_ref[:, B:] = n[2]
+    pair_level(nb, refs[:2], s, n, y_ref)
+
+
+def far_kernel(nb, z2, z3, side_ref, y_ref, x_scr, r_scr):
+    p = tn(z3[:, :B], z3[...])
+    (s,) = unit_inverse([p[:, :B]], x_scr, r_scr)
+    n = exact(s, p[:, B:])
+    pair_level(nb, (z2, z3), (side_ref[:, :B], s), (side_ref[:, B:], n), y_ref)
 
 
 def quad_kernel(
     nb, place_ref, zs0, zs1, zs2, zs3, y01, y23,
-    out_ref, send_ref, own_ref, z, y, act_ref, x_scr, r_scr, sem,
+    out_ref, keep_ref, send_ref, own_ref, z, y, act_ref, x_scr, r_scr, sem,
 ):
     copies = [
         pltpu.make_async_copy(y01, y.at[pl.ds(0, 2 * B), pl.ds(B, (nb - 1) * B)], sem.at[4]),
@@ -187,18 +190,18 @@
         at += nb - a
     rows = pl.ds(pl.multiple_of(place_ref[0] * (B // 4), B // 4), B // 4)
     head, half = cuts(nb)
-    out_ref[:, sl(0, head)] = act_ref[rows, sl(0, head)]
+    out_ref[...] = act_ref[rows, sl(0, head)]
     first = sl(head, head + half)
     second = sl(head + half, head + 2 * half)
 
     @pl.when(place_ref[1] == 0)
     def _():
-        out_ref[:, first] = act_ref[rows, first]
+        keep_ref[...] = act_ref[rows, first]
         send_ref[...] = act_ref[rows, second]
 
     @pl.when(place_ref[1] == 1)
     def _():
-        out_ref[:, first] = act_ref[rows, second]
+        keep_ref[...] = act_ref[rows, second]
         send_ref[...] = act_ref[rows, first]
 
 
@@ -208,7 +211,7 @@
 
 
 def ring_kernel(
-    nb, side_ref, all_ref, own_ref, pay_ref, out_ref,
+    nb, side_ref, all_ref, rest0, rest1, rest2, rest3, own_ref, pay_ref, out_ref,
     act_ref, pas_ref, la, lb, q, m, nn, tot, x_scr, r_scr, s_scr, sem,
 ):
     wide = nb - 3
@@ -264,7 +267,9 @@
 
     tot[:, sl(0, deep)] = over(sl(0, deep))
     lanes = pl.ds(pl.multiple_of((deep + half * side_ref[1]) * B, B), half * B)
-    tot[:, lanes] = over(sl(deep, deep + half))
+    for k, rest in enumerate((rest0, rest1, rest2, rest3)):
+        rows = pl.ds(pl.multiple_of((side_ref[2] ^ k) * (B // 4), B // 4), B // 4)
+        tot[rows, lanes] = rest[...]
     at = 0
     for k in range(deep - 1):
         part = sl(at, at + deep - k)
@@ -397,7 +402,7 @@
     return 1 + (levels - level) + sum(levels + 1 - a for a in range(level + 1, levels))
 
 
-def ring_call(run, levels, side, gathered, own):
+def ring_call(run, levels, side, gathered, rests, own):
     nb = levels + 1
     head, half = cuts(nb)
     active = 2 * levels - 3
@@ -408,10 +413,10 @@
     return run(
         functools.partial(ring_kernel, nb),
         [pay_width(levels, 4), nb - 4],
-        [side, gathered, own],
+        [side, gathered, *rests, own],
         [
             pltpu.VMEM((4 * B, active * B), F32),
-            pltpu.VMEM((4 * B, (head + half - active) * B), F32),
+            pltpu.VMEM((4 * B, (head - active) * B), F32),
             pltpu.VMEM((5 * B, (nb - 4) * B), F32),
             pltpu.VMEM((5 * B, (nb - 4) * B), F32),
             pltpu.VMEM((2, B, (nb - 3) * B), F32),
@@ -422,7 +427,7 @@
             pltpu.VMEM((2, B, B), F32),
             pltpu.SemaphoreType.DMA((2,)),
         ],
-        [smem, anywhere, vmem],
+        [smem, anywhere] + [vmem] * 5,
     )
 
 
@@ -434,7 +439,7 @@
     anywhere = pl.BlockSpec(memory_space=pl.ANY)
     return run(
         functools.partial(quad_kernel, nb),
-        [(B // 4, (head + half) * B), (B // 4, half * B), nb - 2],
+        [(B // 4, head * B), (B // 4, half * B), (B // 4, half * B), nb - 2],
         [place, *zs, *ys],
         [
             pltpu.VMEM((4 * B, nb * B), F32),
@@ -447,6 +452,10 @@
     )
 
 
+def near(x):
+    return pltpu.with_memory_space_constraint(x, pltpu.VMEM)
+
+
 def merge_call(run, levels, level, core, pay, others, behind, half):
     nb = levels + 1
     split = len(others) == 2
@@ -457,7 +466,7 @@
     return run(
         functools.partial(merge_kernel, nb, level, split),
         [pay_width(levels, level + 1), levels - level] + ([half] if half else []),
-        [core, pay, *others, behind],
+        [core, pay, *[near(o) for o in others], behind],
         two + ([pltpu.VMEM((2, *others[0].shape), F32)] if split else []),
         [smem] + [vmem] * (1 + len(others)) + [anywhere],
     )
@@ -471,20 +480,25 @@
     two = [pltpu.VMEM((2, B, B), F32)] * 2
     vmem = pl.BlockSpec(memory_space=pltpu.VMEM)
 
-    z0 = run(part(leaf_kernel, nb), [nb + 1], [leaf_order, leaf_inverse, basis_blocks, right_sides], two)
+    z0 = run(part(leaf_kernel, nb), [nb], [leaf_order, leaf_inverse, basis_blocks, right_sides])
     z1 = swapped(z0, "inner", 0)
     z2 = swapped(z0, "inner", 1)
     z3 = swapped(z2, "inner", 0)
-    ys = [
-        run(part(pair_kernel, nb), [(2 * B, (nb - 1) * B)], pair) for pair in ((z0, z1), (z2, z3))
-    ]
+    stack = (2 * B, (nb - 1) * B)
+    three = [pltpu.VMEM((3, B, B), F32)] * 2
+    y01, side = run(part(near_kernel, nb), [stack, nb], [z0, z1, z2], three)
+    ys = [y01, run(part(far_kernel, nb), [stack], [z2, z3, side], two)]
     place = lax.axis_index("inner").astype(jnp.int32)
     core = lax.axis_index("outer").astype(jnp.int32) & 1
-    mine, send, own = quad_call(run, levels, jnp.stack([place & 3, core]), [z0, z1, z2, z3], ys)
-    cut = cuts(nb)[0] * B
-    mine = jnp.concatenate([mine[:, :cut], mine[:, cut:] + swapped(send, "outer", 0)], axis=1)
+    mine, rest, send, own = quad_call(run, levels, jnp.stack([place & 3, core]), [z0, z1, z2, z3], ys)
     gathered = lax.all_gather(mine, "inner", tiled=True)
-    pay, y = ring_call(run, levels, jnp.stack([place >> 3, core]), gathered, own)
+    rest = rest + swapped(send, "outer", 0)
+    rest = rest + swapped(rest, "inner", 2)
+    rest = rest + swapped(rest, "inner", 3)
+    across = swapped(rest, "inner", 1)
+    rests = [rest, swapped(rest, "inner", 0), across, swapped(across, "inner", 0)]
+    side = jnp.stack([place >> 3, core, place & 3])
+    pay, y = ring_call(run, levels, side, gathered, rests, own)
     core = core.reshape(1)
     half = None
     for level in range(4, levels):
@@ -503,7 +517,7 @@
         y = run(update_kernel, [wide], [pay, found[1], y], (), [head, vmem, vmem], (1,))
         pay = found[0]
         half = found[2] if cut else None
-    return run(finish_kernel, [1], [leaf_order, leaf_inverse, pay, others[0], y])
+    return run(finish_kernel, [1], [leaf_order, leaf_inverse, pay, near(others[0]), y])
 
 
 def solution(mesh):

time: 306 us -> 292 us (0.954)
  the two profiles are of different devices: /device:TPU:2 before, /device:TPU:30 now
where the time goes in v4:
time: 292 us; the launch traced here: 291 us
  waiting for transfers between devices  137 us (47%)
  Pallas kernels  75.1 us (26%)
  starting transfers between devices  61.6 us (21%)
  between operations  13.6 us (5%)
    ppermute x16, waiting for transfers between devices, swapped(): return lax.ppermute(block, axis, [(k, k ^ 1 << bit) for k in range(count)])  106 us
    pallas_call x14, Pallas kernels, call(): pl.pallas_call(kernel, out_shape=shapes[0] if one else shapes, grid=grid,...  75.1 us
    ppermute x16, starting transfers between devices, swapped(): return lax.ppermute(block, axis, [(k, k ^ 1 << bit) for k in range(count)])  61.6 us
    all_gather x1, waiting for transfers between devices, body(): gathered = lax.all_gather(mine, 'inner', tiled=True)  31.3 us
  transfers between devices with their start and end apart: 17, of which 14 were waited for; matrix products, arithmetic and copies ran while one was open for 1% of the time, Pallas kernels for 6%

profile of v4, /device:TPU:30, one launch (start us, length us, event | category | flops | bytes accessed | tf_op | source)
XLA Modules:
  0.0 291.2 jit_solution(14686549948102636947)
XLA Ops:
  6.5 2.6 shard_map.46.z0.zs0
  9.1 5.2 %collective-permute-start.1 = (f32[128,1280]{1,0:T(8,128)}, f32[128,1280]{1,0:T(8,128)S(1)}, u32[]{:S(2)}, u32[]{:S(2)}) collective-permute-start(f32[128,1280]{1,0:T(8,128)} %shard_map.46.z0.zs0), channel_id=1, source_target_pairs={{0,2},{1,3},{2,0},{3,1},{4,6},{5,7},{6,4},{7,5},{8,10},{9,11},{10,... | collective-permute-start | bytes 1966088 | tf_op jit(solution)/shard_map/ppermute | solution.py:398
  14.3 3.8 %collective-permute-start = (f32[128,1280]{1,0:T(8,128)}, f32[128,1280]{1,0:T(8,128)S(1)}, u32[]{:S(2)}, u32[]{:S(2)}) collective-permute-start(f32[128,1280]{1,0:T(8,128)} %shard_map.46.z0.zs0), channel_id=1, source_target_pairs={{0,1},{1,0},{2,3},{3,2},{4,5},{5,4},{6,7},{7,6},{8,9},{9,8},{10,11... | collective-permute-start | bytes 1966088 | tf_op jit(solution)/shard_map/ppermute | solution.py:398
  18.1 25.2 %collective-permute-done.1.z2.zs2 = f32[128,1280]{1,0:T(8,128)S(1)} collective-permute-done((f32[128,1280]{1,0:T(8,128)}, f32[128,1280]{1,0:T(8,128)S(1)}, u32[]{:S(2)}, u32[]{:S(2)}) %collective-permute-start.1) | collective-permute-done | bytes 655392 | tf_op jit(solution)/shard_map/ppermute | solution.py:398
  43.4 2.7 collective-permute-start.2
  47.5 8.7 %shard_map.47 = (f32[256,1152]{1,0:T(8,128)}, f32[128,1280]{1,0:T(8,128)}) custom-call(f32[128,1280]{1,0:T(8,128)} %shard_map.46.z0.zs0, f32[128,1280]{1,0:T(8,128)} %copy-done.1, f32[128,1280]{1,0:T(8,128)} %copy-done), custom_call_target="tpu_custom_call" | custom-call | tf_op jit(solution)/shard_map/pallas_call | solution.py:385
  56.2 4.9 %collective-permute-done.2.z3.zs3 = f32[128,1280]{1,0:T(8,128)S(1)} collective-permute-done((f32[128,1280]{1,0:T(8,128)S(1)}, f32[128,1280]{1,0:T(8,128)S(1)}, u32[]{:S(2)}, u32[]{:S(2)}) %collective-permute-start.2) | collective-permute-done | bytes 655392 | tf_op jit(solution)/shard_map/ppermute | solution.py:398
  61.9 6.6 %shard_map.48.y23 = f32[256,1152]{1,0:T(8,128)} custom-call(f32[128,1280]{1,0:T(8,128)} %copy-done, f32[128,1280]{1,0:T(8,128)} %copy-done.2, f32[128,1280]{1,0:T(8,128)} %get-tuple-element.24.side_ref), custom_call_target="tpu_custom_call" | custom-call | tf_op jit(solution)/shard_map/pallas_call | solution.py:385
  68.5 13.0 %shard_map.49 = (f32[32,2688]{1,0:T(8,128)}, f32[32,896]{1,0:T(8,128)}, f32[32,896]{1,0:T(8,128)}, f32[128,1024]{1,0:T(8,128)}) custom-call(s32[2]{0:T(128)} %pad_add_fusion.1.place_ref, f32[128,1280]{1,0:T(8,128)} %shard_map.46.z0.zs0, f32[128,1280]{1,0:T(8,128)} %copy-done.1, f32[128,1280]{1,0:T(8,128)} %copy-done, f32[128,1280]{1,0:T(8,128)} %copy-done.2, ...), custom_call_target="tpu_custom_call" | custom-call | tf_op jit(solution)/shard_map/pallas_call | solution.py:385
  85.9 9.1 %collective-permute-start.4 = (f32[32,896]{1,0:T(8,128)S(1)}, f32[32,896]{1,0:T(8,128)S(1)}, u32[]{:S(2)}, u32[]{:S(2)}) collective-permute-start(f32[32,896]{1,0:T(8,128)S(1)} %add.9), channel_id=1, source_target_pairs={{0,4},{1,5},{2,6},{3,7},{4,0},{5,1},{6,2},{7,3},{8,12},{9,13},{10,... | collective-permute-start | bytes 344072 | tf_op jit(solution)/shard_map/ppermute | solution.py:398
  95.0 10.9 %collective-permute-done.4 = f32[32,896]{1,0:T(8,128)S(1)} collective-permute-done((f32[32,896]{1,0:T(8,128)S(1)}, f32[32,896]{1,0:T(8,128)S(1)}, u32[]{:S(2)}, u32[]{:S(2)}) %collective-permute-start.4) | collective-permute-done | bytes 114720 | tf_op jit(solution)/shard_map/ppermute | solution.py:398
  106.0 15.9 %collective-permute-start.5 = (f32[32,896]{1,0:T(8,128)S(1)}, f32[32,896]{1,0:T(8,128)S(1)}, u32[]{:S(2)}, u32[]{:S(2)}) collective-permute-start(f32[32,896]{1,0:T(8,128)S(1)} %add.10), channel_id=1, source_target_pairs={{0,8},{1,9},{2,10},{3,11},{4,12},{5,13},{6,14},{7,15},{8,0},{9,1},... | collective-permute-start | bytes 344072 | tf_op jit(solution)/shard_map/ppermute | solution.py:398
  121.9 13.0 %collective-permute-done.5 = f32[32,896]{1,0:T(8,128)S(1)} collective-permute-done((f32[32,896]{1,0:T(8,128)S(1)}, f32[32,896]{1,0:T(8,128)S(1)}, u32[]{:S(2)}, u32[]{:S(2)}) %collective-permute-start.5) | collective-permute-done | bytes 114720 | tf_op jit(solution)/shard_map/ppermute | solution.py:398
  138.7 6.5 %collective-permute-done.7.rest2 = f32[32,896]{1,0:T(8,128)S(1)} collective-permute-done((f32[32,896]{1,0:T(8,128)S(1)}, f32[32,896]{1,0:T(8,128)S(1)}, u32[]{:S(2)}, u32[]{:S(2)}) %collective-permute-start.7) | collective-permute-done | bytes 114720 | tf_op jit(solution)/shard_map/ppermute | solution.py:398
  147.9 6.9 %collective-permute-done.8.rest3 = f32[32,896]{1,0:T(8,128)S(1)} collective-permute-done((f32[32,896]{1,0:T(8,128)S(1)}, f32[32,896]{1,0:T(8,128)S(1)}, u32[]{:S(2)}, u32[]{:S(2)}) %collective-permute-start.8) | collective-permute-done | bytes 114720 | tf_op jit(solution)/shard_map/ppermute | solution.py:398
  154.8 31.3 %all-gather.2.cloned.1.call-done.all_ref = f32[512,2688]{1,0:T(8,128)} async-done(((f32[32,2688]{1,0:T(8,128)}), f32[512,2688]{1,0:T(8,128)}) %all-gather.2.cloned.1.call-update) | async-done | bytes 5505040 | tf_op jit(solution)/shard_map/all_gather | solution.py:494
  186.1 13.1 %shard_map.50 = (f32[128,2560]{1,0:T(8,128)}, f32[128,768]{1,0:T(8,128)}) custom-call(s32[3]{0:T(128)} %pad_add_fusion.side_ref, f32[512,2688]{1,0:T(8,128)} %all-gather.2.cloned.1.call-done.all_ref, f32[32,896]{1,0:T(8,128)} %copy-done.3, f32[32,896]{1,0:T(8,128)} %copy-done.5, f32[32,896]{1,0:T(8,128)} %copy-done.4, f32[32,896]{1,0:T(8,128)} %copy-done.6, ...), custom_call_target="tpu_custom_call" | custom-call | tf_op jit(solution)/shard_map/pallas_call | solution.py:385
  201.1 3.2 %collective-permute-done.9.refs_0_ = f32[128,2560]{1,0:T(8,128)S(1)} collective-permute-done((f32[128,2560]{1,0:T(8,128)}, f32[128,2560]{1,0:T(8,128)S(1)}, u32[]{:S(2)}, u32[]{:S(2)}) %collective-permute-start.9) | collective-permute-done | bytes 1310752 | tf_op jit(solution)/shard_map/ppermute | solution.py:398
  204.3 5.4 %shard_map.51 = (f32[128,1792]{1,0:T(8,128)}, f32[128,640]{1,0:T(8,128)}, f32[128,896]{1,0:T(8,128)}) custom-call(s32[1]{0:T(128)} %bitcast.core_ref, f32[128,2560]{1,0:T(8,128)} %get-tuple-element.29.own_ref.pay_ref, f32[128,2560]{1,0:T(8,128)S(1)} %collective-permute-done.9.refs_0_, f32[128,768]{1,0:T(8,128)} %get-tuple-element.30.refs_1_.y_ref), custom_call_target="tpu_custom_call" | custom-call | tf_op jit(solution)/shard_map/pallas_call | solution.py:385
  209.8 2.7 collective-permute-start.10
  212.5 11.9 %collective-permute-done.10.refs_0_ = f32[128,896]{1,0:T(8,128)S(1)} collective-permute-done((f32[128,896]{1,0:T(8,128)}, f32[128,896]{1,0:T(8,128)S(1)}, u32[]{:S(2)}, u32[]{:S(2)}) %collective-permute-start.10) | collective-permute-done | bytes 458784 | tf_op jit(solution)/shard_map/ppermute | solution.py:398
  226.6 2.4 shard_map.52.refs_2_.y_ref
  229.0 5.0 %shard_map.53 = (f32[128,1152]{1,0:T(8,128)}, f32[128,512]{1,0:T(8,128)}, f32[128,640]{1,0:T(8,128)}) custom-call(s32[1]{0:T(128)} %bitcast.core_ref, f32[128,1792]{1,0:T(8,128)} %get-tuple-element.31.own_ref.pay_ref, f32[128,896]{1,0:T(8,128)S(1)} %collective-permute-done.10.refs_0_, f32[128,896]{1,0:T(8,128)S(1)} %collective-permute-done.11.refs_1_, ...), custom_call_target="tpu_custom_call" | custom-call | tf_op jit(solution)/shard_map/pallas_call | solution.py:385
  234.0 3.3 %collective-permute-start.12 = (f32[128,640]{1,0:T(8,128)}, f32[128,640]{1,0:T(8,128)S(1)}, u32[]{:S(2)}, u32[]{:S(2)}) collective-permute-start(f32[128,640]{1,0:T(8,128)} %get-tuple-element.35), channel_id=1, source_target_pairs={{0,64},{16,80},{32,96},{48,112},{64,0},{80,16},{96,32},{112,48},{1... | collective-permute-start | bytes 983048 | tf_op jit(solution)/shard_map/ppermute | solution.py:398
  237.3 10.4 %collective-permute-done.12.refs_0_ = f32[128,640]{1,0:T(8,128)S(1)} collective-permute-done((f32[128,640]{1,0:T(8,128)}, f32[128,640]{1,0:T(8,128)S(1)}, u32[]{:S(2)}, u32[]{:S(2)}) %collective-permute-start.12) | collective-permute-done | bytes 327712 | tf_op jit(solution)/shard_map/ppermute | solution.py:398
  252.0 4.4 %shard_map.55 = (f32[128,640]{1,0:T(8,128)}, f32[128,384]{1,0:T(8,128)}) custom-call(s32[1]{0:T(128)} %bitcast.core_ref, f32[128,1152]{1,0:T(8,128)} %get-tuple-element.34.own_ref.pay_ref, f32[128,640]{1,0:T(8,128)S(1)} %collective-permute-done.12.refs_0_, f32[128,640]{1,0:T(8,128)S(1)} %collective-permute-done.13.refs_1_, f32[128,512]{1,0:T(8,128)} %shard_map.54.refs_2_.y_ref), custom_call_target="tpu_custom_call" | custom-call | tf_op jit(solution)/shard_map/pallas_call | solution.py:385
  256.4 2.5 collective-permute-start.14
  261.1 7.5 %collective-permute-done.14.refs_0_ = f32[128,640]{1,0:T(8,128)S(1)} collective-permute-done((f32[128,640]{1,0:T(8,128)}, f32[128,640]{1,0:T(8,128)S(1)}, u32[]{:S(2)}, u32[]{:S(2)}) %collective-permute-start.14) | collective-permute-done | bytes 327712 | tf_op jit(solution)/shard_map/ppermute | solution.py:398
  268.6 4.0 %shard_map.57 = (f32[128,256]{1,0:T(8,128)}, f32[128,256]{1,0:T(8,128)}) custom-call(s32[1]{0:T(128)} %bitcast.core_ref, f32[128,640]{1,0:T(8,128)} %get-tuple-element.37.own_ref.pay_ref, f32[128,640]{1,0:T(8,128)S(1)} %collective-permute-done.14.refs_0_, f32[128,384]{1,0:T(8,128)} %shard_map.56.refs_1_.y_ref), custom_call_target="tpu_custom_call" | custom-call | tf_op jit(solution)/shard_map/pallas_call | solution.py:385
  272.5 2.8 collective-permute-start.15
  277.5 3.7 %collective-permute-done.15.other_ref = f32[128,256]{1,0:T(8,128)S(1)} collective-permute-done((f32[128,256]{1,0:T(8,128)}, f32[128,256]{1,0:T(8,128)S(1)}, u32[]{:S(2)}, u32[]{:S(2)}) %collective-permute-start.15) | collective-permute-done | bytes 131104 | tf_op jit(solution)/shard_map/ppermute | solution.py:398
  281.2 3.2 %shard_map.59 = f32[128,128]{1,0:T(8,128)} custom-call(s32[1,128]{1,0:T(1,128)} %order_ref.3, f32[128,128]{1,0:T(8,128)} %r_ref.3, f32[128,256]{1,0:T(8,128)} %get-tuple-element.39.own_ref, f32[128,256]{1,0:T(8,128)S(1)} %collective-permute-done.15.other_ref, f32[128,256]{1,0:T(8,128)} %shard_map.58.y_ref), custom_call_target="tpu_custom_call" | custom-call | tf_op jit(solution)/shard_map/pallas_call | solution.py:385
  (36 shorter events, 25.9 us)
Async XLA Ops:
  6.5 179.6 %all-gather.2.cloned.1.call-start = ((), (), s32[]{:S(2)}) async-start(), calls=%async_computation | async-start | bytes 5849088 | tf_op jit(solution)/shard_map/all_gather | solution.py:494
  9.1 34.2 %collective-permute-start.1 = (f32[128,1280]{1,0:T(8,128)}, f32[128,1280]{1,0:T(8,128)S(1)}, u32[]{:S(2)}, u32[]{:S(2)}) collective-permute-start(f32[128,1280]{1,0:T(8,128)} %shard_map.46.z0.zs0), channel_id=1, source_target_pairs={{0,2},{1,3},{2,0},{3,1},{4,6},{5,7},{6,4},{7,5},{8,10},{9,11},{10,... | collective-permute-start | bytes 1966088 | tf_op jit(solution)/shard_map/ppermute | solution.py:398
  14.3 32.3 %collective-permute-start = (f32[128,1280]{1,0:T(8,128)}, f32[128,1280]{1,0:T(8,128)S(1)}, u32[]{:S(2)}, u32[]{:S(2)}) collective-permute-start(f32[128,1280]{1,0:T(8,128)} %shard_map.46.z0.zs0), channel_id=1, source_target_pairs={{0,1},{1,0},{2,3},{3,2},{4,5},{5,4},{6,7},{7,6},{8,9},{9,8},{10,11... | collective-permute-start | bytes 1966088 | tf_op jit(solution)/shard_map/ppermute | solution.py:398
  43.4 3.3 %copy-start = (f32[128,1280]{1,0:T(8,128)}, f32[128,1280]{1,0:T(8,128)S(1)}, u32[]{:S(2)}) copy-start(f32[128,1280]{1,0:T(8,128)S(1)} %collective-permute-done.1.z2.zs2) | copy-start | bytes 1966084
  43.4 17.7 %collective-permute-start.2 = (f32[128,1280]{1,0:T(8,128)S(1)}, f32[128,1280]{1,0:T(8,128)S(1)}, u32[]{:S(2)}, u32[]{:S(2)}) collective-permute-start(f32[128,1280]{1,0:T(8,128)S(1)} %collective-permute-done.1.z2.zs2), channel_id=1, source_target_pairs={{0,1},{1,0},{2,3},{3,2},{4,5},{5,4},{6,7},{7,6},{8,9},{9,8},{10,11... | collective-permute-start | bytes 1966088 | tf_op jit(solution)/shard_map/ppermute | solution.py:398
  46.7 0.9 copy-start.1
  61.1 0.8 copy-start.2
  81.6 3.4 %collective-permute-start.3 = (f32[32,896]{1,0:T(8,128)}, f32[32,896]{1,0:T(8,128)S(1)}, u32[]{:S(2)}, u32[]{:S(2)}) collective-permute-start(f32[32,896]{1,0:T(8,128)} %get-tuple-element.27), channel_id=1, source_target_pairs={{0,16},{16,0},{32,48},{48,32},{64,80},{80,64},{96,112},{112,96},{1... | collective-permute-start | bytes 344072 | tf_op jit(solution)/shard_map/ppermute | solution.py:398
  85.9 20.0 %collective-permute-start.4 = (f32[32,896]{1,0:T(8,128)S(1)}, f32[32,896]{1,0:T(8,128)S(1)}, u32[]{:S(2)}, u32[]{:S(2)}) collective-permute-start(f32[32,896]{1,0:T(8,128)S(1)} %add.9), channel_id=1, source_target_pairs={{0,4},{1,5},{2,6},{3,7},{4,0},{5,1},{6,2},{7,3},{8,12},{9,13},{10,... | collective-permute-start | bytes 344072 | tf_op jit(solution)/shard_map/ppermute | solution.py:398
  106.0 28.9 %collective-permute-start.5 = (f32[32,896]{1,0:T(8,128)S(1)}, f32[32,896]{1,0:T(8,128)S(1)}, u32[]{:S(2)}, u32[]{:S(2)}) collective-permute-start(f32[32,896]{1,0:T(8,128)S(1)} %add.10), channel_id=1, source_target_pairs={{0,8},{1,9},{2,10},{3,11},{4,12},{5,13},{6,14},{7,15},{8,0},{9,1},... | collective-permute-start | bytes 344072 | tf_op jit(solution)/shard_map/ppermute | solution.py:398
  134.9 51.2 %copy-start.3 = (f32[32,896]{1,0:T(8,128)}, f32[32,896]{1,0:T(8,128)S(1)}, u32[]{:S(2)}) copy-start(f32[32,896]{1,0:T(8,128)S(1)} %add.11.rest0) | copy-start | bytes 344068
  134.9 10.4 %collective-permute-start.7 = (f32[32,896]{1,0:T(8,128)S(1)}, f32[32,896]{1,0:T(8,128)S(1)}, u32[]{:S(2)}, u32[]{:S(2)}) collective-permute-start(f32[32,896]{1,0:T(8,128)S(1)} %add.11.rest0), channel_id=1, source_target_pairs={{0,2},{1,3},{2,0},{3,1},{4,6},{5,7},{6,4},{7,5},{8,10},{9,11},{10,... | collective-permute-start | bytes 344072 | tf_op jit(solution)/shard_map/ppermute | solution.py:398
  136.8 11.1 %collective-permute-start.6 = (f32[32,896]{1,0:T(8,128)S(1)}, f32[32,896]{1,0:T(8,128)S(1)}, u32[]{:S(2)}, u32[]{:S(2)}) collective-permute-start(f32[32,896]{1,0:T(8,128)S(1)} %add.11.rest0), channel_id=1, source_target_pairs={{0,1},{1,0},{2,3},{3,2},{4,5},{5,4},{6,7},{7,6},{8,9},{9,8},{10,11... | collective-permute-start | bytes 344072 | tf_op jit(solution)/shard_map/ppermute | solution.py:398
  145.2 40.8 %copy-start.4 = (f32[32,896]{1,0:T(8,128)}, f32[32,896]{1,0:T(8,128)S(1)}, u32[]{:S(2)}) copy-start(f32[32,896]{1,0:T(8,128)S(1)} %collective-permute-done.7.rest2) | copy-start | bytes 344068
  145.2 9.5 %collective-permute-start.8 = (f32[32,896]{1,0:T(8,128)S(1)}, f32[32,896]{1,0:T(8,128)S(1)}, u32[]{:S(2)}, u32[]{:S(2)}) collective-permute-start(f32[32,896]{1,0:T(8,128)S(1)} %collective-permute-done.7.rest2), channel_id=1, source_target_pairs={{0,1},{1,0},{2,3},{3,2},{4,5},{5,4},{6,7},{7,6},{8,9},{9,8},{10,11... | collective-permute-start | bytes 344072 | tf_op jit(solution)/shard_map/ppermute | solution.py:398
  147.9 38.2 %copy-start.5 = (f32[32,896]{1,0:T(8,128)}, f32[32,896]{1,0:T(8,128)S(1)}, u32[]{:S(2)}) copy-start(f32[32,896]{1,0:T(8,128)S(1)} %collective-permute-done.6.rest1) | copy-start | bytes 344068
  154.8 31.3 %copy-start.6 = (f32[32,896]{1,0:T(8,128)}, f32[32,896]{1,0:T(8,128)S(1)}, u32[]{:S(2)}) copy-start(f32[32,896]{1,0:T(8,128)S(1)} %collective-permute-done.8.rest3) | copy-start | bytes 344068
  199.2 5.1 %collective-permute-start.9 = (f32[128,2560]{1,0:T(8,128)}, f32[128,2560]{1,0:T(8,128)S(1)}, u32[]{:S(2)}, u32[]{:S(2)}) collective-permute-start(f32[128,2560]{1,0:T(8,128)} %get-tuple-element.29.own_ref.pay_ref), channel_id=1, source_target_pairs={{0,16},{16,0},{32,48},{48,32},{64,80},{80,64},{96,112},{112,96},{1... | collective-permute-start | bytes 3932168 | tf_op jit(solution)/shard_map/ppermute | solution.py:398
  209.8 14.7 %collective-permute-start.10 = (f32[128,896]{1,0:T(8,128)}, f32[128,896]{1,0:T(8,128)S(1)}, u32[]{:S(2)}, u32[]{:S(2)}) collective-permute-start(f32[128,896]{1,0:T(8,128)} %get-tuple-element.32), channel_id=1, source_target_pairs={{0,32},{16,48},{32,0},{48,16},{64,96},{80,112},{96,64},{112,80},{1... | collective-permute-start | bytes 1376264 | tf_op jit(solution)/shard_map/ppermute | solution.py:398
  224.4 4.6 %collective-permute-start.11 = (f32[128,896]{1,0:T(8,128)S(1)}, f32[128,896]{1,0:T(8,128)S(1)}, u32[]{:S(2)}, u32[]{:S(2)}) collective-permute-start(f32[128,896]{1,0:T(8,128)S(1)} %collective-permute-done.10.refs_0_), channel_id=1, source_target_pairs={{0,16},{16,0},{32,48},{48,32},{64,80},{80,64},{96,112},{112,96},{1... | collective-permute-start | bytes 1376264 | tf_op jit(solution)/shard_map/ppermute | solution.py:398
  234.0 13.7 %collective-permute-start.12 = (f32[128,640]{1,0:T(8,128)}, f32[128,640]{1,0:T(8,128)S(1)}, u32[]{:S(2)}, u32[]{:S(2)}) collective-permute-start(f32[128,640]{1,0:T(8,128)} %get-tuple-element.35), channel_id=1, source_target_pairs={{0,64},{16,80},{32,96},{48,112},{64,0},{80,16},{96,32},{112,48},{1... | collective-permute-start | bytes 983048 | tf_op jit(solution)/shard_map/ppermute | solution.py:398
  247.7 4.3 %collective-permute-start.13 = (f32[128,640]{1,0:T(8,128)S(1)}, f32[128,640]{1,0:T(8,128)S(1)}, u32[]{:S(2)}, u32[]{:S(2)}) collective-permute-start(f32[128,640]{1,0:T(8,128)S(1)} %collective-permute-done.12.refs_0_), channel_id=1, source_target_pairs={{0,16},{16,0},{32,48},{48,32},{64,80},{80,64},{96,112},{112,96},{1... | collective-permute-start | bytes 983048 | tf_op jit(solution)/shard_map/ppermute | solution.py:398
  256.4 12.2 %collective-permute-start.14 = (f32[128,640]{1,0:T(8,128)}, f32[128,640]{1,0:T(8,128)S(1)}, u32[]{:S(2)}, u32[]{:S(2)}) collective-permute-start(f32[128,640]{1,0:T(8,128)} %get-tuple-element.37.own_ref.pay_ref), channel_id=1, source_target_pairs={{0,128},{16,144},{32,160},{48,176},{64,192},{80,208},{96,224},{112... | collective-permute-start | bytes 983048 | tf_op jit(solution)/shard_map/ppermute | solution.py:398
  272.5 8.6 %collective-permute-start.15 = (f32[128,256]{1,0:T(8,128)}, f32[128,256]{1,0:T(8,128)S(1)}, u32[]{:S(2)}, u32[]{:S(2)}) collective-permute-start(f32[128,256]{1,0:T(8,128)} %get-tuple-element.39.own_ref), channel_id=1, source_target_pairs={{0,256},{16,272},{32,288},{48,304},{64,320},{80,336},{96,352},{112... | collective-permute-start | bytes 393224 | tf_op jit(solution)/shard_map/ppermute | solution.py:398
Sparse Core Ops, SparseCore 0:
  81.7 104.3 all-gather.1

commit v5 on v3

--- a/solution.py
+++ b/solution.py
@@ -95,9 +95,9 @@
     return found
 
 
-def pair_inverse(s_sum):
+def pair_inverse(s_first, s_second):
     unit = eye()
-    r = 0.5 * (s_sum - unit)
+    r = 0.5 * (s_first + s_second - unit)
     t = 7.0
     x = (0.5 * (1.0 + 1.0 / t)) * (unit + r)
     r = (1.0 + 1.0 / t) * mm(r, r) - (1.0 / t) * unit
@@ -110,28 +110,36 @@
     return x
 
 
-def leaf_kernel(nb, order_ref, r_ref, u_ref, rhs_ref, z_ref, x_scr, r_scr):
+def leaf_kernel(nb, order_ref, r_ref, u_ref, rhs_ref, z_ref):
     pick = (lax.broadcasted_iota(jnp.int32, (B, B), 0) == order_ref[...]).astype(F32)
     r = r_ref[...]
     for b in range(nb - 1):
         z_ref[:, sl(b, b + 1)] = mm(r, u_ref[b])
     z_ref[:, sl(nb - 1, nb)] = mm(r, exact_tn(pick, rhs_ref[...]))
-    z0 = z_ref[:, sl(0, 1)]
-    (s,) = unit_inverse([tn(z0, z0)], x_scr, r_scr)
-    z_ref[:, sl(nb, nb + 1)] = s
-
-
-def pair_kernel(nb, first_ref, second_ref, y_ref):
-    refs = (first_ref, second_ref)
-    n = [
-        exact(z[:, sl(nb, nb + 1)], tn(z[:, sl(0, 1)], z[:, sl(1, nb)]))
-        for z in refs
-    ]
-    t = pair_inverse(first_ref[:, sl(nb, nb + 1)] + second_ref[:, sl(nb, nb + 1)])
-    x = mm(t, n[0] + n[1])
+
+
+def pair_level(nb, refs, s, n, y_ref):
+    x = mm(pair_inverse(s[0], s[1]), n[0] + n[1])
     for i, z in enumerate(refs):
-        weights = n[i] + mm(z[:, sl(nb, nb + 1)], x)
+        weights = n[i] + mm(s[i], x)
         y_ref[sl(i, i + 1), :] = z[:, sl(1, nb)] - mm(z[:, sl(0, 1)], weights)
+
+
+def near_kernel(nb, z0, z1, z2, y_ref, side_ref, x_scr, r_scr):
+    refs = (z0, z1, z2)
+    p = [tn(z[:, :B], z[...]) for z in refs]
+    s = unit_inverse([a[:, :B] for a in p], x_scr, r_scr)
+    n = [exact(s[i], p[i][:, B:]) for i in range(3)]
+    side_ref[:, :B] = s[2]
+    side_ref[:, B:] = n[2]
+    pair_level(nb, refs[:2], s, n, y_ref)
+
+
+def far_kernel(nb, z2, z3, side_ref, y_ref, x_scr, r_scr):
+    p = tn(z3[:, :B], z3[...])
+    (s,) = unit_inverse([p[:, :B]], x_scr, r_scr)
+    n = exact(s, p[:, B:])
+    pair_level(nb, (z2, z3), (side_ref[:, :B], s), (side_ref[:, B:], n), y_ref)
 
 
 def quad_kernel(
@@ -157,7 +165,7 @@
     m = [tn(z[rows[n], sl(1, 2)], y[rows[n], sl(1, nb)]) for n in range(2)]
     s = unit_inverse([m[n][:, :B] for n in range(2)], x_scr, r_scr)
     nn = [mm(s[n], m[n][:, B:]) for n in range(2)]
-    x = mm(pair_inverse(s[0] + s[1]), nn[0] + nn[1])
+    x = mm(pair_inverse(s[0], s[1]), nn[0] + nn[1])
     last = nb - 1
     for n in range(2):
         weights = nn[n] + mm(s[n], x)
@@ -215,27 +223,22 @@
     return 1 + 2 * (nb - 3) + nb - 4, rest // 2
 
 
-def ring_kernel(
-    nb, side_ref, all_ref, own_ref, pay_ref, out_ref,
-    act_ref, pas_ref, la, lb, m, nn, tot, x_scr, r_scr, s_scr, sem,
-):
+def ring_kernel(nb, side_ref, *refs):
+    parts, refs = refs[:16], refs[16:]
+    own_ref, pay_ref, out_ref, act_ref, pas_ref, la, lb, m, nn, tot, x_scr, r_scr, s_scr = refs
     wide = nb - 3
     deep = nb - 4
     active = 1 + 2 * wide
-    copies = [
-        pltpu.make_async_copy(all_ref.at[:, pl.ds(0, active * B)], act_ref, sem.at[0]),
-        pltpu.make_async_copy(
-            all_ref.at[:, pl.ds(active * B, pas_ref.shape[1])], pas_ref, sem.at[1]
-        ),
-    ]
-    for copy in copies:
-        copy.start()
-    copies[0].wait()
+    for away, share in enumerate(parts):
+        at = (side_ref[2] + away) & 15
+        rows = pl.ds(pl.multiple_of(at * SHARE, SHARE), SHARE)
+        act_ref[rows, :] = share[:, : active * B]
+        pas_ref[rows, :] = share[:, active * B :]
 
     for node in range(2):
         rows = sl(node, node + 1)
         q = act_ref[rows, sl(1, 1 + wide)]
-        x = mm(pair_inverse(act_ref[rows, :B]), q)
+        x = mm(pair_inverse(act_ref[rows, :B], 0.0), q)
         m[node] = x
         lb[rows, :] = x[:, B:]
         la[rows, :] = q[:, B:]
@@ -246,10 +249,9 @@
         la[sl(2 + node, 3 + node), :] = nn[node, :, B:]
         lb[sl(2 + node, 3 + node), :] = mm(s[node], nn[node, :, B:])
     q3 = lb[sl(2, 3), :] + lb[sl(3, 4), :]
-    x3 = mm(pair_inverse(s[0] + s[1]), q3)
+    x3 = mm(pair_inverse(s[0], s[1]), q3)
     la[sl(4, 5), :] = q3
     lb[sl(4, 5), :] = x3
-    copies[1].wait()
     half = cuts(nb)[1]
     tot[...] = jnp.zeros_like(tot)
 
@@ -311,7 +313,7 @@
     x_scr, r_scr = refs[-2:]
     wide = nb - 1 - level
     q = own_ref[:, sl(1, 1 + wide)] + other(1, 1 + wide)
-    x = mm(pair_inverse(own_ref[:, :B] + other(0, 1)), q)
+    x = mm(pair_inverse(own_ref[:, :B], other(0, 1)), q)
     x_ref[...] = x
 
     def panel(a):
@@ -359,7 +361,7 @@
 def finish_kernel(order_ref, r_ref, own_ref, other_ref, y_ref, out_ref):
     s = own_ref[:, :B]
     n = own_ref[:, B:]
-    x = mm(pair_inverse(s + other_ref[:, :B]), n + other_ref[:, B:])
+    x = mm(pair_inverse(s, other_ref[:, :B]), n + other_ref[:, B:])
     y = y_ref[:, B:] - mm(y_ref[:, :B], n + mm(s, x))
     pick = (lax.broadcasted_iota(jnp.int32, (B, B), 0) == order_ref[...]).astype(F32)
     out_ref[...] = exact(pick, tn(r_ref[...], y))
@@ -391,18 +393,17 @@
     return 1 + (levels - level) + sum(levels + 1 - a for a in range(level + 1, levels))
 
 
-def ring_call(run, levels, side, gathered, own):
+def ring_call(run, levels, side, parts, own):
     nb = levels + 1
     head, half = cuts(nb)
     active = 2 * levels - 3
     two = [pltpu.VMEM((2, B, B), F32)] * 2
     smem = pl.BlockSpec(memory_space=pltpu.SMEM)
     vmem = pl.BlockSpec(memory_space=pltpu.VMEM)
-    anywhere = pl.BlockSpec(memory_space=pl.ANY)
     return run(
         functools.partial(ring_kernel, nb),
         [pay_width(levels, 4), nb - 4],
-        [side, gathered, own],
+        [side, *parts, own],
         [
             pltpu.VMEM((2 * B, active * B), F32),
             pltpu.VMEM((2 * B, (head + half - active) * B), F32),
@@ -413,9 +414,8 @@
             pltpu.VMEM((B, (nb - 4 + 2 * half) * B), F32),
             *two,
             pltpu.VMEM((2, B, B), F32),
-            pltpu.SemaphoreType.DMA((2,)),
         ],
-        [smem, anywhere, vmem],
+        [smem] + [vmem] * 17,
     )
 
 
@@ -468,28 +468,36 @@
     two = [pltpu.VMEM((2, B, B), F32)] * 2
     vmem = pl.BlockSpec(memory_space=pltpu.VMEM)
 
-    z0 = run(part(leaf_kernel, nb), [nb + 1], [leaf_order, leaf_inverse, basis_blocks, right_sides], two)
+    z0 = run(part(leaf_kernel, nb), [nb], [leaf_order, leaf_inverse, basis_blocks, right_sides])
     z1 = swapped(z0, "inner", 0)
     z2 = swapped(z0, "inner", 1)
     z3 = swapped(z2, "inner", 0)
-    ys = [
-        run(part(pair_kernel, nb), [(2 * B, (nb - 1) * B)], pair) for pair in ((z0, z1), (z2, z3))
-    ]
+    stack = (2 * B, (nb - 1) * B)
+    three = [pltpu.VMEM((3, B, B), F32)] * 2
+    y01, side = run(part(near_kernel, nb), [stack, nb], [z0, z1, z2], three)
+    ys = [y01, run(part(far_kernel, nb), [stack], [z2, z3, side], two)]
     place = lax.axis_index("inner").astype(jnp.int32)
     core = lax.axis_index("outer").astype(jnp.int32) & 1
     mine, send, own = quad_call(run, levels, jnp.stack([place & 3, core]), [z0, z1, z2, z3], ys)
-    cut = cuts(nb)[0] * B
     half = (SHARE, mine.shape[1])
     keep, give = run(
-        part(halve_kernel, cut),
+        part(halve_kernel, cuts(nb)[0] * B),
         [half, half],
         [(place >> 2 & 1).reshape(1), mine, near(swapped(send, "outer", 0))],
         (),
         [pl.BlockSpec(memory_space=pltpu.SMEM)] + [pl.BlockSpec(memory_space=pltpu.VMEM)] * 2,
     )
     mine = keep + swapped(give, "inner", 2)
-    gathered = lax.all_gather(mine, "inner", tiled=True)
-    pay, y = ring_call(run, levels, jnp.stack([place >> 3, core]), gathered, own)
+    parts = [mine] + [None] * 15
+    up = down = mine
+    for step in range(1, 9):
+        up = lax.ppermute(up, "inner", [(k, (k + 1) % 16) for k in range(16)])
+        parts[16 - step] = up
+        if step < 8:
+            down = lax.ppermute(down, "inner", [(k, (k - 1) % 16) for k in range(16)])
+            parts[step] = down
+    side = jnp.stack([place >> 3, core, place])
+    pay, y = ring_call(run, levels, side, parts, own)
     core = core.reshape(1)
     half = None
     for level in range(4, levels):

time: 308 us -> 291 us (0.945)
  the two profiles are of different devices: /device:TPU:8 before, /device:TPU:22 now
where the time goes in v5:
time: 291 us; the launch traced here: 290 us
  waiting for transfers between devices  114 us (39%)
  starting transfers between devices  95.4 us (33%)
  Pallas kernels  76.1 us (26%)
    ppermute x12, waiting for transfers between devices, swapped(): return lax.ppermute(block, axis, [(k, k ^ 1 << bit) for k in range(count)])  89 us
    pallas_call x15, Pallas kernels, call(): pl.pallas_call(kernel, out_shape=shapes[0] if one else shapes, grid=grid,...  76.1 us
    ppermute x7, starting transfers between devices, body(): down = lax.ppermute(down, 'inner', [(k, (k - 1) % 16) for k in range(16)])  40.3 us
    ppermute x12, starting transfers between devices, swapped(): return lax.ppermute(block, axis, [(k, k ^ 1 << bit) for k in range(count)])  39.8 us
    ppermute x8, waiting for transfers between devices, body(): up = lax.ppermute(up, 'inner', [(k, (k + 1) % 16) for k in range(16)])  24.7 us
    ppermute x8, starting transfers between devices, body(): up = lax.ppermute(up, 'inner', [(k, (k + 1) % 16) for k in range(16)])  15.3 us
  transfers between devices with their start and end apart: 27, of which 17 were waited for; matrix products, arithmetic and copies ran while one was open for 0% of the time, Pallas kernels for 6%

profile of v5, /device:TPU:22, one launch (start us, length us, event | category | flops | bytes accessed | tf_op | source)
XLA Modules:
  0.0 289.7 jit_solution(3656127809794236338)
XLA Ops:
  2.6 5.2 %collective-permute-start.1 = (f32[128,1280]{1,0:T(8,128)}, f32[128,1280]{1,0:T(8,128)S(1)}, u32[]{:S(2)}, u32[]{:S(2)}) collective-permute-start(f32[128,1280]{1,0:T(8,128)} %shard_map.46.z0.zs0), channel_id=1, source_target_pairs={{0,2},{1,3},{2,0},{3,1},{4,6},{5,7},{6,4},{7,5},{8,10},{9,11},{10,... | collective-permute-start | bytes 1966088 | tf_op jit(solution)/shard_map/ppermute | solution.py:389
  7.8 3.8 %collective-permute-start = (f32[128,1280]{1,0:T(8,128)}, f32[128,1280]{1,0:T(8,128)S(1)}, u32[]{:S(2)}, u32[]{:S(2)}) collective-permute-start(f32[128,1280]{1,0:T(8,128)} %shard_map.46.z0.zs0), channel_id=1, source_target_pairs={{0,1},{1,0},{2,3},{3,2},{4,5},{5,4},{6,7},{7,6},{8,9},{9,8},{10,11... | collective-permute-start | bytes 1966088 | tf_op jit(solution)/shard_map/ppermute | solution.py:389
  11.6 25.2 %collective-permute-done.1.z2.zs2 = f32[128,1280]{1,0:T(8,128)S(1)} collective-permute-done((f32[128,1280]{1,0:T(8,128)}, f32[128,1280]{1,0:T(8,128)S(1)}, u32[]{:S(2)}, u32[]{:S(2)}) %collective-permute-start.1) | collective-permute-done | bytes 655392 | tf_op jit(solution)/shard_map/ppermute | solution.py:389
  41.0 8.7 %shard_map.47 = (f32[256,1152]{1,0:T(8,128)}, f32[128,1280]{1,0:T(8,128)}) custom-call(f32[128,1280]{1,0:T(8,128)} %shard_map.46.z0.zs0, f32[128,1280]{1,0:T(8,128)} %copy-done.1, f32[128,1280]{1,0:T(8,128)} %copy-done), custom_call_target="tpu_custom_call" | custom-call | tf_op jit(solution)/shard_map/pallas_call | solution.py:376
  49.7 4.9 %collective-permute-done.2.z3.zs3 = f32[128,1280]{1,0:T(8,128)S(1)} collective-permute-done((f32[128,1280]{1,0:T(8,128)S(1)}, f32[128,1280]{1,0:T(8,128)S(1)}, u32[]{:S(2)}, u32[]{:S(2)}) %collective-permute-start.2) | collective-permute-done | bytes 655392 | tf_op jit(solution)/shard_map/ppermute | solution.py:389
  55.4 6.6 %shard_map.48.y23 = f32[256,1152]{1,0:T(8,128)} custom-call(f32[128,1280]{1,0:T(8,128)} %copy-done, f32[128,1280]{1,0:T(8,128)} %copy-done.2, f32[128,1280]{1,0:T(8,128)} %get-tuple-element.25.side_ref), custom_call_target="tpu_custom_call" | custom-call | tf_op jit(solution)/shard_map/pallas_call | solution.py:376
  62.0 13.1 %shard_map.49 = (f32[32,3584]{1,0:T(8,128)}, f32[32,896]{1,0:T(8,128)}, f32[128,1024]{1,0:T(8,128)}) custom-call(s32[2]{0:T(128)} %pad_add_fusion.1.place_ref, f32[128,1280]{1,0:T(8,128)} %shard_map.46.z0.zs0, f32[128,1280]{1,0:T(8,128)} %copy-done.1, f32[128,1280]{1,0:T(8,128)} %copy-done, f32[128,1280]{1,0:T(8,128)} %copy-done.2, ...), custom_call_target="tpu_custom_call" | custom-call | tf_op jit(solution)/shard_map/pallas_call | solution.py:376
  80.3 9.1 %collective-permute-start.4 = (f32[16,3584]{1,0:T(8,128)}, f32[16,3584]{1,0:T(8,128)S(1)}, u32[]{:S(2)}, u32[]{:S(2)}) collective-permute-start(f32[16,3584]{1,0:T(8,128)} %get-tuple-element.29), channel_id=1, source_target_pairs={{0,4},{1,5},{2,6},{3,7},{4,0},{5,1},{6,2},{7,3},{8,12},{9,13},{10,... | collective-permute-start | bytes 688136 | tf_op jit(solution)/shard_map/ppermute | solution.py:389
  89.4 20.9 %collective-permute-done.4 = f32[16,3584]{1,0:T(8,128)S(1)} collective-permute-done((f32[16,3584]{1,0:T(8,128)}, f32[16,3584]{1,0:T(8,128)S(1)}, u32[]{:S(2)}, u32[]{:S(2)}) %collective-permute-start.4) | collective-permute-done | bytes 229408 | tf_op jit(solution)/shard_map/ppermute | solution.py:389
  113.2 9.3 %collective-permute-start.5 = (f32[16,3584]{1,0:T(8,128)S(1)}, f32[16,3584]{1,0:T(8,128)S(1)}, u32[]{:S(2)}, u32[]{:S(2)}) collective-permute-start(f32[16,3584]{1,0:T(8,128)S(1)} %add.3.refs_0_), channel_id=1, source_target_pairs={{0,15},{1,0},{2,1},{3,2},{4,3},{5,4},{6,5},{7,6},{8,7},{9,8},{10,9... | collective-permute-start | bytes 688136 | tf_op jit(solution)/shard_map/ppermute | solution.py:497
  122.5 3.9 %collective-permute-done.12.refs_15_ = f32[16,3584]{1,0:T(8,128)S(1)} collective-permute-done((f32[16,3584]{1,0:T(8,128)S(1)}, f32[16,3584]{1,0:T(8,128)S(1)}, u32[]{:S(2)}, u32[]{:S(2)}) %collective-permute-start.12) | collective-permute-done | bytes 229408 | tf_op jit(solution)/shard_map/ppermute | solution.py:494
  128.3 5.1 %collective-permute-start.6 = (f32[16,3584]{1,0:T(8,128)S(1)}, f32[16,3584]{1,0:T(8,128)S(1)}, u32[]{:S(2)}, u32[]{:S(2)}) collective-permute-start(f32[16,3584]{1,0:T(8,128)S(1)} %collective-permute-done.5.refs_1_), channel_id=1, source_target_pairs={{0,15},{1,0},{2,1},{3,2},{4,3},{5,4},{6,5},{7,6},{8,7},{9,8},{10,9... | collective-permute-start | bytes 688136 | tf_op jit(solution)/shard_map/ppermute | solution.py:497
  133.4 3.0 %collective-permute-done.13.refs_14_ = f32[16,3584]{1,0:T(8,128)S(1)} collective-permute-done((f32[16,3584]{1,0:T(8,128)S(1)}, f32[16,3584]{1,0:T(8,128)S(1)}, u32[]{:S(2)}, u32[]{:S(2)}) %collective-permute-start.13) | collective-permute-done | bytes 229408 | tf_op jit(solution)/shard_map/ppermute | solution.py:494
  138.4 5.1 %collective-permute-start.7 = (f32[16,3584]{1,0:T(8,128)S(1)}, f32[16,3584]{1,0:T(8,128)S(1)}, u32[]{:S(2)}, u32[]{:S(2)}) collective-permute-start(f32[16,3584]{1,0:T(8,128)S(1)} %collective-permute-done.6.refs_2_), channel_id=1, source_target_pairs={{0,15},{1,0},{2,1},{3,2},{4,3},{5,4},{6,5},{7,6},{8,7},{9,8},{10,9... | collective-permute-start | bytes 688136 | tf_op jit(solution)/shard_map/ppermute | solution.py:497
  147.6 5.1 %collective-permute-start.8 = (f32[16,3584]{1,0:T(8,128)S(1)}, f32[16,3584]{1,0:T(8,128)S(1)}, u32[]{:S(2)}, u32[]{:S(2)}) collective-permute-start(f32[16,3584]{1,0:T(8,128)S(1)} %collective-permute-done.7.refs_3_), channel_id=1, source_target_pairs={{0,15},{1,0},{2,1},{3,2},{4,3},{5,4},{6,5},{7,6},{8,7},{9,8},{10,9... | collective-permute-start | bytes 688136 | tf_op jit(solution)/shard_map/ppermute | solution.py:497
  156.7 5.1 %collective-permute-start.9 = (f32[16,3584]{1,0:T(8,128)S(1)}, f32[16,3584]{1,0:T(8,128)S(1)}, u32[]{:S(2)}, u32[]{:S(2)}) collective-permute-start(f32[16,3584]{1,0:T(8,128)S(1)} %collective-permute-done.8.refs_4_), channel_id=1, source_target_pairs={{0,15},{1,0},{2,1},{3,2},{4,3},{5,4},{6,5},{7,6},{8,7},{9,8},{10,9... | collective-permute-start | bytes 688136 | tf_op jit(solution)/shard_map/ppermute | solution.py:497
  165.8 5.1 %collective-permute-start.10 = (f32[16,3584]{1,0:T(8,128)S(1)}, f32[16,3584]{1,0:T(8,128)S(1)}, u32[]{:S(2)}, u32[]{:S(2)}) collective-permute-start(f32[16,3584]{1,0:T(8,128)S(1)} %collective-permute-done.9.refs_5_), channel_id=1, source_target_pairs={{0,15},{1,0},{2,1},{3,2},{4,3},{5,4},{6,5},{7,6},{8,7},{9,8},{10,9... | collective-permute-start | bytes 688136 | tf_op jit(solution)/shard_map/ppermute | solution.py:497
  174.9 5.4 %collective-permute-start.11 = (f32[16,3584]{1,0:T(8,128)S(1)}, f32[16,3584]{1,0:T(8,128)S(1)}, u32[]{:S(2)}, u32[]{:S(2)}) collective-permute-start(f32[16,3584]{1,0:T(8,128)S(1)} %collective-permute-done.10.refs_6_), channel_id=1, source_target_pairs={{0,15},{1,0},{2,1},{3,2},{4,3},{5,4},{6,5},{7,6},{8,7},{9,8},{10,9... | collective-permute-start | bytes 688136 | tf_op jit(solution)/shard_map/ppermute | solution.py:497
  185.8 6.7 %collective-permute-done.19.refs_8_ = f32[16,3584]{1,0:T(8,128)} collective-permute-done((f32[16,3584]{1,0:T(8,128)S(1)}, f32[16,3584]{1,0:T(8,128)}, u32[]{:S(2)}, u32[]{:S(2)}) %collective-permute-start.19) | collective-permute-done | bytes 229408 | tf_op jit(solution)/shard_map/ppermute | solution.py:494
  192.6 11.9 %shard_map.51 = (f32[128,2560]{1,0:T(8,128)}, f32[128,768]{1,0:T(8,128)}) custom-call(s32[3]{0:T(128)} %pad_add_fusion.side_ref, f32[16,3584]{1,0:T(8,128)} %copy-done.3, f32[16,3584]{1,0:T(8,128)} %copy-done.5, f32[16,3584]{1,0:T(8,128)} %copy-done.7, f32[16,3584]{1,0:T(8,128)} %copy-done.9, f32[16,3584]{1,0:T(8,128)} %copy-done.11, f32[16,3584]{1,0:T(8,128)} %copy-done.13, ...), custom_call_target="tpu_custom_call" | custom-call | tf_op jit(solution)/shard_map/pallas_call | solution.py:376
  206.4 3.2 %collective-permute-done.20.refs_0_ = f32[128,2560]{1,0:T(8,128)S(1)} collective-permute-done((f32[128,2560]{1,0:T(8,128)}, f32[128,2560]{1,0:T(8,128)S(1)}, u32[]{:S(2)}, u32[]{:S(2)}) %collective-permute-start.20) | collective-permute-done | bytes 1310752 | tf_op jit(solution)/shard_map/ppermute | solution.py:389
  209.6 5.6 %shard_map.52 = (f32[128,1792]{1,0:T(8,128)}, f32[128,640]{1,0:T(8,128)}, f32[128,896]{1,0:T(8,128)}) custom-call(s32[1]{0:T(128)} %bitcast.core_ref, f32[128,2560]{1,0:T(8,128)} %get-tuple-element.31.own_ref.pay_ref, f32[128,2560]{1,0:T(8,128)S(1)} %collective-permute-done.20.refs_0_, f32[128,768]{1,0:T(8,128)} %get-tuple-element.32.refs_1_.y_ref), custom_call_target="tpu_custom_call" | custom-call | tf_op jit(solution)/shard_map/pallas_call | solution.py:376
  217.9 11.9 %collective-permute-done.21.refs_0_ = f32[128,896]{1,0:T(8,128)S(1)} collective-permute-done((f32[128,896]{1,0:T(8,128)}, f32[128,896]{1,0:T(8,128)S(1)}, u32[]{:S(2)}, u32[]{:S(2)}) %collective-permute-start.21) | collective-permute-done | bytes 458784 | tf_op jit(solution)/shard_map/ppermute | solution.py:389
  234.3 5.0 %shard_map.54 = (f32[128,1152]{1,0:T(8,128)}, f32[128,512]{1,0:T(8,128)}, f32[128,640]{1,0:T(8,128)}) custom-call(s32[1]{0:T(128)} %bitcast.core_ref, f32[128,1792]{1,0:T(8,128)} %get-tuple-element.33.own_ref.pay_ref, f32[128,896]{1,0:T(8,128)S(1)} %collective-permute-done.21.refs_0_, f32[128,896]{1,0:T(8,128)S(1)} %collective-permute-done.22.refs_1_, ...), custom_call_target="tpu_custom_call" | custom-call | tf_op jit(solution)/shard_map/pallas_call | solution.py:376
  239.2 3.3 %collective-permute-start.23 = (f32[128,640]{1,0:T(8,128)}, f32[128,640]{1,0:T(8,128)S(1)}, u32[]{:S(2)}, u32[]{:S(2)}) collective-permute-start(f32[128,640]{1,0:T(8,128)} %get-tuple-element.37), channel_id=1, source_target_pairs={{0,64},{16,80},{32,96},{48,112},{64,0},{80,16},{96,32},{112,48},{1... | collective-permute-start | bytes 983048 | tf_op jit(solution)/shard_map/ppermute | solution.py:389
  242.6 10.4 %collective-permute-done.23.refs_0_ = f32[128,640]{1,0:T(8,128)S(1)} collective-permute-done((f32[128,640]{1,0:T(8,128)}, f32[128,640]{1,0:T(8,128)S(1)}, u32[]{:S(2)}, u32[]{:S(2)}) %collective-permute-start.23) | collective-permute-done | bytes 327712 | tf_op jit(solution)/shard_map/ppermute | solution.py:389
  257.2 4.4 %shard_map.56 = (f32[128,640]{1,0:T(8,128)}, f32[128,384]{1,0:T(8,128)}) custom-call(s32[1]{0:T(128)} %bitcast.core_ref, f32[128,1152]{1,0:T(8,128)} %get-tuple-element.36.own_ref.pay_ref, f32[128,640]{1,0:T(8,128)S(1)} %collective-permute-done.23.refs_0_, f32[128,640]{1,0:T(8,128)S(1)} %collective-permute-done.24.refs_1_, f32[128,512]{1,0:T(8,128)} %shard_map.55.refs_2_.y_ref), custom_call_target="tpu_custom_call" | custom-call | tf_op jit(solution)/shard_map/pallas_call | solution.py:376
  261.6 3.2 %collective-permute-start.25 = (f32[128,640]{1,0:T(8,128)}, f32[128,640]{1,0:T(8,128)S(1)}, u32[]{:S(2)}, u32[]{:S(2)}) collective-permute-start(f32[128,640]{1,0:T(8,128)} %get-tuple-element.39.own_ref.pay_ref), channel_id=1, source_target_pairs={{0,128},{16,144},{32,160},{48,176},{64,192},{80,208},{96,224},{112... | collective-permute-start | bytes 983048 | tf_op jit(solution)/shard_map/ppermute | solution.py:389
  267.1 6.8 %collective-permute-done.25.refs_0_ = f32[128,640]{1,0:T(8,128)S(1)} collective-permute-done((f32[128,640]{1,0:T(8,128)}, f32[128,640]{1,0:T(8,128)S(1)}, u32[]{:S(2)}, u32[]{:S(2)}) %collective-permute-start.25) | collective-permute-done | bytes 327712 | tf_op jit(solution)/shard_map/ppermute | solution.py:389
  273.8 4.0 %shard_map.58 = (f32[128,256]{1,0:T(8,128)}, f32[128,256]{1,0:T(8,128)}) custom-call(s32[1]{0:T(128)} %bitcast.core_ref, f32[128,640]{1,0:T(8,128)} %get-tuple-element.39.own_ref.pay_ref, f32[128,640]{1,0:T(8,128)S(1)} %collective-permute-done.25.refs_0_, f32[128,384]{1,0:T(8,128)} %shard_map.57.refs_1_.y_ref), custom_call_target="tpu_custom_call" | custom-call | tf_op jit(solution)/shard_map/pallas_call | solution.py:376
  282.2 4.2 %collective-permute-done.26.other_ref = f32[128,256]{1,0:T(8,128)S(1)} collective-permute-done((f32[128,256]{1,0:T(8,128)}, f32[128,256]{1,0:T(8,128)S(1)}, u32[]{:S(2)}, u32[]{:S(2)}) %collective-permute-start.26) | collective-permute-done | bytes 131104 | tf_op jit(solution)/shard_map/ppermute | solution.py:389
  286.4 3.2 %shard_map.60 = f32[128,128]{1,0:T(8,128)} custom-call(s32[1,128]{1,0:T(1,128)} %order_ref.3, f32[128,128]{1,0:T(8,128)} %r_ref.3, f32[128,256]{1,0:T(8,128)} %get-tuple-element.41.own_ref, f32[128,256]{1,0:T(8,128)S(1)} %collective-permute-done.26.other_ref, f32[128,256]{1,0:T(8,128)} %shard_map.59.y_ref), custom_call_target="tpu_custom_call" | custom-call | tf_op jit(solution)/shard_map/pallas_call | solution.py:376
  (76 shorter events, 60.8 us)
Async XLA Ops:
  2.6 34.2 %collective-permute-start.1 = (f32[128,1280]{1,0:T(8,128)}, f32[128,1280]{1,0:T(8,128)S(1)}, u32[]{:S(2)}, u32[]{:S(2)}) collective-permute-start(f32[128,1280]{1,0:T(8,128)} %shard_map.46.z0.zs0), channel_id=1, source_target_pairs={{0,2},{1,3},{2,0},{3,1},{4,6},{5,7},{6,4},{7,5},{8,10},{9,11},{10,... | collective-permute-start | bytes 1966088 | tf_op jit(solution)/shard_map/ppermute | solution.py:389
  7.8 32.4 %collective-permute-start = (f32[128,1280]{1,0:T(8,128)}, f32[128,1280]{1,0:T(8,128)S(1)}, u32[]{:S(2)}, u32[]{:S(2)}) collective-permute-start(f32[128,1280]{1,0:T(8,128)} %shard_map.46.z0.zs0), channel_id=1, source_target_pairs={{0,1},{1,0},{2,3},{3,2},{4,5},{5,4},{6,7},{7,6},{8,9},{9,8},{10,11... | collective-permute-start | bytes 1966088 | tf_op jit(solution)/shard_map/ppermute | solution.py:389
  36.9 17.7 %collective-permute-start.2 = (f32[128,1280]{1,0:T(8,128)S(1)}, f32[128,1280]{1,0:T(8,128)S(1)}, u32[]{:S(2)}, u32[]{:S(2)}) collective-permute-start(f32[128,1280]{1,0:T(8,128)S(1)} %collective-permute-done.1.z2.zs2), channel_id=1, source_target_pairs={{0,1},{1,0},{2,3},{3,2},{4,5},{5,4},{6,7},{7,6},{8,9},{9,8},{10,11... | collective-permute-start | bytes 1966088 | tf_op jit(solution)/shard_map/ppermute | solution.py:389
  75.1 3.4 %collective-permute-start.3 = (f32[32,896]{1,0:T(8,128)}, f32[32,896]{1,0:T(8,128)S(1)}, u32[]{:S(2)}, u32[]{:S(2)}) collective-permute-start(f32[32,896]{1,0:T(8,128)} %get-tuple-element.27), channel_id=1, source_target_pairs={{0,16},{16,0},{32,48},{48,32},{64,80},{80,64},{96,112},{112,96},{1... | collective-permute-start | bytes 344072 | tf_op jit(solution)/shard_map/ppermute | solution.py:389
  80.3 29.9 %collective-permute-start.4 = (f32[16,3584]{1,0:T(8,128)}, f32[16,3584]{1,0:T(8,128)S(1)}, u32[]{:S(2)}, u32[]{:S(2)}) collective-permute-start(f32[16,3584]{1,0:T(8,128)} %get-tuple-element.29), channel_id=1, source_target_pairs={{0,4},{1,5},{2,6},{3,7},{4,0},{5,1},{6,2},{7,3},{8,12},{9,13},{10,... | collective-permute-start | bytes 688136 | tf_op jit(solution)/shard_map/ppermute | solution.py:389
  111.3 81.2 %copy-start.3 = (f32[16,3584]{1,0:T(8,128)}, f32[16,3584]{1,0:T(8,128)S(1)}, u32[]{:S(2)}) copy-start(f32[16,3584]{1,0:T(8,128)S(1)} %add.3.refs_0_) | copy-start | bytes 688132
  111.3 15.1 %collective-permute-start.12 = (f32[16,3584]{1,0:T(8,128)S(1)}, f32[16,3584]{1,0:T(8,128)S(1)}, u32[]{:S(2)}, u32[]{:S(2)}) collective-permute-start(f32[16,3584]{1,0:T(8,128)S(1)} %add.3.refs_0_), channel_id=1, source_target_pairs={{0,1},{1,2},{2,3},{3,4},{4,5},{5,6},{6,7},{7,8},{8,9},{9,10},{10,1... | collective-permute-start | bytes 688136 | tf_op jit(solution)/shard_map/ppermute | solution.py:494
  113.2 15.1 %collective-permute-start.5 = (f32[16,3584]{1,0:T(8,128)S(1)}, f32[16,3584]{1,0:T(8,128)S(1)}, u32[]{:S(2)}, u32[]{:S(2)}) collective-permute-start(f32[16,3584]{1,0:T(8,128)S(1)} %add.3.refs_0_), channel_id=1, source_target_pairs={{0,15},{1,0},{2,1},{3,2},{4,3},{5,4},{6,5},{7,6},{8,7},{9,8},{10,9... | collective-permute-start | bytes 688136 | tf_op jit(solution)/shard_map/ppermute | solution.py:497
  126.3 66.1 %copy-start.4 = (f32[16,3584]{1,0:T(8,128)}, f32[16,3584]{1,0:T(8,128)S(1)}, u32[]{:S(2)}) copy-start(f32[16,3584]{1,0:T(8,128)S(1)} %collective-permute-done.12.refs_15_) | copy-start | bytes 688132
  126.3 10.1 %collective-permute-start.13 = (f32[16,3584]{1,0:T(8,128)S(1)}, f32[16,3584]{1,0:T(8,128)S(1)}, u32[]{:S(2)}, u32[]{:S(2)}) collective-permute-start(f32[16,3584]{1,0:T(8,128)S(1)} %collective-permute-done.12.refs_15_), channel_id=1, source_target_pairs={{0,1},{1,2},{2,3},{3,4},{4,5},{5,6},{6,7},{7,8},{8,9},{9,10},{10,1... | collective-permute-start | bytes 688136 | tf_op jit(solution)/shard_map/ppermute | solution.py:494
  128.3 64.2 %copy-start.5 = (f32[16,3584]{1,0:T(8,128)}, f32[16,3584]{1,0:T(8,128)S(1)}, u32[]{:S(2)}) copy-start(f32[16,3584]{1,0:T(8,128)S(1)} %collective-permute-done.5.refs_1_) | copy-start | bytes 688132
  128.3 10.0 %collective-permute-start.6 = (f32[16,3584]{1,0:T(8,128)S(1)}, f32[16,3584]{1,0:T(8,128)S(1)}, u32[]{:S(2)}, u32[]{:S(2)}) collective-permute-start(f32[16,3584]{1,0:T(8,128)S(1)} %collective-permute-done.5.refs_1_), channel_id=1, source_target_pairs={{0,15},{1,0},{2,1},{3,2},{4,3},{5,4},{6,5},{7,6},{8,7},{9,8},{10,9... | collective-permute-start | bytes 688136 | tf_op jit(solution)/shard_map/ppermute | solution.py:497
  136.4 56.1 %copy-start.6 = (f32[16,3584]{1,0:T(8,128)}, f32[16,3584]{1,0:T(8,128)S(1)}, u32[]{:S(2)}) copy-start(f32[16,3584]{1,0:T(8,128)S(1)} %collective-permute-done.13.refs_14_) | copy-start | bytes 688132
  136.4 9.2 %collective-permute-start.14 = (f32[16,3584]{1,0:T(8,128)S(1)}, f32[16,3584]{1,0:T(8,128)S(1)}, u32[]{:S(2)}, u32[]{:S(2)}) collective-permute-start(f32[16,3584]{1,0:T(8,128)S(1)} %collective-permute-done.13.refs_14_), channel_id=1, source_target_pairs={{0,1},{1,2},{2,3},{3,4},{4,5},{5,6},{6,7},{7,8},{8,9},{9,10},{10,1... | collective-permute-start | bytes 688136 | tf_op jit(solution)/shard_map/ppermute | solution.py:494
  138.3 54.1 %copy-start.7 = (f32[16,3584]{1,0:T(8,128)}, f32[16,3584]{1,0:T(8,128)S(1)}, u32[]{:S(2)}) copy-start(f32[16,3584]{1,0:T(8,128)S(1)} %collective-permute-done.6.refs_2_) | copy-start | bytes 688132
  138.4 9.2 %collective-permute-start.7 = (f32[16,3584]{1,0:T(8,128)S(1)}, f32[16,3584]{1,0:T(8,128)S(1)}, u32[]{:S(2)}, u32[]{:S(2)}) collective-permute-start(f32[16,3584]{1,0:T(8,128)S(1)} %collective-permute-done.6.refs_2_), channel_id=1, source_target_pairs={{0,15},{1,0},{2,1},{3,2},{4,3},{5,4},{6,5},{7,6},{8,7},{9,8},{10,9... | collective-permute-start | bytes 688136 | tf_op jit(solution)/shard_map/ppermute | solution.py:497
  145.6 9.1 %collective-permute-start.15 = (f32[16,3584]{1,0:T(8,128)S(1)}, f32[16,3584]{1,0:T(8,128)S(1)}, u32[]{:S(2)}, u32[]{:S(2)}) collective-permute-start(f32[16,3584]{1,0:T(8,128)S(1)} %collective-permute-done.14.refs_13_), channel_id=1, source_target_pairs={{0,1},{1,2},{2,3},{3,4},{4,5},{5,6},{6,7},{7,8},{8,9},{9,10},{10,1... | collective-permute-start | bytes 688136 | tf_op jit(solution)/shard_map/ppermute | solution.py:494
  147.6 9.1 %collective-permute-start.8 = (f32[16,3584]{1,0:T(8,128)S(1)}, f32[16,3584]{1,0:T(8,128)S(1)}, u32[]{:S(2)}, u32[]{:S(2)}) collective-permute-start(f32[16,3584]{1,0:T(8,128)S(1)} %collective-permute-done.7.refs_3_), channel_id=1, source_target_pairs={{0,15},{1,0},{2,1},{3,2},{4,3},{5,4},{6,5},{7,6},{8,7},{9,8},{10,9... | collective-permute-start | bytes 688136 | tf_op jit(solution)/shard_map/ppermute | solution.py:497
  154.7 9.1 %collective-permute-start.16 = (f32[16,3584]{1,0:T(8,128)S(1)}, f32[16,3584]{1,0:T(8,128)S(1)}, u32[]{:S(2)}, u32[]{:S(2)}) collective-permute-start(f32[16,3584]{1,0:T(8,128)S(1)} %collective-permute-done.15.refs_12_), channel_id=1, source_target_pairs={{0,1},{1,2},{2,3},{3,4},{4,5},{5,6},{6,7},{7,8},{8,9},{9,10},{10,1... | collective-permute-start | bytes 688136 | tf_op jit(solution)/shard_map/ppermute | solution.py:494
  156.7 9.1 %collective-permute-start.9 = (f32[16,3584]{1,0:T(8,128)S(1)}, f32[16,3584]{1,0:T(8,128)S(1)}, u32[]{:S(2)}, u32[]{:S(2)}) collective-permute-start(f32[16,3584]{1,0:T(8,128)S(1)} %collective-permute-done.8.refs_4_), channel_id=1, source_target_pairs={{0,15},{1,0},{2,1},{3,2},{4,3},{5,4},{6,5},{7,6},{8,7},{9,8},{10,9... | collective-permute-start | bytes 688136 | tf_op jit(solution)/shard_map/ppermute | solution.py:497
  163.9 9.1 %collective-permute-start.17 = (f32[16,3584]{1,0:T(8,128)S(1)}, f32[16,3584]{1,0:T(8,128)S(1)}, u32[]{:S(2)}, u32[]{:S(2)}) collective-permute-start(f32[16,3584]{1,0:T(8,128)S(1)} %collective-permute-done.16.refs_11_), channel_id=1, source_target_pairs={{0,1},{1,2},{2,3},{3,4},{4,5},{5,6},{6,7},{7,8},{8,9},{9,10},{10,1... | collective-permute-start | bytes 688136 | tf_op jit(solution)/shard_map/ppermute | solution.py:494
  165.8 9.1 %collective-permute-start.10 = (f32[16,3584]{1,0:T(8,128)S(1)}, f32[16,3584]{1,0:T(8,128)S(1)}, u32[]{:S(2)}, u32[]{:S(2)}) collective-permute-start(f32[16,3584]{1,0:T(8,128)S(1)} %collective-permute-done.9.refs_5_), channel_id=1, source_target_pairs={{0,15},{1,0},{2,1},{3,2},{4,3},{5,4},{6,5},{7,6},{8,7},{9,8},{10,9... | collective-permute-start | bytes 688136 | tf_op jit(solution)/shard_map/ppermute | solution.py:497
  173.0 10.3 %collective-permute-start.18 = (f32[16,3584]{1,0:T(8,128)S(1)}, f32[16,3584]{1,0:T(8,128)S(1)}, u32[]{:S(2)}, u32[]{:S(2)}) collective-permute-start(f32[16,3584]{1,0:T(8,128)S(1)} %collective-permute-done.17.refs_10_), channel_id=1, source_target_pairs={{0,1},{1,2},{2,3},{3,4},{4,5},{5,6},{6,7},{7,8},{8,9},{9,10},{10,1... | collective-permute-start | bytes 688136 | tf_op jit(solution)/shard_map/ppermute | solution.py:494
  174.9 10.8 %collective-permute-start.11 = (f32[16,3584]{1,0:T(8,128)S(1)}, f32[16,3584]{1,0:T(8,128)S(1)}, u32[]{:S(2)}, u32[]{:S(2)}) collective-permute-start(f32[16,3584]{1,0:T(8,128)S(1)} %collective-permute-done.10.refs_6_), channel_id=1, source_target_pairs={{0,15},{1,0},{2,1},{3,2},{4,3},{5,4},{6,5},{7,6},{8,7},{9,8},{10,9... | collective-permute-start | bytes 688136 | tf_op jit(solution)/shard_map/ppermute | solution.py:497
  183.2 9.2 %collective-permute-start.19 = (f32[16,3584]{1,0:T(8,128)S(1)}, f32[16,3584]{1,0:T(8,128)}, u32[]{:S(2)}, u32[]{:S(2)}) collective-permute-start(f32[16,3584]{1,0:T(8,128)S(1)} %collective-permute-done.18.refs_9_), channel_id=1, source_target_pairs={{0,1},{1,2},{2,3},{3,4},{4,5},{5,6},{6,7},{7,8},{8,9},{9,10},{10,1... | collective-permute-start | bytes 688136 | tf_op jit(solution)/shard_map/ppermute | solution.py:494
  204.5 5.1 %collective-permute-start.20 = (f32[128,2560]{1,0:T(8,128)}, f32[128,2560]{1,0:T(8,128)S(1)}, u32[]{:S(2)}, u32[]{:S(2)}) collective-permute-start(f32[128,2560]{1,0:T(8,128)} %get-tuple-element.31.own_ref.pay_ref), channel_id=1, source_target_pairs={{0,16},{16,0},{32,48},{48,32},{64,80},{80,64},{96,112},{112,96},{1... | collective-permute-start | bytes 3932168 | tf_op jit(solution)/shard_map/ppermute | solution.py:389
  215.2 14.7 %collective-permute-start.21 = (f32[128,896]{1,0:T(8,128)}, f32[128,896]{1,0:T(8,128)S(1)}, u32[]{:S(2)}, u32[]{:S(2)}) collective-permute-start(f32[128,896]{1,0:T(8,128)} %get-tuple-element.34), channel_id=1, source_target_pairs={{0,32},{16,48},{32,0},{48,16},{64,96},{80,112},{96,64},{112,80},{1... | collective-permute-start | bytes 1376264 | tf_op jit(solution)/shard_map/ppermute | solution.py:389
  229.9 4.4 %collective-permute-start.22 = (f32[128,896]{1,0:T(8,128)S(1)}, f32[128,896]{1,0:T(8,128)S(1)}, u32[]{:S(2)}, u32[]{:S(2)}) collective-permute-start(f32[128,896]{1,0:T(8,128)S(1)} %collective-permute-done.21.refs_0_), channel_id=1, source_target_pairs={{0,16},{16,0},{32,48},{48,32},{64,80},{80,64},{96,112},{112,96},{1... | collective-permute-start | bytes 1376264 | tf_op jit(solution)/shard_map/ppermute | solution.py:389
  239.2 13.7 %collective-permute-start.23 = (f32[128,640]{1,0:T(8,128)}, f32[128,640]{1,0:T(8,128)S(1)}, u32[]{:S(2)}, u32[]{:S(2)}) collective-permute-start(f32[128,640]{1,0:T(8,128)} %get-tuple-element.37), channel_id=1, source_target_pairs={{0,64},{16,80},{32,96},{48,112},{64,0},{80,16},{96,32},{112,48},{1... | collective-permute-start | bytes 983048 | tf_op jit(solution)/shard_map/ppermute | solution.py:389
  253.0 4.2 %collective-permute-start.24 = (f32[128,640]{1,0:T(8,128)S(1)}, f32[128,640]{1,0:T(8,128)S(1)}, u32[]{:S(2)}, u32[]{:S(2)}) collective-permute-start(f32[128,640]{1,0:T(8,128)S(1)} %collective-permute-done.23.refs_0_), channel_id=1, source_target_pairs={{0,16},{16,0},{32,48},{48,32},{64,80},{80,64},{96,112},{112,96},{1... | collective-permute-start | bytes 983048 | tf_op jit(solution)/shard_map/ppermute | solution.py:389
  261.6 12.2 %collective-permute-start.25 = (f32[128,640]{1,0:T(8,128)}, f32[128,640]{1,0:T(8,128)S(1)}, u32[]{:S(2)}, u32[]{:S(2)}) collective-permute-start(f32[128,640]{1,0:T(8,128)} %get-tuple-element.39.own_ref.pay_ref), channel_id=1, source_target_pairs={{0,128},{16,144},{32,160},{48,176},{64,192},{80,208},{96,224},{112... | collective-permute-start | bytes 983048 | tf_op jit(solution)/shard_map/ppermute | solution.py:389
  277.8 8.6 %collective-permute-start.26 = (f32[128,256]{1,0:T(8,128)}, f32[128,256]{1,0:T(8,128)S(1)}, u32[]{:S(2)}, u32[]{:S(2)}) collective-permute-start(f32[128,256]{1,0:T(8,128)} %get-tuple-element.41.own_ref), channel_id=1, source_target_pairs={{0,256},{16,272},{32,288},{48,304},{64,320},{80,336},{96,352},{112... | collective-permute-start | bytes 393224 | tf_op jit(solution)/shard_map/ppermute | solution.py:389
  (13 other events, 279.4 us)

commit v6 on v5

--- a/solution.py
+++ b/solution.py
@@ -144,7 +144,7 @@
 
 def quad_kernel(
     nb, place_ref, zs0, zs1, zs2, zs3, y01, y23,
-    out_ref, send_ref, own_ref, z, y, act_ref, x_scr, r_scr, sem,
+    hold_ref, give_ref, keep_ref, send_ref, own_ref, z, y, act_ref, x_scr, r_scr, sem,
 ):
     copies = [
         pltpu.make_async_copy(y01, y.at[pl.ds(0, 2 * B), pl.ds(B, (nb - 1) * B)], sem.at[4]),
@@ -194,28 +194,34 @@
     for part in range(2):
         rows = pl.ds(pl.multiple_of(part * (B // 2) + place_ref[0] * SHARE, SHARE), SHARE)
         put = slice(part * SHARE, (part + 1) * SHARE)
-        out_ref[put, sl(0, head)] = act_ref[rows, sl(0, head)]
+
+        @pl.when(place_ref[2] == part)
+        def _():
+            hold_ref[...] = act_ref[rows, sl(0, head)]
+
+        @pl.when(place_ref[2] != part)
+        def _():
+            give_ref[...] = act_ref[rows, sl(0, head)]
 
         @pl.when(place_ref[1] == 0)
         def _():
-            out_ref[put, first] = act_ref[rows, first]
+            keep_ref[put, :] = act_ref[rows, first]
             send_ref[put, :] = act_ref[rows, second]
 
         @pl.when(place_ref[1] == 1)
         def _():
-            out_ref[put, first] = act_ref[rows, second]
+            keep_ref[put, :] = act_ref[rows, second]
             send_ref[put, :] = act_ref[rows, first]
 
 
 SHARE = B // 8
 
 
-def halve_kernel(cut, bit_ref, out_ref, got_ref, keep_ref, give_ref):
+def halve_kernel(bit_ref, mine_ref, got_ref, keep_ref, give_ref):
     bit = bit_ref[0]
     for to, at in ((keep_ref, bit), (give_ref, 1 - bit)):
         rows = pl.ds(pl.multiple_of(at * SHARE, SHARE), SHARE)
-        to[:, :cut] = out_ref[rows, :cut]
-        to[:, cut:] = out_ref[rows, cut:] + got_ref[rows, :]
+        to[...] = mine_ref[rows, :] + got_ref[rows, :]
 
 
 def cuts(nb):
@@ -427,7 +433,7 @@
     anywhere = pl.BlockSpec(memory_space=pl.ANY)
     return run(
         functools.partial(quad_kernel, nb),
-        [(2 * SHARE, (head + half) * B), (2 * SHARE, half * B), nb - 2],
+        [(SHARE, head * B)] * 2 + [(2 * SHARE, half * B)] * 2 + [nb - 2],
         [place, *zs, *ys],
         [
             pltpu.VMEM((4 * B, nb * B), F32),
@@ -478,16 +484,20 @@
     ys = [y01, run(part(far_kernel, nb), [stack], [z2, z3, side], two)]
     place = lax.axis_index("inner").astype(jnp.int32)
     core = lax.axis_index("outer").astype(jnp.int32) & 1
-    mine, send, own = quad_call(run, levels, jnp.stack([place & 3, core]), [z0, z1, z2, z3], ys)
-    half = (SHARE, mine.shape[1])
+    bit = place >> 2 & 1
+    hold, give, rest, send, own = quad_call(
+        run, levels, jnp.stack([place & 3, core, bit]), [z0, z1, z2, z3], ys
+    )
+    hold = hold + swapped(give, "inner", 2)
+    half = (SHARE, rest.shape[1])
     keep, give = run(
-        part(halve_kernel, cuts(nb)[0] * B),
+        halve_kernel,
         [half, half],
-        [(place >> 2 & 1).reshape(1), mine, near(swapped(send, "outer", 0))],
+        [bit.reshape(1), rest, near(swapped(send, "outer", 0))],
         (),
         [pl.BlockSpec(memory_space=pltpu.SMEM)] + [pl.BlockSpec(memory_space=pltpu.VMEM)] * 2,
     )
-    mine = keep + swapped(give, "inner", 2)
+    mine = jnp.concatenate([hold, keep + swapped(give, "inner", 2)], axis=1)
     parts = [mine] + [None] * 15
     up = down = mine
     for step in range(1, 9):

time: 291 us -> 288 us (0.990)
  the two profiles are of different devices: /device:TPU:22 before, /device:TPU:30 now
where the time goes in v6:
time: 288 us; the launch traced here: 287 us
  waiting for transfers between devices  108 us (38%)
  starting transfers between devices  97.7 us (34%)
  Pallas kernels  75.7 us (26%)
  other arithmetic  3.04 us (1%)
    ppermute x13, waiting for transfers between devices, swapped(): return lax.ppermute(block, axis, [(k, k ^ 1 << bit) for k in range(count)])  83.1 us
    pallas_call x15, Pallas kernels, call(): pl.pallas_call(kernel, out_shape=shapes[0] if one else shapes, grid=grid,...  75.7 us
    ppermute x13, starting transfers between devices, swapped(): return lax.ppermute(block, axis, [(k, k ^ 1 << bit) for k in range(count)])  42.1 us
    ppermute x7, starting transfers between devices, body(): down = lax.ppermute(down, 'inner', [(k, (k - 1) % 16) for k in range(16)])  40.3 us
    ppermute x8, waiting for transfers between devices, body(): up = lax.ppermute(up, 'inner', [(k, (k + 1) % 16) for k in range(16)])  24.7 us
    ppermute x8, starting transfers between devices, body(): up = lax.ppermute(up, 'inner', [(k, (k + 1) % 16) for k in range(16)])  15.3 us
  transfers between devices with their start and end apart: 28, of which 17 were waited for; matrix products, arithmetic and copies ran while one was open for 1% of the time, Pallas kernels for 7%

profile of v6, /device:TPU:30, one launch (start us, length us, event | category | flops | bytes accessed | tf_op | source)
XLA Modules:
  0.0 286.6 jit_solution(4021951464059609892)
XLA Ops:
  2.6 5.2 %collective-permute-start.1 = (f32[128,1280]{1,0:T(8,128)}, f32[128,1280]{1,0:T(8,128)S(1)}, u32[]{:S(2)}, u32[]{:S(2)}) collective-permute-start(f32[128,1280]{1,0:T(8,128)} %shard_map.46.z0.zs0), channel_id=1, source_target_pairs={{0,2},{1,3},{2,0},{3,1},{4,6},{5,7},{6,4},{7,5},{8,10},{9,11},{10,... | collective-permute-start | bytes 1966088 | tf_op jit(solution)/shard_map/ppermute | solution.py:395
  7.8 3.8 %collective-permute-start = (f32[128,1280]{1,0:T(8,128)}, f32[128,1280]{1,0:T(8,128)S(1)}, u32[]{:S(2)}, u32[]{:S(2)}) collective-permute-start(f32[128,1280]{1,0:T(8,128)} %shard_map.46.z0.zs0), channel_id=1, source_target_pairs={{0,1},{1,0},{2,3},{3,2},{4,5},{5,4},{6,7},{7,6},{8,9},{9,8},{10,11... | collective-permute-start | bytes 1966088 | tf_op jit(solution)/shard_map/ppermute | solution.py:395
  11.6 25.2 %collective-permute-done.1.z2.zs2 = f32[128,1280]{1,0:T(8,128)S(1)} collective-permute-done((f32[128,1280]{1,0:T(8,128)}, f32[128,1280]{1,0:T(8,128)S(1)}, u32[]{:S(2)}, u32[]{:S(2)}) %collective-permute-start.1) | collective-permute-done | bytes 655392 | tf_op jit(solution)/shard_map/ppermute | solution.py:395
  41.0 8.7 %shard_map.47 = (f32[256,1152]{1,0:T(8,128)}, f32[128,1280]{1,0:T(8,128)}) custom-call(f32[128,1280]{1,0:T(8,128)} %shard_map.46.z0.zs0, f32[128,1280]{1,0:T(8,128)} %copy-done.1, f32[128,1280]{1,0:T(8,128)} %copy-done), custom_call_target="tpu_custom_call" | custom-call | tf_op jit(solution)/shard_map/pallas_call | solution.py:382
  49.7 4.8 %collective-permute-done.2.z3.zs3 = f32[128,1280]{1,0:T(8,128)S(1)} collective-permute-done((f32[128,1280]{1,0:T(8,128)S(1)}, f32[128,1280]{1,0:T(8,128)S(1)}, u32[]{:S(2)}, u32[]{:S(2)}) %collective-permute-start.2) | collective-permute-done | bytes 655392 | tf_op jit(solution)/shard_map/ppermute | solution.py:395
  55.4 6.6 %shard_map.48.y23 = f32[256,1152]{1,0:T(8,128)} custom-call(f32[128,1280]{1,0:T(8,128)} %copy-done, f32[128,1280]{1,0:T(8,128)} %copy-done.2, f32[128,1280]{1,0:T(8,128)} %get-tuple-element.27.side_ref), custom_call_target="tpu_custom_call" | custom-call | tf_op jit(solution)/shard_map/pallas_call | solution.py:382
  62.0 13.1 %shard_map.49 = (f32[16,2688]{1,0:T(8,128)}, f32[16,2688]{1,0:T(8,128)}, f32[32,896]{1,0:T(8,128)}, f32[32,896]{1,0:T(8,128)}, f32[128,1024]{1,0:T(8,128)}) custom-call(s32[3]{0:T(128)} %pad_add_fusion.1.place_ref, f32[128,1280]{1,0:T(8,128)} %shard_map.46.z0.zs0, f32[128,1280]{1,0:T(8,128)} %copy-done.1, f32[128,1280]{1,0:T(8,128)} %copy-done, ...), custom_call_target="tpu_custom_call" | custom-call | tf_op jit(solution)/shard_map/pallas_call | solution.py:382
  77.0 9.1 %collective-permute-start.3 = (f32[16,2688]{1,0:T(8,128)}, f32[16,2688]{1,0:T(8,128)S(1)}, u32[]{:S(2)}, u32[]{:S(2)}) collective-permute-start(f32[16,2688]{1,0:T(8,128)} %get-tuple-element.29), channel_id=1, source_target_pairs={{0,4},{1,5},{2,6},{3,7},{4,0},{5,1},{6,2},{7,3},{8,12},{9,13},{10,... | collective-permute-start | bytes 516104 | tf_op jit(solution)/shard_map/ppermute | solution.py:395
  89.6 16.7 %collective-permute-done.3 = f32[16,2688]{1,0:T(8,128)S(1)} collective-permute-done((f32[16,2688]{1,0:T(8,128)}, f32[16,2688]{1,0:T(8,128)S(1)}, u32[]{:S(2)}, u32[]{:S(2)}) %collective-permute-start.3) | collective-permute-done | bytes 172064 | tf_op jit(solution)/shard_map/ppermute | solution.py:395
  110.1 9.3 %collective-permute-start.6 = (f32[16,3584]{1,0:T(8,128)S(1)}, f32[16,3584]{1,0:T(8,128)S(1)}, u32[]{:S(2)}, u32[]{:S(2)}) collective-permute-start(f32[16,3584]{1,0:T(8,128)S(1)} %pad_maximum_fusion.refs_0_), channel_id=1, source_target_pairs={{0,15},{1,0},{2,1},{3,2},{4,3},{5,4},{6,5},{7,6},{8,7},{9,8},{10,9... | collective-permute-start | bytes 688136 | tf_op jit(solution)/shard_map/ppermute | solution.py:507
  119.4 3.9 %collective-permute-done.13.refs_15_ = f32[16,3584]{1,0:T(8,128)S(1)} collective-permute-done((f32[16,3584]{1,0:T(8,128)S(1)}, f32[16,3584]{1,0:T(8,128)S(1)}, u32[]{:S(2)}, u32[]{:S(2)}) %collective-permute-start.13) | collective-permute-done | bytes 229408 | tf_op jit(solution)/shard_map/ppermute | solution.py:504
  125.2 5.1 %collective-permute-start.7 = (f32[16,3584]{1,0:T(8,128)S(1)}, f32[16,3584]{1,0:T(8,128)S(1)}, u32[]{:S(2)}, u32[]{:S(2)}) collective-permute-start(f32[16,3584]{1,0:T(8,128)S(1)} %collective-permute-done.6.refs_1_), channel_id=1, source_target_pairs={{0,15},{1,0},{2,1},{3,2},{4,3},{5,4},{6,5},{7,6},{8,7},{9,8},{10,9... | collective-permute-start | bytes 688136 | tf_op jit(solution)/shard_map/ppermute | solution.py:507
  130.4 3.0 %collective-permute-done.14.refs_14_ = f32[16,3584]{1,0:T(8,128)S(1)} collective-permute-done((f32[16,3584]{1,0:T(8,128)S(1)}, f32[16,3584]{1,0:T(8,128)S(1)}, u32[]{:S(2)}, u32[]{:S(2)}) %collective-permute-start.14) | collective-permute-done | bytes 229408 | tf_op jit(solution)/shard_map/ppermute | solution.py:504
  135.3 5.1 %collective-permute-start.8 = (f32[16,3584]{1,0:T(8,128)S(1)}, f32[16,3584]{1,0:T(8,128)S(1)}, u32[]{:S(2)}, u32[]{:S(2)}) collective-permute-start(f32[16,3584]{1,0:T(8,128)S(1)} %collective-permute-done.7.refs_2_), channel_id=1, source_target_pairs={{0,15},{1,0},{2,1},{3,2},{4,3},{5,4},{6,5},{7,6},{8,7},{9,8},{10,9... | collective-permute-start | bytes 688136 | tf_op jit(solution)/shard_map/ppermute | solution.py:507
  144.6 5.1 %collective-permute-start.9 = (f32[16,3584]{1,0:T(8,128)S(1)}, f32[16,3584]{1,0:T(8,128)S(1)}, u32[]{:S(2)}, u32[]{:S(2)}) collective-permute-start(f32[16,3584]{1,0:T(8,128)S(1)} %collective-permute-done.8.refs_3_), channel_id=1, source_target_pairs={{0,15},{1,0},{2,1},{3,2},{4,3},{5,4},{6,5},{7,6},{8,7},{9,8},{10,9... | collective-permute-start | bytes 688136 | tf_op jit(solution)/shard_map/ppermute | solution.py:507
  153.7 5.1 %collective-permute-start.10 = (f32[16,3584]{1,0:T(8,128)S(1)}, f32[16,3584]{1,0:T(8,128)S(1)}, u32[]{:S(2)}, u32[]{:S(2)}) collective-permute-start(f32[16,3584]{1,0:T(8,128)S(1)} %collective-permute-done.9.refs_4_), channel_id=1, source_target_pairs={{0,15},{1,0},{2,1},{3,2},{4,3},{5,4},{6,5},{7,6},{8,7},{9,8},{10,9... | collective-permute-start | bytes 688136 | tf_op jit(solution)/shard_map/ppermute | solution.py:507
  162.8 5.1 %collective-permute-start.11 = (f32[16,3584]{1,0:T(8,128)S(1)}, f32[16,3584]{1,0:T(8,128)S(1)}, u32[]{:S(2)}, u32[]{:S(2)}) collective-permute-start(f32[16,3584]{1,0:T(8,128)S(1)} %collective-permute-done.10.refs_5_), channel_id=1, source_target_pairs={{0,15},{1,0},{2,1},{3,2},{4,3},{5,4},{6,5},{7,6},{8,7},{9,8},{10,9... | collective-permute-start | bytes 688136 | tf_op jit(solution)/shard_map/ppermute | solution.py:507
  171.9 5.4 %collective-permute-start.12 = (f32[16,3584]{1,0:T(8,128)S(1)}, f32[16,3584]{1,0:T(8,128)S(1)}, u32[]{:S(2)}, u32[]{:S(2)}) collective-permute-start(f32[16,3584]{1,0:T(8,128)S(1)} %collective-permute-done.11.refs_6_), channel_id=1, source_target_pairs={{0,15},{1,0},{2,1},{3,2},{4,3},{5,4},{6,5},{7,6},{8,7},{9,8},{10,9... | collective-permute-start | bytes 688136 | tf_op jit(solution)/shard_map/ppermute | solution.py:507
  182.8 6.7 %collective-permute-done.20.refs_8_ = f32[16,3584]{1,0:T(8,128)} collective-permute-done((f32[16,3584]{1,0:T(8,128)S(1)}, f32[16,3584]{1,0:T(8,128)}, u32[]{:S(2)}, u32[]{:S(2)}) %collective-permute-start.20) | collective-permute-done | bytes 229408 | tf_op jit(solution)/shard_map/ppermute | solution.py:504
  189.6 11.9 %shard_map.51 = (f32[128,2560]{1,0:T(8,128)}, f32[128,768]{1,0:T(8,128)}) custom-call(s32[3]{0:T(128)} %pad_add_fusion.side_ref, f32[16,3584]{1,0:T(8,128)} %copy-done.3, f32[16,3584]{1,0:T(8,128)} %copy-done.5, f32[16,3584]{1,0:T(8,128)} %copy-done.7, f32[16,3584]{1,0:T(8,128)} %copy-done.9, f32[16,3584]{1,0:T(8,128)} %copy-done.11, f32[16,3584]{1,0:T(8,128)} %copy-done.13, ...), custom_call_target="tpu_custom_call" | custom-call | tf_op jit(solution)/shard_map/pallas_call | solution.py:382
  203.3 3.2 %collective-permute-done.21.refs_0_ = f32[128,2560]{1,0:T(8,128)S(1)} collective-permute-done((f32[128,2560]{1,0:T(8,128)}, f32[128,2560]{1,0:T(8,128)S(1)}, u32[]{:S(2)}, u32[]{:S(2)}) %collective-permute-start.21) | collective-permute-done | bytes 1310752 | tf_op jit(solution)/shard_map/ppermute | solution.py:395
  206.6 5.6 %shard_map.52 = (f32[128,1792]{1,0:T(8,128)}, f32[128,640]{1,0:T(8,128)}, f32[128,896]{1,0:T(8,128)}) custom-call(s32[1]{0:T(128)} %bitcast.core_ref, f32[128,2560]{1,0:T(8,128)} %get-tuple-element.35.own_ref.pay_ref, f32[128,2560]{1,0:T(8,128)S(1)} %collective-permute-done.21.refs_0_, f32[128,768]{1,0:T(8,128)} %get-tuple-element.36.refs_1_.y_ref), custom_call_target="tpu_custom_call" | custom-call | tf_op jit(solution)/shard_map/pallas_call | solution.py:382
  214.9 11.9 %collective-permute-done.22.refs_0_ = f32[128,896]{1,0:T(8,128)S(1)} collective-permute-done((f32[128,896]{1,0:T(8,128)}, f32[128,896]{1,0:T(8,128)S(1)}, u32[]{:S(2)}, u32[]{:S(2)}) %collective-permute-start.22) | collective-permute-done | bytes 458784 | tf_op jit(solution)/shard_map/ppermute | solution.py:395
  231.2 5.0 %shard_map.54 = (f32[128,1152]{1,0:T(8,128)}, f32[128,512]{1,0:T(8,128)}, f32[128,640]{1,0:T(8,128)}) custom-call(s32[1]{0:T(128)} %bitcast.core_ref, f32[128,1792]{1,0:T(8,128)} %get-tuple-element.37.own_ref.pay_ref, f32[128,896]{1,0:T(8,128)S(1)} %collective-permute-done.22.refs_0_, f32[128,896]{1,0:T(8,128)S(1)} %collective-permute-done.23.refs_1_, ...), custom_call_target="tpu_custom_call" | custom-call | tf_op jit(solution)/shard_map/pallas_call | solution.py:382
  236.1 3.3 %collective-permute-start.24 = (f32[128,640]{1,0:T(8,128)}, f32[128,640]{1,0:T(8,128)S(1)}, u32[]{:S(2)}, u32[]{:S(2)}) collective-permute-start(f32[128,640]{1,0:T(8,128)} %get-tuple-element.41), channel_id=1, source_target_pairs={{0,64},{16,80},{32,96},{48,112},{64,0},{80,16},{96,32},{112,48},{1... | collective-permute-start | bytes 983048 | tf_op jit(solution)/shard_map/ppermute | solution.py:395
  239.5 10.4 %collective-permute-done.24.refs_0_ = f32[128,640]{1,0:T(8,128)S(1)} collective-permute-done((f32[128,640]{1,0:T(8,128)}, f32[128,640]{1,0:T(8,128)S(1)}, u32[]{:S(2)}, u32[]{:S(2)}) %collective-permute-start.24) | collective-permute-done | bytes 327712 | tf_op jit(solution)/shard_map/ppermute | solution.py:395
  254.1 4.4 %shard_map.56 = (f32[128,640]{1,0:T(8,128)}, f32[128,384]{1,0:T(8,128)}) custom-call(s32[1]{0:T(128)} %bitcast.core_ref, f32[128,1152]{1,0:T(8,128)} %get-tuple-element.40.own_ref.pay_ref, f32[128,640]{1,0:T(8,128)S(1)} %collective-permute-done.24.refs_0_, f32[128,640]{1,0:T(8,128)S(1)} %collective-permute-done.25.refs_1_, f32[128,512]{1,0:T(8,128)} %shard_map.55.refs_2_.y_ref), custom_call_target="tpu_custom_call" | custom-call | tf_op jit(solution)/shard_map/pallas_call | solution.py:382
  263.4 7.3 %collective-permute-done.26.refs_0_ = f32[128,640]{1,0:T(8,128)S(1)} collective-permute-done((f32[128,640]{1,0:T(8,128)}, f32[128,640]{1,0:T(8,128)S(1)}, u32[]{:S(2)}, u32[]{:S(2)}) %collective-permute-start.26) | collective-permute-done | bytes 327712 | tf_op jit(solution)/shard_map/ppermute | solution.py:395
  270.7 3.9 %shard_map.58 = (f32[128,256]{1,0:T(8,128)}, f32[128,256]{1,0:T(8,128)}) custom-call(s32[1]{0:T(128)} %bitcast.core_ref, f32[128,640]{1,0:T(8,128)} %get-tuple-element.43.own_ref.pay_ref, f32[128,640]{1,0:T(8,128)S(1)} %collective-permute-done.26.refs_0_, f32[128,384]{1,0:T(8,128)} %shard_map.57.refs_1_.y_ref), custom_call_target="tpu_custom_call" | custom-call | tf_op jit(solution)/shard_map/pallas_call | solution.py:382
  274.7 3.1 %collective-permute-start.27 = (f32[128,256]{1,0:T(8,128)}, f32[128,256]{1,0:T(8,128)S(1)}, u32[]{:S(2)}, u32[]{:S(2)}) collective-permute-start(f32[128,256]{1,0:T(8,128)} %get-tuple-element.45.own_ref), channel_id=1, source_target_pairs={{0,256},{16,272},{32,288},{48,304},{64,320},{80,336},{96,352},{112... | collective-permute-start | bytes 393224 | tf_op jit(solution)/shard_map/ppermute | solution.py:395
  280.0 3.3 %collective-permute-done.27.other_ref = f32[128,256]{1,0:T(8,128)S(1)} collective-permute-done((f32[128,256]{1,0:T(8,128)}, f32[128,256]{1,0:T(8,128)S(1)}, u32[]{:S(2)}, u32[]{:S(2)}) %collective-permute-start.27) | collective-permute-done | bytes 131104 | tf_op jit(solution)/shard_map/ppermute | solution.py:395
  283.3 3.2 %shard_map.60 = f32[128,128]{1,0:T(8,128)} custom-call(s32[1,128]{1,0:T(1,128)} %order_ref.3, f32[128,128]{1,0:T(8,128)} %r_ref.3, f32[128,256]{1,0:T(8,128)} %get-tuple-element.45.own_ref, f32[128,256]{1,0:T(8,128)S(1)} %collective-permute-done.27.other_ref, f32[128,256]{1,0:T(8,128)} %shard_map.59.y_ref), custom_call_target="tpu_custom_call" | custom-call | tf_op jit(solution)/shard_map/pallas_call | solution.py:382
  (80 shorter events, 62.3 us)
Async XLA Ops:
  2.6 34.2 %collective-permute-start.1 = (f32[128,1280]{1,0:T(8,128)}, f32[128,1280]{1,0:T(8,128)S(1)}, u32[]{:S(2)}, u32[]{:S(2)}) collective-permute-start(f32[128,1280]{1,0:T(8,128)} %shard_map.46.z0.zs0), channel_id=1, source_target_pairs={{0,2},{1,3},{2,0},{3,1},{4,6},{5,7},{6,4},{7,5},{8,10},{9,11},{10,... | collective-permute-start | bytes 1966088 | tf_op jit(solution)/shard_map/ppermute | solution.py:395
  7.8 32.4 %collective-permute-start = (f32[128,1280]{1,0:T(8,128)}, f32[128,1280]{1,0:T(8,128)S(1)}, u32[]{:S(2)}, u32[]{:S(2)}) collective-permute-start(f32[128,1280]{1,0:T(8,128)} %shard_map.46.z0.zs0), channel_id=1, source_target_pairs={{0,1},{1,0},{2,3},{3,2},{4,5},{5,4},{6,7},{7,6},{8,9},{9,8},{10,11... | collective-permute-start | bytes 1966088 | tf_op jit(solution)/shard_map/ppermute | solution.py:395
  36.9 17.7 %collective-permute-start.2 = (f32[128,1280]{1,0:T(8,128)S(1)}, f32[128,1280]{1,0:T(8,128)S(1)}, u32[]{:S(2)}, u32[]{:S(2)}) collective-permute-start(f32[128,1280]{1,0:T(8,128)S(1)} %collective-permute-done.1.z2.zs2), channel_id=1, source_target_pairs={{0,1},{1,0},{2,3},{3,2},{4,5},{5,4},{6,7},{7,6},{8,9},{9,8},{10,11... | collective-permute-start | bytes 1966088 | tf_op jit(solution)/shard_map/ppermute | solution.py:395
  75.1 11.0 %collective-permute-start.4 = (f32[32,896]{1,0:T(8,128)}, f32[32,896]{1,0:T(8,128)S(1)}, u32[]{:S(2)}, u32[]{:S(2)}) collective-permute-start(f32[32,896]{1,0:T(8,128)} %get-tuple-element.31), channel_id=1, source_target_pairs={{0,16},{16,0},{32,48},{48,32},{64,80},{80,64},{96,112},{112,96},{1... | collective-permute-start | bytes 344072 | tf_op jit(solution)/shard_map/ppermute | solution.py:395
  77.0 29.3 %collective-permute-start.3 = (f32[16,2688]{1,0:T(8,128)}, f32[16,2688]{1,0:T(8,128)S(1)}, u32[]{:S(2)}, u32[]{:S(2)}) collective-permute-start(f32[16,2688]{1,0:T(8,128)} %get-tuple-element.29), channel_id=1, source_target_pairs={{0,4},{1,5},{2,6},{3,7},{4,0},{5,1},{6,2},{7,3},{8,12},{9,13},{10,... | collective-permute-start | bytes 516104 | tf_op jit(solution)/shard_map/ppermute | solution.py:395
  87.7 19.6 %collective-permute-start.5 = (f32[16,896]{1,0:T(8,128)}, f32[16,896]{1,0:T(8,128)S(1)}, u32[]{:S(2)}, u32[]{:S(2)}) collective-permute-start(f32[16,896]{1,0:T(8,128)} %get-tuple-element.33), channel_id=1, source_target_pairs={{0,4},{1,5},{2,6},{3,7},{4,0},{5,1},{6,2},{7,3},{8,12},{9,13},{10,... | collective-permute-start | bytes 172040 | tf_op jit(solution)/shard_map/ppermute | solution.py:395
  108.2 81.3 %copy-start.3 = (f32[16,3584]{1,0:T(8,128)}, f32[16,3584]{1,0:T(8,128)S(1)}, u32[]{:S(2)}) copy-start(f32[16,3584]{1,0:T(8,128)S(1)} %pad_maximum_fusion.refs_0_) | copy-start | bytes 688132
  108.2 15.1 %collective-permute-start.13 = (f32[16,3584]{1,0:T(8,128)S(1)}, f32[16,3584]{1,0:T(8,128)S(1)}, u32[]{:S(2)}, u32[]{:S(2)}) collective-permute-start(f32[16,3584]{1,0:T(8,128)S(1)} %pad_maximum_fusion.refs_0_), channel_id=1, source_target_pairs={{0,1},{1,2},{2,3},{3,4},{4,5},{5,6},{6,7},{7,8},{8,9},{9,10},{10,1... | collective-permute-start | bytes 688136 | tf_op jit(solution)/shard_map/ppermute | solution.py:504
  110.1 15.1 %collective-permute-start.6 = (f32[16,3584]{1,0:T(8,128)S(1)}, f32[16,3584]{1,0:T(8,128)S(1)}, u32[]{:S(2)}, u32[]{:S(2)}) collective-permute-start(f32[16,3584]{1,0:T(8,128)S(1)} %pad_maximum_fusion.refs_0_), channel_id=1, source_target_pairs={{0,15},{1,0},{2,1},{3,2},{4,3},{5,4},{6,5},{7,6},{8,7},{9,8},{10,9... | collective-permute-start | bytes 688136 | tf_op jit(solution)/shard_map/ppermute | solution.py:507
  123.3 66.2 %copy-start.4 = (f32[16,3584]{1,0:T(8,128)}, f32[16,3584]{1,0:T(8,128)S(1)}, u32[]{:S(2)}) copy-start(f32[16,3584]{1,0:T(8,128)S(1)} %collective-permute-done.13.refs_15_) | copy-start | bytes 688132
  123.3 10.1 %collective-permute-start.14 = (f32[16,3584]{1,0:T(8,128)S(1)}, f32[16,3584]{1,0:T(8,128)S(1)}, u32[]{:S(2)}, u32[]{:S(2)}) collective-permute-start(f32[16,3584]{1,0:T(8,128)S(1)} %collective-permute-done.13.refs_15_), channel_id=1, source_target_pairs={{0,1},{1,2},{2,3},{3,4},{4,5},{5,6},{6,7},{7,8},{8,9},{9,10},{10,1... | collective-permute-start | bytes 688136 | tf_op jit(solution)/shard_map/ppermute | solution.py:504
  125.2 64.2 %copy-start.5 = (f32[16,3584]{1,0:T(8,128)}, f32[16,3584]{1,0:T(8,128)S(1)}, u32[]{:S(2)}) copy-start(f32[16,3584]{1,0:T(8,128)S(1)} %collective-permute-done.6.refs_1_) | copy-start | bytes 688132
  125.2 10.1 %collective-permute-start.7 = (f32[16,3584]{1,0:T(8,128)S(1)}, f32[16,3584]{1,0:T(8,128)S(1)}, u32[]{:S(2)}, u32[]{:S(2)}) collective-permute-start(f32[16,3584]{1,0:T(8,128)S(1)} %collective-permute-done.6.refs_1_), channel_id=1, source_target_pairs={{0,15},{1,0},{2,1},{3,2},{4,3},{5,4},{6,5},{7,6},{8,7},{9,8},{10,9... | collective-permute-start | bytes 688136 | tf_op jit(solution)/shard_map/ppermute | solution.py:507
  133.4 56.1 %copy-start.6 = (f32[16,3584]{1,0:T(8,128)}, f32[16,3584]{1,0:T(8,128)S(1)}, u32[]{:S(2)}) copy-start(f32[16,3584]{1,0:T(8,128)S(1)} %collective-permute-done.14.refs_14_) | copy-start | bytes 688132
  133.4 9.2 %collective-permute-start.15 = (f32[16,3584]{1,0:T(8,128)S(1)}, f32[16,3584]{1,0:T(8,128)S(1)}, u32[]{:S(2)}, u32[]{:S(2)}) collective-permute-start(f32[16,3584]{1,0:T(8,128)S(1)} %collective-permute-done.14.refs_14_), channel_id=1, source_target_pairs={{0,1},{1,2},{2,3},{3,4},{4,5},{5,6},{6,7},{7,8},{8,9},{9,10},{10,1... | collective-permute-start | bytes 688136 | tf_op jit(solution)/shard_map/ppermute | solution.py:504
  135.3 9.2 %collective-permute-start.8 = (f32[16,3584]{1,0:T(8,128)S(1)}, f32[16,3584]{1,0:T(8,128)S(1)}, u32[]{:S(2)}, u32[]{:S(2)}) collective-permute-start(f32[16,3584]{1,0:T(8,128)S(1)} %collective-permute-done.7.refs_2_), channel_id=1, source_target_pairs={{0,15},{1,0},{2,1},{3,2},{4,3},{5,4},{6,5},{7,6},{8,7},{9,8},{10,9... | collective-permute-start | bytes 688136 | tf_op jit(solution)/shard_map/ppermute | solution.py:507
  142.6 9.1 %collective-permute-start.16 = (f32[16,3584]{1,0:T(8,128)S(1)}, f32[16,3584]{1,0:T(8,128)S(1)}, u32[]{:S(2)}, u32[]{:S(2)}) collective-permute-start(f32[16,3584]{1,0:T(8,128)S(1)} %collective-permute-done.15.refs_13_), channel_id=1, source_target_pairs={{0,1},{1,2},{2,3},{3,4},{4,5},{5,6},{6,7},{7,8},{8,9},{9,10},{10,1... | collective-permute-start | bytes 688136 | tf_op jit(solution)/shard_map/ppermute | solution.py:504
  144.6 9.1 %collective-permute-start.9 = (f32[16,3584]{1,0:T(8,128)S(1)}, f32[16,3584]{1,0:T(8,128)S(1)}, u32[]{:S(2)}, u32[]{:S(2)}) collective-permute-start(f32[16,3584]{1,0:T(8,128)S(1)} %collective-permute-done.8.refs_3_), channel_id=1, source_target_pairs={{0,15},{1,0},{2,1},{3,2},{4,3},{5,4},{6,5},{7,6},{8,7},{9,8},{10,9... | collective-permute-start | bytes 688136 | tf_op jit(solution)/shard_map/ppermute | solution.py:507
  151.7 9.1 %collective-permute-start.17 = (f32[16,3584]{1,0:T(8,128)S(1)}, f32[16,3584]{1,0:T(8,128)S(1)}, u32[]{:S(2)}, u32[]{:S(2)}) collective-permute-start(f32[16,3584]{1,0:T(8,128)S(1)} %collective-permute-done.16.refs_12_), channel_id=1, source_target_pairs={{0,1},{1,2},{2,3},{3,4},{4,5},{5,6},{6,7},{7,8},{8,9},{9,10},{10,1... | collective-permute-start | bytes 688136 | tf_op jit(solution)/shard_map/ppermute | solution.py:504
  153.7 9.1 %collective-permute-start.10 = (f32[16,3584]{1,0:T(8,128)S(1)}, f32[16,3584]{1,0:T(8,128)S(1)}, u32[]{:S(2)}, u32[]{:S(2)}) collective-permute-start(f32[16,3584]{1,0:T(8,128)S(1)} %collective-permute-done.9.refs_4_), channel_id=1, source_target_pairs={{0,15},{1,0},{2,1},{3,2},{4,3},{5,4},{6,5},{7,6},{8,7},{9,8},{10,9... | collective-permute-start | bytes 688136 | tf_op jit(solution)/shard_map/ppermute | solution.py:507
  160.8 9.1 %collective-permute-start.18 = (f32[16,3584]{1,0:T(8,128)S(1)}, f32[16,3584]{1,0:T(8,128)S(1)}, u32[]{:S(2)}, u32[]{:S(2)}) collective-permute-start(f32[16,3584]{1,0:T(8,128)S(1)} %collective-permute-done.17.refs_11_), channel_id=1, source_target_pairs={{0,1},{1,2},{2,3},{3,4},{4,5},{5,6},{6,7},{7,8},{8,9},{9,10},{10,1... | collective-permute-start | bytes 688136 | tf_op jit(solution)/shard_map/ppermute | solution.py:504
  162.8 9.1 %collective-permute-start.11 = (f32[16,3584]{1,0:T(8,128)S(1)}, f32[16,3584]{1,0:T(8,128)S(1)}, u32[]{:S(2)}, u32[]{:S(2)}) collective-permute-start(f32[16,3584]{1,0:T(8,128)S(1)} %collective-permute-done.10.refs_5_), channel_id=1, source_target_pairs={{0,15},{1,0},{2,1},{3,2},{4,3},{5,4},{6,5},{7,6},{8,7},{9,8},{10,9... | collective-permute-start | bytes 688136 | tf_op jit(solution)/shard_map/ppermute | solution.py:507
  170.0 10.2 %collective-permute-start.19 = (f32[16,3584]{1,0:T(8,128)S(1)}, f32[16,3584]{1,0:T(8,128)S(1)}, u32[]{:S(2)}, u32[]{:S(2)}) collective-permute-start(f32[16,3584]{1,0:T(8,128)S(1)} %collective-permute-done.18.refs_10_), channel_id=1, source_target_pairs={{0,1},{1,2},{2,3},{3,4},{4,5},{5,6},{6,7},{7,8},{8,9},{9,10},{10,1... | collective-permute-start | bytes 688136 | tf_op jit(solution)/shard_map/ppermute | solution.py:504
  171.9 10.9 %collective-permute-start.12 = (f32[16,3584]{1,0:T(8,128)S(1)}, f32[16,3584]{1,0:T(8,128)S(1)}, u32[]{:S(2)}, u32[]{:S(2)}) collective-permute-start(f32[16,3584]{1,0:T(8,128)S(1)} %collective-permute-done.11.refs_6_), channel_id=1, source_target_pairs={{0,15},{1,0},{2,1},{3,2},{4,3},{5,4},{6,5},{7,6},{8,7},{9,8},{10,9... | collective-permute-start | bytes 688136 | tf_op jit(solution)/shard_map/ppermute | solution.py:507
  180.2 9.2 %collective-permute-start.20 = (f32[16,3584]{1,0:T(8,128)S(1)}, f32[16,3584]{1,0:T(8,128)}, u32[]{:S(2)}, u32[]{:S(2)}) collective-permute-start(f32[16,3584]{1,0:T(8,128)S(1)} %collective-permute-done.19.refs_9_), channel_id=1, source_target_pairs={{0,1},{1,2},{2,3},{3,4},{4,5},{5,6},{6,7},{7,8},{8,9},{9,10},{10,1... | collective-permute-start | bytes 688136 | tf_op jit(solution)/shard_map/ppermute | solution.py:504
  201.4 5.1 %collective-permute-start.21 = (f32[128,2560]{1,0:T(8,128)}, f32[128,2560]{1,0:T(8,128)S(1)}, u32[]{:S(2)}, u32[]{:S(2)}) collective-permute-start(f32[128,2560]{1,0:T(8,128)} %get-tuple-element.35.own_ref.pay_ref), channel_id=1, source_target_pairs={{0,16},{16,0},{32,48},{48,32},{64,80},{80,64},{96,112},{112,96},{1... | collective-permute-start | bytes 3932168 | tf_op jit(solution)/shard_map/ppermute | solution.py:395
  212.1 14.7 %collective-permute-start.22 = (f32[128,896]{1,0:T(8,128)}, f32[128,896]{1,0:T(8,128)S(1)}, u32[]{:S(2)}, u32[]{:S(2)}) collective-permute-start(f32[128,896]{1,0:T(8,128)} %get-tuple-element.38), channel_id=1, source_target_pairs={{0,32},{16,48},{32,0},{48,16},{64,96},{80,112},{96,64},{112,80},{1... | collective-permute-start | bytes 1376264 | tf_op jit(solution)/shard_map/ppermute | solution.py:395
  226.8 4.4 %collective-permute-start.23 = (f32[128,896]{1,0:T(8,128)S(1)}, f32[128,896]{1,0:T(8,128)S(1)}, u32[]{:S(2)}, u32[]{:S(2)}) collective-permute-start(f32[128,896]{1,0:T(8,128)S(1)} %collective-permute-done.22.refs_0_), channel_id=1, source_target_pairs={{0,16},{16,0},{32,48},{48,32},{64,80},{80,64},{96,112},{112,96},{1... | collective-permute-start | bytes 1376264 | tf_op jit(solution)/shard_map/ppermute | solution.py:395
  236.1 13.7 %collective-permute-start.24 = (f32[128,640]{1,0:T(8,128)}, f32[128,640]{1,0:T(8,128)S(1)}, u32[]{:S(2)}, u32[]{:S(2)}) collective-permute-start(f32[128,640]{1,0:T(8,128)} %get-tuple-element.41), channel_id=1, source_target_pairs={{0,64},{16,80},{32,96},{48,112},{64,0},{80,16},{96,32},{112,48},{1... | collective-permute-start | bytes 983048 | tf_op jit(solution)/shard_map/ppermute | solution.py:395
  249.9 4.2 %collective-permute-start.25 = (f32[128,640]{1,0:T(8,128)S(1)}, f32[128,640]{1,0:T(8,128)S(1)}, u32[]{:S(2)}, u32[]{:S(2)}) collective-permute-start(f32[128,640]{1,0:T(8,128)S(1)} %collective-permute-done.24.refs_0_), channel_id=1, source_target_pairs={{0,16},{16,0},{32,48},{48,32},{64,80},{80,64},{96,112},{112,96},{1... | collective-permute-start | bytes 983048 | tf_op jit(solution)/shard_map/ppermute | solution.py:395
  258.5 12.2 %collective-permute-start.26 = (f32[128,640]{1,0:T(8,128)}, f32[128,640]{1,0:T(8,128)S(1)}, u32[]{:S(2)}, u32[]{:S(2)}) collective-permute-start(f32[128,640]{1,0:T(8,128)} %get-tuple-element.43.own_ref.pay_ref), channel_id=1, source_target_pairs={{0,128},{16,144},{32,160},{48,176},{64,192},{80,208},{96,224},{112... | collective-permute-start | bytes 983048 | tf_op jit(solution)/shard_map/ppermute | solution.py:395
  274.7 8.6 %collective-permute-start.27 = (f32[128,256]{1,0:T(8,128)}, f32[128,256]{1,0:T(8,128)S(1)}, u32[]{:S(2)}, u32[]{:S(2)}) collective-permute-start(f32[128,256]{1,0:T(8,128)} %get-tuple-element.45.own_ref), channel_id=1, source_target_pairs={{0,256},{16,272},{32,288},{48,304},{64,320},{80,336},{96,352},{112... | collective-permute-start | bytes 393224 | tf_op jit(solution)/shard_map/ppermute | solution.py:395
  (14 other events, 333.1 us)
